TPU v7x, 128 devices: a whole 4x4x4 slice. The times are simulated.
128 devices in a mesh: seq: 16 (over x_lo, z, core), head: 8 (over x_hi, y).
Axes of the slice: x: 4 (x_hi: 2, x_lo: 2; x = x_hi * 2 + x_lo), y: 4, z: 4, core: 2. Of those that a mesh axis runs over, the one named last changes fastest.
Arguments:
- video_query: bfloat16 [16384, 3072], P(('seq', 'head')), may hold values from -8 to 8
- video_key: bfloat16 [16384, 3072], P(('seq', 'head')), may hold values from -8 to 8
- video_value: bfloat16 [16384, 3072], P(('seq', 'head')), may hold values from -6 to 6
- video_grad: bfloat16 [16384, 3072], P(('seq', 'head')), may hold values from -6 to 6
- text_query: bfloat16 [256, 3072], P(None, 'head'), may hold values from -8 to 8
- text_key: bfloat16 [256, 3072], P(None, 'head'), may hold values from -8 to 8
- text_value: bfloat16 [256, 3072], P(None, 'head'), may hold values from -6 to 6
- text_grad: bfloat16 [256, 3072], P(None, 'head'), may hold values from -6 to 6
- tile_list: int32 [128, 8], replicated, may hold values from 0 to 127, as said below
- tile_count: int32 [128], replicated, may hold values from 1 to 8, as said below
- text_mask: int32 [256], replicated, may hold values from 0 to 1, as said below
Outputs:
- attended_video: bfloat16 [16384, 3072], P(('seq', 'head'))
- video_query_grad: bfloat16 [16384, 3072], P(('seq', 'head'))
- video_key_grad: bfloat16 [16384, 3072], P(('seq', 'head'))
- video_value_grad: bfloat16 [16384, 3072], P(('seq', 'head'))
- attended_text: bfloat16 [256, 3072], P(None, 'head')
- text_query_grad: bfloat16 [256, 3072], P(None, 'head')
- text_key_grad: bfloat16 [256, 3072], P(None, 'head')
- text_value_grad: bfloat16 [256, 3072], P(None, 'head')
Inputs may be any that keep to these rules, and one draw needn't show every extreme that they name: `tile_list`: the 8 entries of one query tile's list are distinct. Query tiles fall in aligned blocks of 8; the used entries of one block together name at most 2 distinct tiles of any other block of 8 tiles, and every block names exactly 2 from some other block. `tile_count`: every aligned block of 8 query tiles has a tile that uses all 8 entries. `text_mask`: the ones form a prefix of at least 64 entries.
All inputs are finite; a program needn't handle non-finite values.
Results may differ from a plain program's by a relative error of at most 0.012.
Values may be sent and summed in bfloat16 or wider, within the bound.
No kernel may reach another device: no remote copies, remote signals or barrier semaphores. Data moves between devices by JAX's collectives and lax.ppermute only.
A program may use at most 192 MiB of HBM per device.

v0:
```python
import jax
import jax.numpy as jnp
from jax import lax
from jax.sharding import PartitionSpec as P

HD = 128
TXT = 256
TILE = 128
KT = 8
MOST = 2


NEGATIVE = -1e30
HIGHEST_PRECISION = lax.Precision.HIGHEST


def sent_together(arrays, axis, split_dim, concat_dim, along):
    ends, at = ([], 0)
    for a in arrays[:-1]:
        at += a.shape[along]
        ends.append(at)
    both = jnp.concatenate(arrays, axis=along)
    return tuple(
        jnp.split(
            lax.all_to_all(both, axis, split_axis=split_dim, concat_axis=concat_dim, tiled=True),
            ends,
            axis=along,
        )
    )


def from_everyone(shard, axis):
    length = lax.axis_size(axis)
    return lax.all_to_all(
        jnp.broadcast_to(shard[None], (length, *shard.shape)), axis, 0, 0, tiled=True
    )


def taken_together(shard, axis):
    return from_everyone(shard, axis).max(axis=0)


def of_everyone(shard, axis):
    everything = from_everyone(shard, axis)
    return jnp.sum(everything, axis=0)


def packed_total(arrays, axis):
    ends = [0]
    for a in arrays:
        ends.append(ends[-1] + a.size)
    running = of_everyone(jnp.concatenate([a.ravel() for a in arrays]), axis)
    return tuple((running[b:e].reshape(a.shape) for a, b, e in zip(arrays, ends, ends[1:])))


def split_product(form, weights, data):
    upper = weights.astype(jnp.bfloat16)
    lower = (weights - upper.astype(jnp.float32)).astype(jnp.bfloat16)
    return jnp.einsum(form, upper, data, preferred_element_type=jnp.float32) + jnp.einsum(
        form, lower, data, preferred_element_type=jnp.float32
    )


def block_scores(query_blk, key_blk, live_blk, factor):
    scores = (
        jnp.einsum("bthd,bkhd->bhtk", query_blk, key_blk, preferred_element_type=jnp.float32)
        * factor
    )
    scores = jnp.where(live_blk[:, None, None, :], scores, NEGATIVE)
    maximum = jnp.max(scores, axis=-1)
    log_total = maximum + jnp.log(jnp.sum(jnp.exp(scores - maximum[..., None]), axis=-1))
    return (scores, log_total)


def block_forward(scores, log_total, value_blk, grad_blk):
    weights = jnp.exp(scores - log_total[..., None]).astype(jnp.bfloat16)
    output = jnp.einsum("bhtk,bkhd->bthd", weights, value_blk, preferred_element_type=jnp.float32)
    offset = jnp.sum(grad_blk.astype(jnp.float32) * output, axis=-1)
    return (output, jnp.transpose(offset, (0, 2, 1)))


def block_backward(scores, log_total, offset, query_blk, key_blk, value_blk, grad_blk, factor):
    probability = jnp.exp(scores - log_total[..., None])
    weights = probability.astype(jnp.bfloat16)
    prob_grad = jnp.einsum(
        "bthd,bkhd->bhtk", grad_blk, value_blk, preferred_element_type=jnp.float32
    )
    score_grad = (probability * (prob_grad - offset[..., None])).astype(jnp.bfloat16)
    query_grad = (
        jnp.einsum("bhtk,bkhd->bthd", score_grad, key_blk, preferred_element_type=jnp.float32)
        * factor
    )
    key_grad = (
        jnp.einsum("bhtk,bthd->bkhd", score_grad, query_blk, preferred_element_type=jnp.float32)
        * factor
    )
    value_grad = jnp.einsum(
        "bhtk,bthd->bkhd", weights, grad_blk, preferred_element_type=jnp.float32
    )
    return (query_grad, key_grad, value_grad)


def spread_grads(pool_total, text_total, grad_blk, pool_slot):
    block_tiles = grad_blk.shape[0]
    tile_part = grad_blk[:, : KT * TILE].reshape(block_tiles, KT, TILE, pool_total.shape[2])
    return (
        pool_total.at[pool_slot].add(tile_part),
        text_total + jnp.sum(grad_blk[:, KT * TILE :], axis=0),
    )


def body(
    video_query,
    video_key,
    video_value,
    video_grad,
    text_query,
    text_key,
    text_value,
    text_grad,
    tile_list,
    tile_count,
    text_mask,
):
    factor = HD ** (-0.5)
    groups = lax.axis_size("seq")
    own_group = lax.axis_index("seq")
    query_rows, key_rows, value_rows, grad_rows = (
        lax.all_to_all(video_query, "head", split_axis=1, concat_axis=0, tiled=True),
        lax.all_to_all(video_key, "head", split_axis=1, concat_axis=0, tiled=True),
        lax.all_to_all(video_value, "head", split_axis=1, concat_axis=0, tiled=True),
        lax.all_to_all(video_grad, "head", split_axis=1, concat_axis=0, tiled=True),
    )
    token_rows, feature_width = query_rows.shape
    head_count = feature_width // HD
    shard_tiles = token_rows // TILE
    tile_total = tile_list.shape[0]
    text_ok = text_mask > 0
    entry_live = jnp.arange(KT)[None, :] < tile_count[:, None]
    tile_hits = (tile_list[:, :, None] == jnp.arange(tile_total)[None, None, :]) & entry_live[
        :, :, None
    ]
    wanted = jnp.any(
        jnp.any(tile_hits, axis=1).reshape(groups, shard_tiles, tile_total), axis=1
    ).reshape(groups, groups, shard_tiles)
    slot_rank = jnp.cumsum(wanted.astype(jnp.int32), axis=2) - 1
    distinct = (jnp.arange(groups)[:, None] != jnp.arange(groups)[None, :])[:, :, None, None]
    select = (
        wanted[:, :, None, :]
        & (slot_rank[:, :, None, :] == jnp.arange(MOST)[None, None, :, None])
        & distinct
    )
    outgoing = lax.dynamic_index_in_dim(select, own_group, 1, keepdims=False)
    incoming = lax.dynamic_index_in_dim(select, own_group, 0, keepdims=False)
    picker = outgoing.reshape(groups * MOST, shard_tiles).astype(jnp.bfloat16)
    send_keys = jnp.dot(
        picker,
        key_rows.reshape(shard_tiles, TILE * feature_width),
        preferred_element_type=jnp.float32,
    )
    send_keys = send_keys.astype(jnp.bfloat16).reshape(groups, MOST * TILE, feature_width)
    send_values = jnp.dot(
        picker,
        value_rows.reshape(shard_tiles, TILE * feature_width),
        preferred_element_type=jnp.float32,
    )
    send_values = send_values.astype(jnp.bfloat16).reshape(groups, MOST * TILE, feature_width)
    owner_base = (
        jnp.arange(groups, dtype=jnp.int32)[:, None, None] * shard_tiles
        + jnp.arange(shard_tiles, dtype=jnp.int32)[None, None, :]
    )
    slot_ids = jnp.where(
        jnp.any(incoming, axis=2), jnp.sum(jnp.where(incoming, owner_base, 0), axis=2), -1
    ).reshape(groups * MOST)
    pool_ids = jnp.concatenate(
        [own_group * shard_tiles + jnp.arange(shard_tiles, dtype=jnp.int32), slot_ids]
    )
    pool_size = shard_tiles + groups * MOST
    my_list = lax.dynamic_slice_in_dim(tile_list, own_group * shard_tiles, shard_tiles, 0)
    my_count = lax.dynamic_slice_in_dim(tile_count, own_group * shard_tiles, shard_tiles, 0)
    pool_match = my_list[:, :, None] == pool_ids[None, None, :]
    pool_slot = jnp.sum(jnp.where(pool_match, jnp.arange(pool_size, dtype=jnp.int32), 0), axis=2)
    live_entry = jnp.any(pool_match, axis=2) & (jnp.arange(KT)[None, :] < my_count[:, None])
    text_query3 = text_query.reshape(TXT, head_count, HD)
    text_key3 = text_key.reshape(TXT, head_count, HD)
    text_value3 = text_value.reshape(TXT, head_count, HD)
    text_grad3 = text_grad.reshape(TXT, head_count, HD)
    block_tiles = min(shard_tiles, max(1, 512 // TILE))
    block_count = shard_tiles // block_tiles
    query_blocks = query_rows.reshape(block_count, block_tiles, TILE, head_count, HD)
    grad_blocks = grad_rows.reshape(block_count, block_tiles, TILE, head_count, HD)
    slot_blocks = pool_slot.reshape(block_count, block_tiles, KT)
    live_blocks = jnp.concatenate(
        [
            jnp.repeat(live_entry, TILE, axis=1),
            jnp.broadcast_to(text_ok[None, :], (shard_tiles, TXT)),
        ],
        axis=1,
    )
    live_blocks = live_blocks.reshape(block_count, block_tiles, KT * TILE + TXT)
    local_keys = key_rows.reshape(shard_tiles, TILE, feature_width)
    local_values = value_rows.reshape(shard_tiles, TILE, feature_width)

    def block_rows(pool, slot_blk, text_part):
        picked = pool[slot_blk].reshape(block_tiles, KT * TILE, head_count, HD)
        return jnp.concatenate(
            [picked, jnp.broadcast_to(text_part[None], (block_tiles, TXT, head_count, HD))], axis=1
        )

    got_keys, got_values = sent_together((send_keys, send_values), "seq", 0, 0, 1)
    pool_keys = jnp.concatenate(
        [local_keys, got_keys.reshape(groups * MOST, TILE, feature_width)], axis=0
    )
    pool_values = jnp.concatenate(
        [local_values, got_values.reshape(groups * MOST, TILE, feature_width)], axis=0
    )
    start = (
        jnp.zeros((pool_size, TILE, feature_width), jnp.float32),
        jnp.zeros((pool_size, TILE, feature_width), jnp.float32),
        jnp.zeros((TXT, head_count, HD), jnp.float32),
        jnp.zeros((TXT, head_count, HD), jnp.float32),
    )

    def joined_step(running, inputs):
        key_acc, value_acc, text_key_acc, text_value_acc = running
        query_blk, grad_blk, slot_blk, live_blk = inputs
        key_blk = block_rows(pool_keys, slot_blk, text_key3)
        value_blk = block_rows(pool_values, slot_blk, text_value3)
        scores, log_total = block_scores(query_blk, key_blk, live_blk, factor)
        output, offset = block_forward(scores, log_total, value_blk, grad_blk)
        query_grad, key_grad, value_grad = block_backward(
            scores, log_total, offset, query_blk, key_blk, value_blk, grad_blk, factor
        )
        key_acc, text_key_acc = spread_grads(key_acc, text_key_acc, key_grad, slot_blk)
        value_acc, text_value_acc = spread_grads(value_acc, text_value_acc, value_grad, slot_blk)
        return (
            (key_acc, value_acc, text_key_acc, text_value_acc),
            (output.astype(jnp.bfloat16), query_grad.astype(jnp.bfloat16)),
        )

    finals, outputs = lax.scan(
        joined_step, start, (query_blocks, grad_blocks, slot_blocks, live_blocks)
    )
    attended_blocks, query_grad_blocks = outputs
    key_acc, value_acc, text_key_acc, text_value_acc = finals
    back_keys, back_values = sent_together(
        (
            key_acc[shard_tiles:].reshape(groups, MOST * TILE, feature_width),
            value_acc[shard_tiles:].reshape(groups, MOST * TILE, feature_width),
        ),
        "seq",
        0,
        0,
        1,
    )
    out_flat = outgoing.reshape(groups * MOST, shard_tiles)
    target_tile = jnp.where(
        jnp.any(out_flat, axis=1),
        jnp.sum(jnp.where(out_flat, jnp.arange(shard_tiles, dtype=jnp.int32)[None, :], 0), axis=1),
        shard_tiles,
    )
    own_key_grad = (
        key_acc[:shard_tiles]
        .at[target_tile]
        .add(back_keys.reshape(groups * MOST, TILE, feature_width), mode="drop")
    )
    own_value_grad = (
        value_acc[:shard_tiles]
        .at[target_tile]
        .add(back_values.reshape(groups * MOST, TILE, feature_width), mode="drop")
    )
    key_rows3 = key_rows.reshape(token_rows, head_count, HD)
    value_rows3 = value_rows.reshape(token_rows, head_count, HD)
    text_query32 = text_query3.astype(jnp.float32)
    text_key32 = text_key3.astype(jnp.float32)
    text_value32 = text_value3.astype(jnp.float32)
    text_grad32 = text_grad3.astype(jnp.float32)
    video_scores = (
        jnp.einsum("thd,khd->htk", text_query3, key_rows3, preferred_element_type=jnp.float32)
        * factor
    )
    text_scores = (
        jnp.einsum("thd,khd->htk", text_query3, text_key3, preferred_element_type=jnp.float32)
        * factor
    )
    text_scores = jnp.where(text_ok[None, None, :], text_scores, NEGATIVE)
    maximum = jnp.maximum(
        taken_together(jnp.max(video_scores, axis=-1), "seq"), jnp.max(text_scores, axis=-1)
    )
    video_exp = jnp.exp(video_scores - maximum[..., None])
    denominator, numerator = packed_total(
        (jnp.sum(video_exp, axis=-1), split_product("htk,khd->thd", video_exp, value_rows3)), "seq"
    )
    text_exp = jnp.exp(text_scores - maximum[..., None])
    denominator = denominator + jnp.sum(text_exp, axis=-1)
    numerator = numerator + jnp.einsum(
        "htk,khd->thd", text_exp, text_value32, precision=HIGHEST_PRECISION
    )
    log_total = maximum + jnp.log(denominator)
    text_out = numerator / denominator.T[:, :, None]
    video_prob = jnp.exp(video_scores - log_total[..., None])
    text_prob = jnp.exp(text_scores - log_total[..., None])
    text_offset = jnp.sum(text_grad32 * text_out, axis=-1).T
    video_dscore = video_prob * (
        jnp.einsum("thd,khd->htk", text_grad3, value_rows3, preferred_element_type=jnp.float32)
        - text_offset[..., None]
    )
    text_dscore = text_prob * (
        jnp.einsum("thd,khd->htk", text_grad3, text_value3, preferred_element_type=jnp.float32)
        - text_offset[..., None]
    )
    query_part = split_product("htk,khd->thd", video_dscore, key_rows3) * factor
    video_key_from_text = split_product("htk,thd->khd", video_dscore, text_query3) * factor
    video_value_from_text = split_product("htk,thd->khd", video_prob, text_grad3)
    query_sum, key_sum, value_sum = lax.psum((query_part, text_key_acc, text_value_acc), "seq")
    text_query_grad = (
        query_sum
        + jnp.einsum("htk,khd->thd", text_dscore, text_key32, precision=HIGHEST_PRECISION) * factor
    )
    text_key_grad = (
        key_sum
        + jnp.einsum("htk,thd->khd", text_dscore, text_query32, precision=HIGHEST_PRECISION)
        * factor
    )
    text_value_grad = value_sum + jnp.einsum(
        "htk,thd->khd", text_prob, text_grad32, precision=HIGHEST_PRECISION
    )
    attended_rows = attended_blocks.reshape(token_rows, feature_width)
    query_grad_rows = query_grad_blocks.reshape(token_rows, feature_width)
    key_grad_rows = (
        own_key_grad.reshape(token_rows, feature_width)
        + video_key_from_text.reshape(token_rows, feature_width)
    ).astype(jnp.bfloat16)
    value_grad_rows = (
        own_value_grad.reshape(token_rows, feature_width)
        + video_value_from_text.reshape(token_rows, feature_width)
    ).astype(jnp.bfloat16)
    attended_video, video_query_grad, video_key_grad, video_value_grad = (
        lax.all_to_all(attended_rows, "head", split_axis=0, concat_axis=1, tiled=True),
        lax.all_to_all(query_grad_rows, "head", split_axis=0, concat_axis=1, tiled=True),
        lax.all_to_all(key_grad_rows, "head", split_axis=0, concat_axis=1, tiled=True),
        lax.all_to_all(value_grad_rows, "head", split_axis=0, concat_axis=1, tiled=True),
    )
    return (
        attended_video,
        video_query_grad,
        video_key_grad,
        video_value_grad,
        text_out.reshape(TXT, feature_width).astype(jnp.bfloat16),
        text_query_grad.reshape(TXT, feature_width).astype(jnp.bfloat16),
        text_key_grad.reshape(TXT, feature_width).astype(jnp.bfloat16),
        text_value_grad.reshape(TXT, feature_width).astype(jnp.bfloat16),
    )


def solution(mesh):
    placed = (
        P(("seq", "head"), None),
        P(("seq", "head"), None),
        P(("seq", "head"), None),
        P(("seq", "head"), None),
        P(None, "head"),
        P(None, "head"),
        P(None, "head"),
        P(None, "head"),
        P(),
        P(),
        P(),
    )
    return jax.shard_map(
        body,
        mesh=mesh,
        in_specs=placed,
        out_specs=(
            P(("seq", "head"), None),
            P(("seq", "head"), None),
            P(("seq", "head"), None),
            P(("seq", "head"), None),
            P(None, "head"),
            P(None, "head"),
            P(None, "head"),
            P(None, "head"),
        ),
        check_vma=False,
    )
```

profile of v0, /device:TPU:6, one launch (start us, length us, event | category | flops | bytes accessed | tf_op | source)
XLA Modules:
  0.0 818.9 jit_solution(423882828849883886)
XLA Ops:
  9.6 7.6 all-to-all-start.2
  19.0 9.5 %all-to-all-done.2 = bf16[128,8,384]{0,2,1:T(8,128)(2,1)S(1)} async-done(((bf16[128,8,384]{0,2,1:T(8,128)(2,1)}), bf16[128,8,384]{0,2,1:T(8,128)(2,1)S(1)}, u32[]{:S(2)}, u32[]{:S(2)}) %all-to-all-start.2) | async-done | bytes 786464 | tf_op jit(solution)/shard_map/all_to_all | solution.py:131
  28.6 5.7 all-to-all-start.1
  39.7 6.1 all-to-all-done.1
  45.9 6.1 all-to-all-start
  73.9 6.8 all-to-all-start.7
  80.7 6.3 pad_maximum_fusion.17
  87.6 6.3 all-to-all-start.3
  116.3 64.3 %all-to-all-done.3 = bf16[16,512,384]{2,1,0:T(8,128)(2,1)} async-done(((bf16[16,512,384]{2,1,0:T(8,128)(2,1)}), bf16[16,512,384]{2,1,0:T(8,128)(2,1)}, u32[]{:S(2)}, u32[]{:S(2)}) %all-to-all-start.3) | async-done | bytes 6291488 | tf_op jit(solution)/shard_map/all_to_all | solution.py:25
  180.6 7.2 all-to-all-start.4
  198.1 5.6 broadcast_in_dim.156
  203.7 15.3 %all-to-all-start.8 = ((f32[16,1,99072]{2,1,0:T(1,128)}), f32[16,1,99072]{2,1,0:T(1,128)}, u32[]{:S(2)}, u32[]{:S(2)}) async-start(f32[16,1,99072]{2,1,0:T(1,128)} %broadcast_in_dim.156), calls=%async_computation.8 | async-start | bytes 12681216 | tf_op jit(solution)/shard_map/all_to_all | solution.py:34
  219.0 4.1 broadcast.150.clone
  223.1 4.0 broadcast.150
  227.2 254.2 %while.21 = (s32[]{:T(128)}, f32[40,128,384]{2,1,0:T(8,128)}, f32[40,128,384]{2,1,0:T(8,128)}, f32[256,3,128]{0,2,1:T(8,128)}, f32[256,3,128]{0,2,1:T(8,128)}, /...) while((s32[]{:T(128)}, f32[40,128,384]{2,1,0:T(8,128)}, ...), condition=%wide.region_15.16_spmd.clone, body=%wide.region_7.15_spmd.clone.sunk | while | flops 3084187648 | bytes 308372384 | solution.py:241
  235.4 3.8 reshape.483
  239.3 4.6 copy.643
  247.2 3.8 reshape.482
  273.5 9.3 %copy.645 = f32[4,1024,3,128]{3,2,1,0:T(4,128)} copy(f32[4,1024,3,128]{1,3,2,0:T(8,128)} %slice.87) | data formatting | bytes 12582912 | tf_op jit(solution)/shard_map/while/body/eval_jaxpr/reshape | solution.py:105
  282.8 10.9 %reshape.485 = f32[32,128,384]{2,1,0:T(8,128)} reshape(f32[4,1024,3,128]{3,2,1,0:T(4,128)} %copy.645) | data formatting | bytes 12582912 | tf_op jit(solution)/shard_map/while/body/eval_jaxpr/reshape | solution.py:105
  293.7 16.4 %scatter_fusion.1 = f32[40,128,384]{2,1,0:T(8,128)} fusion(f32[40,128,384]{2,1,0:T(8,128)} %get-tuple-element.482, s32[32]{0:T(128)S(1)} %reshape.481, f32[32,128,384]{2,1,0:T(8,128)} %reshape.485), kind=kCustom, calls=%fused_computation.3.clone.clone.1 | custom fusion | flops 1572864 | bytes 18874496 | tf_op jit(solution)/shard_map/while/body/eval_jaxpr/scatter-add | solution.py:107
  317.5 9.4 %copy.644 = f32[4,1024,3,128]{3,2,1,0:T(4,128)} copy(f32[4,1024,3,128]{1,3,2,0:T(8,128)} %slice.86) | data formatting | bytes 12582912 | tf_op jit(solution)/shard_map/while/body/eval_jaxpr/reshape | solution.py:105
  326.9 10.9 %reshape.484 = f32[32,128,384]{2,1,0:T(8,128)} reshape(f32[4,1024,3,128]{3,2,1,0:T(4,128)} %copy.644) | data formatting | bytes 12582912 | tf_op jit(solution)/shard_map/while/body/eval_jaxpr/reshape | solution.py:105
  337.8 16.2 %scatter_fusion = f32[40,128,384]{2,1,0:T(8,128)} fusion(f32[40,128,384]{2,1,0:T(8,128)} %get-tuple-element.481, s32[32]{0:T(128)S(1)} %reshape.481, f32[32,128,384]{2,1,0:T(8,128)} %reshape.484), kind=kCustom, calls=%fused_computation.2.clone.clone.1 | custom fusion | flops 1572864 | bytes 18874496 | tf_op jit(solution)/shard_map/while/body/eval_jaxpr/scatter-add | solution.py:107
  362.2 3.8 reshape.483
  366.0 4.6 copy.643
  374.0 3.8 reshape.482
  400.3 9.3 %copy.645 = f32[4,1024,3,128]{3,2,1,0:T(4,128)} copy(f32[4,1024,3,128]{1,3,2,0:T(8,128)} %slice.87) | data formatting | bytes 12582912 | tf_op jit(solution)/shard_map/while/body/eval_jaxpr/reshape | solution.py:105
  409.6 10.9 %reshape.485 = f32[32,128,384]{2,1,0:T(8,128)} reshape(f32[4,1024,3,128]{3,2,1,0:T(4,128)} %copy.645) | data formatting | bytes 12582912 | tf_op jit(solution)/shard_map/while/body/eval_jaxpr/reshape | solution.py:105
  420.5 16.3 %scatter_fusion.1 = f32[40,128,384]{2,1,0:T(8,128)} fusion(f32[40,128,384]{2,1,0:T(8,128)} %get-tuple-element.482, s32[32]{0:T(128)S(1)} %reshape.481, f32[32,128,384]{2,1,0:T(8,128)} %reshape.485), kind=kCustom, calls=%fused_computation.3.clone.clone.1 | custom fusion | flops 1572864 | bytes 18874496 | tf_op jit(solution)/shard_map/while/body/eval_jaxpr/scatter-add | solution.py:107
  444.3 9.4 %copy.644 = f32[4,1024,3,128]{3,2,1,0:T(4,128)} copy(f32[4,1024,3,128]{1,3,2,0:T(8,128)} %slice.86) | data formatting | bytes 12582912 | tf_op jit(solution)/shard_map/while/body/eval_jaxpr/reshape | solution.py:105
  453.6 10.9 %reshape.484 = f32[32,128,384]{2,1,0:T(8,128)} reshape(f32[4,1024,3,128]{3,2,1,0:T(4,128)} %copy.644) | data formatting | bytes 12582912 | tf_op jit(solution)/shard_map/while/body/eval_jaxpr/reshape | solution.py:105
  464.6 16.3 %scatter_fusion = f32[40,128,384]{2,1,0:T(8,128)} fusion(f32[40,128,384]{2,1,0:T(8,128)} %get-tuple-element.481, s32[32]{0:T(128)S(1)} %reshape.481, f32[32,128,384]{2,1,0:T(8,128)} %reshape.484), kind=kCustom, calls=%fused_computation.2.clone.clone.1 | custom fusion | flops 1572864 | bytes 18874496 | tf_op jit(solution)/shard_map/while/body/eval_jaxpr/scatter-add | solution.py:107
  483.6 5.7 all-to-all-start.6
  489.3 6.0 slice.55
  495.4 6.1 slice.56
  501.5 10.4 %pad_maximum_fusion.16 = f32[16,512,384]{2,1,0:T(8,128)} fusion(f32[16,256,384]{2,1,0:T(8,128)} %bitcast.197, f32[16,256,384]{2,1,0:T(8,128)} %bitcast.196), kind=kLoop, calls=%fused_computation.48 | loop fusion | flops 3145728 | bytes 25165824 | tf_op jit(solution)/shard_map/concatenate | solution.py:22
  512.8 5.1 all-to-all-start.9
  520.8 11.2 %reduce_sum.102 = f32[99072]{0:T(1024)} reduce(f32[16,1,99072]{2,1,0:T(1,128)} %all-to-all-done.8, f32[]{:T(128)} %constant.16.clone.1), dimensions={0,1}, to_apply=%region_20.21 | reduce | flops 1486080 | bytes 6736900 | tf_op jit(solution)/shard_map/reduce_sum | solution.py:45
  547.6 3.8 reshape.453
  561.4 153.7 %all-to-all-done.9 = f32[16,512,384]{2,1,0:T(8,128)} async-done(((f32[16,512,384]{2,1,0:T(8,128)}), f32[16,512,384]{2,1,0:T(8,128)}, u32[]{:S(2)}, u32[]{:S(2)}) %all-to-all-start.9) | async-done | bytes 12582944 | tf_op jit(solution)/shard_map/all_to_all | solution.py:25
  715.2 7.4 all-to-all-start.5
  722.6 10.7 %fusion.69 = (f32[16,256,384]{2,1,0:T(8,128)}, f32[16,256,384]{2,1,0:T(8,128)}) fusion(f32[16,512,384]{2,1,0:T(8,128)} %all-to-all-done.9), kind=kLoop, calls=%fused_computation.145 | loop fusion | bytes 25165824 | tf_op jit(solution)/shard_map/split | solution.py:24
  733.3 15.3 %scatter_fusion.2 = f32[8,128,384]{2,1,0:T(8,128)} fusion(f32[8,128,384]{2,1,0:T(8,128)} %slice_add_fusion.1, s32[32]{0:T(128)S(1)} %copy-done.55, f32[32,128,384]{2,1,0:T(8,128)} %bitcast.199), kind=kCustom, calls=%fused_computation.4 | custom fusion | flops 1572864 | bytes 18874496 | tf_op jit(solution)/shard_map/scatter-add | solution.py:265
  751.0 7.2 all-to-all-start.10
  763.7 4.0 copy.610
  781.6 10.0 %scatter_fusion.3 = f32[8,128,384]{2,1,0:T(8,128)S(1)} fusion(f32[8,128,384]{2,1,0:T(8,128)S(1)} %slice_add_fusion, s32[32]{0:T(128)S(1)} %copy-done.55, f32[32,128,384]{2,1,0:T(8,128)} %bitcast.198), kind=kCustom, calls=%fused_computation.5 | custom fusion | flops 1572864 | bytes 18874496 | tf_op jit(solution)/shard_map/scatter-add | solution.py:270
  792.5 7.4 all-to-all-start.11
  (338 shorter events, 213.0 us)
Async XLA Ops:
  7.2 10.0 %copy-start.54 = (s32[128,8]{0,1:T(8,128)S(1)}, s32[128,8]{0,1:T(8,128)}, u32[]{:S(2)}) copy-start(s32[128,8]{0,1:T(8,128)} %param.21) | copy-start | bytes 12292
  7.2 10.1 %copy-start.57 = (s32[128]{0:T(128)S(1)}, s32[128]{0:T(128)}, u32[]{:S(2)}) copy-start(s32[128]{0:T(128)} %param.22) | copy-start | bytes 1540
  7.2 10.7 %copy-start.37 = (bf16[128,3072]{1,0:T(8,128)(2,1)S(1)}, bf16[128,3072]{1,0:T(8,128)(2,1)}, u32[]{:S(2)}) copy-start(bf16[128,3072]{1,0:T(8,128)(2,1)} %param.14) | copy-start | bytes 2359300
  9.6 27.1 %copy-start.42 = (bf16[256,384]{1,0:T(8,128)(2,1)S(1)}, bf16[256,384]{1,0:T(8,128)(2,1)}, u32[]{:S(2)}) copy-start(bf16[256,384]{1,0:T(8,128)(2,1)} %param.17) | copy-start | bytes 589828
  9.6 27.3 %copy-start.38 = (bf16[128,3072]{1,0:T(8,128)(2,1)S(1)}, bf16[128,3072]{1,0:T(8,128)(2,1)}, u32[]{:S(2)}) copy-start(bf16[128,3072]{1,0:T(8,128)(2,1)} %param.13) | copy-start | bytes 2359300
  9.6 19.0 %all-to-all-start.2 = ((bf16[128,8,384]{0,2,1:T(8,128)(2,1)}), bf16[128,8,384]{0,2,1:T(8,128)(2,1)S(1)}, u32[]{:S(2)}, u32[]{:S(2)}) async-start(bf16[128,8,384]{0,2,1:T(8,128)(2,1)} %bitcast.9), calls=%async_computation.2 | async-start | bytes 1572864 | tf_op jit(solution)/shard_map/all_to_all | solution.py:131
  28.6 11.2 %copy-start.29 = (bf16[128,8,384]{0,2,1:T(8,128)(2,1)}, bf16[128,8,384]{0,2,1:T(8,128)(2,1)S(1)}, u32[]{:S(2)}) copy-start(bf16[128,8,384]{0,2,1:T(8,128)(2,1)S(1)} %all-to-all-done.2) | copy-start | bytes 2359300
  28.6 17.3 %all-to-all-start.1 = ((bf16[128,8,384]{0,2,1:T(8,128)(2,1)}), bf16[128,8,384]{0,2,1:T(8,128)(2,1)S(1)}, u32[]{:S(2)}, u32[]{:S(2)}) async-start(bf16[128,8,384]{0,2,1:T(8,128)(2,1)} %bitcast.7), calls=%async_computation.1 | async-start | bytes 1572864 | tf_op jit(solution)/shard_map/all_to_all | solution.py:130
  36.7 9.2 %copy-start.48 = (pred[16,1,2,8]{3,2,0,1:T(4,128)(4,1)}, pred[16,1,2,8]{3,2,0,1:T(4,128)(4,1)S(1)}, u32[]{:S(2)}) copy-start(pred[16,1,2,8]{3,2,0,1:T(4,128)(4,1)S(1)} %get-tuple-element.339) | copy-start | bytes 772
  36.9 34.5 %copy-start.24 = (bf16[256,384]{0,1:T(8,128)(2,1)}, bf16[256,384]{0,1:T(8,128)(2,1)S(1)}, u32[]{:S(2)}) copy-start(bf16[256,384]{0,1:T(8,128)(2,1)S(1)} %copy.523) | copy-start | bytes 589828
  38.4 13.6 %copy-start.33 = (bf16[8,128,384]{2,1,0:T(8,128)(2,1)}, bf16[8,128,384]{2,1,0:T(8,128)(2,1)S(1)}, u32[]{:S(2)}) copy-start(bf16[8,128,384]{2,1,0:T(8,128)(2,1)S(1)} %copy.511) | copy-start | bytes 2359300
  45.9 27.4 %all-to-all-start = ((bf16[128,8,384]{0,2,1:T(8,128)(2,1)}), bf16[128,8,384]{0,2,1:T(8,128)(2,1)}, u32[]{:S(2)}, u32[]{:S(2)}) async-start(bf16[128,8,384]{0,2,1:T(8,128)(2,1)} %bitcast.4), calls=%async_computation | async-start | bytes 1572864 | tf_op jit(solution)/shard_map/all_to_all | solution.py:129
  73.2 40.9 %copy-start.2 = (f32[3,256,1024]{2,1,0:T(8,128)}, f32[3,256,1024]{2,1,0:T(8,128)S(1)}, u32[]{:S(2)}) copy-start(f32[3,256,1024]{2,1,0:T(8,128)S(1)} %get-tuple-element.355) | copy-start | bytes 9437188
  73.9 13.1 %all-to-all-start.7 = ((f32[16,3,256]{2,1,0:T(4,128)}), f32[16,3,256]{2,1,0:T(4,128)S(1)}, u32[]{:S(2)}, u32[]{:S(2)}) async-start(f32[16,3,256]{2,1,0:T(4,128)} %broadcast_in_dim.153), calls=%async_computation.7 | async-start | bytes 131072 | tf_op jit(solution)/shard_map/all_to_all | solution.py:34
  87.0 10.3 %copy-start.43 = (bf16[256,384]{1,0:T(8,128)(2,1)S(1)}, bf16[256,384]{1,0:T(8,128)(2,1)}, u32[]{:S(2)}) copy-start(bf16[256,384]{1,0:T(8,128)(2,1)} %param.18) | copy-start | bytes 589828
  87.6 93.0 %all-to-all-start.3 = ((bf16[16,512,384]{2,1,0:T(8,128)(2,1)}), bf16[16,512,384]{2,1,0:T(8,128)(2,1)}, u32[]{:S(2)}, u32[]{:S(2)}) async-start(bf16[16,512,384]{2,1,0:T(8,128)(2,1)} %pad_maximum_fusion.17), calls=%async_computation.3 | async-start | bytes 12582912 | tf_op jit(solution)/shard_map/all_to_all | solution.py:25
  180.6 17.5 %all-to-all-start.4 = ((bf16[128,8,384]{0,2,1:T(8,128)(2,1)}), bf16[128,8,384]{0,2,1:T(8,128)(2,1)S(1)}, u32[]{:S(2)}, u32[]{:S(2)}) async-start(bf16[128,8,384]{0,2,1:T(8,128)(2,1)} %bitcast.226), calls=%async_computation.4 | async-start | bytes 1572864 | tf_op jit(solution)/shard_map/all_to_all | solution.py:132
  203.7 279.9 %all-to-all-start.8 = ((f32[16,1,99072]{2,1,0:T(1,128)}), f32[16,1,99072]{2,1,0:T(1,128)}, u32[]{:S(2)}, u32[]{:S(2)}) async-start(f32[16,1,99072]{2,1,0:T(1,128)} %broadcast_in_dim.156), calls=%async_computation.8 | async-start | bytes 12681216 | tf_op jit(solution)/shard_map/all_to_all | solution.py:34
  273.5 9.3 %copy-start.40 = (bf16[2,4,128,3,128]{2,4,3,1,0:T(8,128)(2,1)}, bf16[2,4,128,3,128]{2,4,3,1,0:T(8,128)(2,1)S(1)}, u32[]{:S(2)}) copy-start(bf16[2,4,128,3,128]{2,4,3,1,0:T(8,128)(2,1)S(1)} %constant_dynamic-update-slice_fusion.2) | copy-start | bytes 2359300 | tf_op jit(solution)/shard_map/while
  317.5 9.4 %copy-start.9 = (f32[256,3,128]{0,2,1:T(8,128)}, f32[256,3,128]{0,2,1:T(8,128)S(1)}, u32[]{:S(2)}) copy-start(f32[256,3,128]{0,2,1:T(8,128)S(1)} %get-tuple-element.500) | copy-start | bytes 1179652 | tf_op jit(solution)/shard_map/while
  317.5 9.4 %copy-start.12 = (f32[256,3,128]{0,2,1:T(8,128)}, f32[256,3,128]{0,2,1:T(8,128)S(1)}, u32[]{:S(2)}) copy-start(f32[256,3,128]{0,2,1:T(8,128)S(1)} %get-tuple-element.501) | copy-start | bytes 1179652 | tf_op jit(solution)/shard_map/while
  337.8 16.2 %copy-start.17 = (bf16[256,384]{0,1:T(8,128)(2,1)S(1)}, bf16[256,384]{0,1:T(8,128)(2,1)}, u32[]{:S(2)}) copy-start(bf16[256,384]{0,1:T(8,128)(2,1)} %copy-done.16) | copy-start | bytes 589828 | tf_op jit(solution)/shard_map/while
  337.8 16.2 %copy-start.21 = (bf16[2,4,128,3,128]{2,4,3,1,0:T(8,128)(2,1)S(1)}, bf16[2,4,128,3,128]{2,4,3,1,0:T(8,128)(2,1)}, u32[]{:S(2)}) copy-start(bf16[2,4,128,3,128]{2,4,3,1,0:T(8,128)(2,1)} %copy-done.20) | copy-start | bytes 2359300 | tf_op jit(solution)/shard_map/while
  337.8 16.2 %copy-start.23 = (bf16[256,384]{0,1:T(8,128)(2,1)S(1)}, bf16[256,384]{0,1:T(8,128)(2,1)}, u32[]{:S(2)}) copy-start(bf16[256,384]{0,1:T(8,128)(2,1)} %copy-done.22) | copy-start | bytes 589828 | tf_op jit(solution)/shard_map/while
  337.8 16.2 %copy-start.51 = (s32[2,4,8]{2,1,0:T(4,128)S(1)}, s32[2,4,8]{2,1,0:T(4,128)}, u32[]{:S(2)}) copy-start(s32[2,4,8]{2,1,0:T(4,128)} %copy-done.50) | copy-start | bytes 772 | tf_op jit(solution)/shard_map/while
  400.2 9.3 %copy-start.40 = (bf16[2,4,128,3,128]{2,4,3,1,0:T(8,128)(2,1)}, bf16[2,4,128,3,128]{2,4,3,1,0:T(8,128)(2,1)S(1)}, u32[]{:S(2)}) copy-start(bf16[2,4,128,3,128]{2,4,3,1,0:T(8,128)(2,1)S(1)} %constant_dynamic-update-slice_fusion.2) | copy-start | bytes 2359300 | tf_op jit(solution)/shard_map/while
  444.3 9.4 %copy-start.9 = (f32[256,3,128]{0,2,1:T(8,128)}, f32[256,3,128]{0,2,1:T(8,128)S(1)}, u32[]{:S(2)}) copy-start(f32[256,3,128]{0,2,1:T(8,128)S(1)} %get-tuple-element.500) | copy-start | bytes 1179652 | tf_op jit(solution)/shard_map/while
  444.3 9.4 %copy-start.12 = (f32[256,3,128]{0,2,1:T(8,128)}, f32[256,3,128]{0,2,1:T(8,128)S(1)}, u32[]{:S(2)}) copy-start(f32[256,3,128]{0,2,1:T(8,128)S(1)} %get-tuple-element.501) | copy-start | bytes 1179652 | tf_op jit(solution)/shard_map/while
  464.6 16.3 %copy-start.17 = (bf16[256,384]{0,1:T(8,128)(2,1)S(1)}, bf16[256,384]{0,1:T(8,128)(2,1)}, u32[]{:S(2)}) copy-start(bf16[256,384]{0,1:T(8,128)(2,1)} %copy-done.16) | copy-start | bytes 589828 | tf_op jit(solution)/shard_map/while
  464.6 16.3 %copy-start.21 = (bf16[2,4,128,3,128]{2,4,3,1,0:T(8,128)(2,1)S(1)}, bf16[2,4,128,3,128]{2,4,3,1,0:T(8,128)(2,1)}, u32[]{:S(2)}) copy-start(bf16[2,4,128,3,128]{2,4,3,1,0:T(8,128)(2,1)} %copy-done.20) | copy-start | bytes 2359300 | tf_op jit(solution)/shard_map/while
  464.6 16.3 %copy-start.23 = (bf16[256,384]{0,1:T(8,128)(2,1)S(1)}, bf16[256,384]{0,1:T(8,128)(2,1)}, u32[]{:S(2)}) copy-start(bf16[256,384]{0,1:T(8,128)(2,1)} %copy-done.22) | copy-start | bytes 589828 | tf_op jit(solution)/shard_map/while
  464.6 16.3 %copy-start.51 = (s32[2,4,8]{2,1,0:T(4,128)S(1)}, s32[2,4,8]{2,1,0:T(4,128)}, u32[]{:S(2)}) copy-start(s32[2,4,8]{2,1,0:T(4,128)} %copy-done.50) | copy-start | bytes 772 | tf_op jit(solution)/shard_map/while
  483.6 28.3 %all-to-all-start.6 = ((bf16[8,128,384]{2,1,0:T(8,128)(2,1)}), bf16[8,128,384]{2,1,0:T(8,128)(2,1)S(1)}, u32[]{:S(2)}, u32[]{:S(2)}) async-start(bf16[8,128,384]{2,1,0:T(8,128)(2,1)} %copy.521), calls=%async_computation.6 | async-start | bytes 1572864 | tf_op jit(solution)/shard_map/all_to_all | solution.py:340
  511.9 6.6 copy-start.44
  511.9 7.9 copy-start.13
  511.9 7.9 copy-start.47
  511.9 8.0 copy-start.10
  512.8 202.4 %all-to-all-start.9 = ((f32[16,512,384]{2,1,0:T(8,128)}), f32[16,512,384]{2,1,0:T(8,128)}, u32[]{:S(2)}, u32[]{:S(2)}) async-start(f32[16,512,384]{2,1,0:T(8,128)} %pad_maximum_fusion.16), calls=%async_computation.9 | async-start | bytes 25165824 | tf_op jit(solution)/shard_map/all_to_all | solution.py:25
  517.9 282.0 %all-reduce.3.cloned.1.call-start = ((), (), s32[]{:S(2)}) async-start(), calls=%async_computation.12 | async-start | bytes 2359296 | tf_op jit(solution)/shard_map/psum | solution.py:315
  532.0 9.2 %copy-start.3 = (f32[3,256,1024]{2,1,0:T(8,128)S(1)}, f32[3,256,1024]{2,1,0:T(8,128)}, u32[]{:S(2)}) copy-start(f32[3,256,1024]{2,1,0:T(8,128)} %copy-done.2) | copy-start | bytes 9437188
  715.2 35.8 %all-to-all-start.5 = ((bf16[8,128,384]{1,2,0:T(8,128)(2,1)}), bf16[8,128,384]{1,2,0:T(8,128)(2,1)}, u32[]{:S(2)}, u32[]{:S(2)}) async-start(bf16[8,128,384]{1,2,0:T(8,128)(2,1)} %bitcast.235), calls=%async_computation.5 | async-start | bytes 1572864 | tf_op jit(solution)/shard_map/all_to_all | solution.py:339
  722.6 10.7 %copy-start.55 = (s32[32]{0:T(128)S(1)}, s32[32]{0:T(128)}, u32[]{:S(2)}) copy-start(s32[32]{0:T(128)} %fusion.59) | copy-start | bytes 388
  751.0 41.5 %all-to-all-start.10 = ((bf16[8,128,384]{2,1,0:T(8,128)(2,1)}), bf16[8,128,384]{2,1,0:T(8,128)(2,1)}, u32[]{:S(2)}, u32[]{:S(2)}) async-start(bf16[8,128,384]{2,1,0:T(8,128)(2,1)} %convert_element_type.111), calls=%async_computation.10 | async-start | bytes 1572864 | tf_op jit(solution)/shard_map/all_to_all | solution.py:341
  763.7 7.7 copy-start.14
  763.7 7.7 copy-start.28
  791.5 10.8 %copy-start.26 = (bf16[256,384]{0,1:T(8,128)(2,1)S(1)}, bf16[256,384]{0,1:T(8,128)(2,1)}, u32[]{:S(2)}) copy-start(bf16[256,384]{0,1:T(8,128)(2,1)} %copy-done.24) | copy-start | bytes 589828
  792.5 9.8 %copy-start.31 = (f32[3,256,256]{1,2,0:T(8,128)S(1)}, f32[3,256,256]{1,2,0:T(8,128)}, u32[]{:S(2)}) copy-start(f32[3,256,256]{1,2,0:T(8,128)} %fusion.35) | copy-start | bytes 2359300
  792.5 17.8 %all-to-all-start.11 = ((bf16[8,128,384]{2,1,0:T(8,128)(2,1)}), bf16[8,128,384]{2,1,0:T(8,128)(2,1)S(1)}, u32[]{:S(2)}, u32[]{:S(2)}) async-start(bf16[8,128,384]{2,1,0:T(8,128)(2,1)} %convert_element_type.115), calls=%async_computation.11 | async-start | bytes 1572864 | tf_op jit(solution)/shard_map/all_to_all | solution.py:342
  (43 other events, 122.1 us)
Sparse Core Ops, SparseCore 0:
  556.1 220.8 all-reduce.2
where the time goes:
time: 834 us; the launch traced here: 819 us
  local copies, waits for them, and re-layouts  266 us (32%)
  waiting for transfers between devices  237 us (28%)
  other arithmetic  145 us (17%)
  starting transfers between devices  87.9 us (11%)
  matrix products  67.1 us (8%)
  between operations  14.9 us (2%)
    all_to_all x2, waiting for transfers between devices, sent_together(): lax.all_to_all(both, axis, split_axis=split_dim, concat_axis=concat_dim,...  218 us
    reshape x8, local copies, waits for them, and re-layouts, spread_grads(): grad_blk[:, :KT * TILE].reshape(block_tiles, KT, TILE, pool_total.shape[2])  81.1 us
    scatter-add x4, other arithmetic, spread_grads(): pool_total.at[pool_slot].add(tile_part)  65.2 us
    reshape x8, local copies, waits for them, and re-layouts, block_rows(): picked = pool[slot_blk].reshape(block_tiles, KT * TILE, head_count, HD)  30.4 us
    unnamed x95, local copies, waits for them, and re-layouts  27.3 us
    all_to_all x2, starting transfers between devices, from_everyone(): lax.all_to_all(jnp.broadcast_to(shard[None], (length, *shard.shape)), axi...  22.1 us
  transfers between devices with their start and end apart: 13, of which 5 were waited for; matrix products, arithmetic and copies ran while one was open for 56% of the time, Pallas kernels for 0%

commit v1 on v0

v1 whole, which is shorter than its diff:
```python
import functools

import jax
import jax.numpy as jnp
from jax import lax
from jax.experimental import pallas as pl
from jax.experimental.pallas import tpu as pltpu
from jax.sharding import PartitionSpec as P

HD = 128
TXT = 256
TILE = 128
KT = 8
MOST = 2
GROUPS = 16
HEADS = 8
TILES = 8
NH = 3
W = NH * HD
SLOTS = GROUPS * MOST
POOL = TILES + SLOTS
TROWS = TXT // GROUPS
TLOCAL = TILES * TILE
TCHUNKS = TLOCAL // 256 + 1
BACK = MOST * 2 * TILE + 3 * TROWS

NEGATIVE = -1e30
FACTOR = HD**-0.5
LOG2E = 1.4426950408889634
FACTOR2 = FACTOR * LOG2E
VMEM_LIMIT = 60 * 1024 * 1024

F32 = jnp.float32
BF16 = jnp.bfloat16
SMEM = pltpu.SMEM
ANY = pl.ANY


def dot_nt(a, b):
    return lax.dot_general(a, b, (((1,), (1,)), ((), ())), preferred_element_type=F32)


def dot_nn(a, b):
    return lax.dot_general(a, b, (((1,), (0,)), ((), ())), preferred_element_type=F32)


def dot_tn(a, b):
    return lax.dot_general(a, b, (((0,), (0,)), ((), ())), preferred_element_type=F32)


def params(**kw):
    return pltpu.CompilerParams(vmem_limit_bytes=VMEM_LIMIT, **kw)


def cost(flops, nbytes, exps=0):
    return pl.CostEstimate(
        flops=int(flops), bytes_accessed=int(nbytes), transcendentals=int(exps)
    )


def pack_kernel(k_ref, v_ref, q_ref, g_ref, o_ref):
    for n, ref in enumerate((k_ref, v_ref, q_ref, g_ref)):
        o_ref[0, n] = ref[...]


def pack(k, v, q, g):
    spec = pl.BlockSpec((TILE, W), lambda h: (0, h))
    return pl.pallas_call(
        pack_kernel,
        grid=(HEADS,),
        in_specs=[spec] * 4,
        out_specs=pl.BlockSpec((1, 4, TILE, W), lambda h: (h, 0, 0, 0)),
        out_shape=jax.ShapeDtypeStruct((HEADS, 4, TILE, W), BF16),
        compiler_params=params(),
        cost_estimate=cost(0, 8 * TILE * HEADS * W * 2),
        name="pack",
    )(k, v, q, g)


def unpack_kernel(x_ref, a_ref, b_ref, c_ref, d_ref):
    for n, ref in enumerate((a_ref, b_ref, c_ref, d_ref)):
        ref[...] = x_ref[0, n]


def unpack(x):
    spec = pl.BlockSpec((TILE, W), lambda h: (0, h))
    return pl.pallas_call(
        unpack_kernel,
        grid=(HEADS,),
        in_specs=[pl.BlockSpec((1, 4, TILE, W), lambda h: (h, 0, 0, 0))],
        out_specs=[spec] * 4,
        out_shape=[jax.ShapeDtypeStruct((TILE, HEADS * W), BF16)] * 4,
        compiler_params=params(),
        cost_estimate=cost(0, 8 * TILE * HEADS * W * 2),
        name="unpack",
    )(x)


def pick_kernel(sel_ref, x_ref, o_ref, sems):
    copies = [
        pltpu.make_async_copy(x_ref.at[sel_ref[s]], o_ref.at[s], sems.at[s])
        for s in range(SLOTS)
    ]
    for copy in copies:
        copy.start()
    for copy in copies:
        copy.wait()


def pick(sel, x):
    return pl.pallas_call(
        pick_kernel,
        grid=(1,),
        in_specs=[
            pl.BlockSpec(memory_space=SMEM),
            pl.BlockSpec((TILES, 2, TILE, W), lambda i: (0, 0, 0, 0)),
        ],
        out_specs=pl.BlockSpec(memory_space=ANY),
        out_shape=jax.ShapeDtypeStruct((SLOTS, 2, TILE, W), BF16),
        scratch_shapes=[pltpu.SemaphoreType.DMA((SLOTS,))],
        compiler_params=params(),
        cost_estimate=cost(0, (SLOTS + TILES) * 2 * TILE * W * 2),
        name="pick",
    )(sel, x)


def text_chunk(x_ref, text_ref, which, c, lanes):
    if c < TCHUNKS - 1:
        return x_ref[2 * c : 2 * c + 2, which, :, lanes].reshape(256, HD)
    return text_ref[:, lanes]


def head_lanes(j):
    return pl.ds(pl.multiple_of(j * HD, HD), HD)


def text_forward_kernel(n_ref, tq_ref, tk_ref, tv_ref, x_ref, o_ref, s_ref):
    live = lax.broadcasted_iota(jnp.int32, (TXT, TXT), 1) < n_ref[0]
    lane = lax.broadcasted_iota(jnp.int32, (TXT, HD), 1)
    o_ref[:, W:] = jnp.zeros((TXT, HD), F32)

    def head(j, carry):
        lanes = head_lanes(j)
        query = tq_ref[:, lanes]
        top = None
        for c in range(TCHUNKS):
            s = dot_nt(query, text_chunk(x_ref, tk_ref, 0, c, lanes)) * FACTOR2
            if c == TCHUNKS - 1:
                s = jnp.where(live, s, NEGATIVE)
            s_ref[c] = s
            top = s if top is None else jnp.maximum(top, s)
        top = jnp.max(top, axis=1, keepdims=True)
        total, out = None, None
        for c in range(TCHUNKS):
            p = jnp.exp2(s_ref[c] - top)
            part = dot_nn(p.astype(BF16), text_chunk(x_ref, tv_ref, 1, c, lanes))
            total = p if total is None else total + p
            out = part if out is None else out + part
        total = jnp.sum(total, axis=1, keepdims=True)
        o_ref[:, lanes] = out
        stats = o_ref[:, W:]
        stats = jnp.where(lane == j, top, stats)
        o_ref[:, W:] = jnp.where(lane == j + 8, total, stats)
        return carry

    lax.fori_loop(0, NH, head, 0)


def whole(shape):
    return pl.BlockSpec(shape, lambda i: (0,) * len(shape))


TEXT = (TXT, W)
LOCAL_KV = (TILES, 2, TILE, W)


def text_forward(n, tq, tk, tv, x):
    return pl.pallas_call(
        text_forward_kernel,
        grid=(1,),
        in_specs=[pl.BlockSpec(memory_space=SMEM)] + [whole(TEXT)] * 3 + [whole(LOCAL_KV)],
        out_specs=whole((TXT, W + HD)),
        out_shape=jax.ShapeDtypeStruct((TXT, W + HD), F32),
        scratch_shapes=[pltpu.VMEM((TCHUNKS, TXT, 256), F32)],
        compiler_params=params(),
        cost_estimate=cost(4 * NH * TXT * TCHUNKS * 256 * HD, 3 << 20, NH * TXT * 1280),
        name="text_forward",
    )(n, tq, tk, tv, x)


def merged(flag_ref, a_ref, b_ref, j, lanes):
    swap = flag_ref[0] > 0
    stats_a = jnp.where(swap, b_ref[:, W:], a_ref[:, W:])
    stats_b = jnp.where(swap, a_ref[:, W:], b_ref[:, W:])
    lane = lax.broadcasted_iota(jnp.int32, (TXT, HD), 1)

    def column(stats, at):
        return jnp.sum(jnp.where(lane == at, stats, 0.0), axis=1, keepdims=True)

    top_a, top_b = column(stats_a, j), column(stats_b, j)
    top = jnp.maximum(top_a, top_b)
    scale_a, scale_b = jnp.exp2(top_a - top), jnp.exp2(top_b - top)
    total = column(stats_a, j + 8) * scale_a + column(stats_b, j + 8) * scale_b
    out_a = jnp.where(swap, b_ref[:, lanes], a_ref[:, lanes])
    out_b = jnp.where(swap, a_ref[:, lanes], b_ref[:, lanes])
    out = out_a * scale_a + out_b * scale_b
    return top, total, out


def text_merge_kernel(flag_ref, a_ref, b_ref, o_ref):
    lane = lax.broadcasted_iota(jnp.int32, (TXT, HD), 1)
    stats = jnp.zeros((TXT, HD), F32)
    for j in range(NH):
        lanes = slice(j * HD, (j + 1) * HD)
        top, total, out = merged(flag_ref, a_ref, b_ref, j, lanes)
        o_ref[:, lanes] = out
        stats = jnp.where(lane == j, top, stats)
        stats = jnp.where(lane == j + 8, total, stats)
    o_ref[:, W:] = stats


def text_merge(flag, a, b):
    return pl.pallas_call(
        text_merge_kernel,
        grid=(1,),
        in_specs=[pl.BlockSpec(memory_space=SMEM)] + [whole((TXT, W + HD))] * 2,
        out_specs=whole((TXT, W + HD)),
        out_shape=jax.ShapeDtypeStruct((TXT, W + HD), F32),
        compiler_params=params(),
        cost_estimate=cost(TXT * W * 4, 3 * TXT * (W + HD) * 4),
        name="text_merge",
    )(flag, a, b)


def text_backward_kernel(
    n_ref, flag_ref, a_ref, b_ref, tq_ref, tk_ref, tv_ref, tg_ref, x_ref, out_ref, tqg_ref, acc_ref, dx_ref
):
    live = lax.broadcasted_iota(jnp.int32, (TXT, TXT), 1) < n_ref[0]

    def head(j, carry):
        lanes = head_lanes(j)
        top, total, out = merged(flag_ref, a_ref, b_ref, j, lanes)
        out = out / total
        out_ref[:, lanes] = out.astype(BF16)
        log_total = top + jnp.log2(total)
        query, grad = tq_ref[:, lanes], tg_ref[:, lanes]
        offset = jnp.sum(grad.astype(F32) * out, axis=1, keepdims=True)
        query_grad = None
        for c in range(TCHUNKS):
            key = text_chunk(x_ref, tk_ref, 0, c, lanes)
            value = text_chunk(x_ref, tv_ref, 1, c, lanes)
            s = dot_nt(query, key) * FACTOR2
            if c == TCHUNKS - 1:
                s = jnp.where(live, s, NEGATIVE)
            p = jnp.exp2(s - log_total)
            ds = (p * (dot_nt(grad, value) - offset)).astype(BF16)
            p = p.astype(BF16)
            part = dot_nn(ds, key)
            query_grad = part if query_grad is None else query_grad + part
            key_grad = dot_tn(ds, query)
            value_grad = dot_tn(p, grad)
            if c < TCHUNKS - 1:
                dx_ref[2 * c : 2 * c + 2, 0, :, lanes] = key_grad.reshape(2, TILE, HD)
                dx_ref[2 * c : 2 * c + 2, 1, :, lanes] = value_grad.reshape(2, TILE, HD)
            else:
                acc_ref[0, :, lanes] = key_grad
                acc_ref[1, :, lanes] = value_grad
        tqg_ref[:, lanes] = query_grad * FACTOR
        return carry

    lax.fori_loop(0, NH, head, 0)


def text_backward(n, flag, a, b, tq, tk, tv, tg, x):
    return pl.pallas_call(
        text_backward_kernel,
        grid=(1,),
        in_specs=[pl.BlockSpec(memory_space=SMEM)] * 2
        + [whole((TXT, W + HD))] * 2
        + [whole(TEXT)] * 4
        + [whole(LOCAL_KV)],
        out_specs=[whole(TEXT), whole(TEXT), whole((2, TXT, W)), whole(LOCAL_KV)],
        out_shape=[
            jax.ShapeDtypeStruct(TEXT, BF16),
            jax.ShapeDtypeStruct(TEXT, F32),
            jax.ShapeDtypeStruct((2, TXT, W), F32),
            jax.ShapeDtypeStruct(LOCAL_KV, F32),
        ],
        compiler_params=params(),
        cost_estimate=cost(10 * NH * TXT * TCHUNKS * 256 * HD, 8 << 20, NH * TXT * 1280),
        name="text_backward",
    )(n, flag, a, b, tq, tk, tv, tg, x)


CHUNKS = KT // 2 + 1


def video_kernel(
    slot_ref,
    count_ref,
    n_ref,
    kv_ref,
    qg_ref,
    got_ref,
    tk_ref,
    tv_ref,
    tqg_ref,
    tacc_ref,
    dx_ref,
    out_ref,
    back_ref,
    own_ref,
    keys,
    values,
    s_ref,
    p_ref,
    dk_acc,
    dv_acc,
    tk_acc,
    tv_acc,
    pool,
):
    pool[:TILES] = kv_ref[...]
    pool[TILES:] = got_ref[...]
    keys[0] = tk_ref[...]
    values[0] = tv_ref[...]
    dk_acc[:TILES] = dx_ref[:, 0]
    dv_acc[:TILES] = dx_ref[:, 1]
    dk_acc[TILES:] = jnp.zeros((SLOTS, TILE, HD), F32)
    dv_acc[TILES:] = jnp.zeros((SLOTS, TILE, HD), F32)
    tk_acc[...] = tacc_ref[0]
    tv_acc[...] = tacc_ref[1]
    text_live = lax.broadcasted_iota(jnp.int32, (TXT, TILE), 0) < n_ref[0]

    def tile(i, carry):
        count = count_ref[i]
        query, grad = qg_ref[i, 0], qg_ref[i, 1]

        def run(pairs):
            slots = [slot_ref[i * KT + e] for e in range(2 * pairs)]
            for e in range(2 * pairs):
                half = pl.ds((e % 2) * TILE, TILE)
                keys[1 + e // 2, half] = pool[slots[e], 0]
                values[1 + e // 2, half] = pool[slots[e], 1]
            top = None
            for c in range(pairs + 1):
                s = dot_nt(keys[c], query) * FACTOR2
                if c == 0:
                    s = jnp.where(text_live, s, NEGATIVE)
                elif c == pairs:
                    s = jnp.concatenate(
                        [s[:TILE], jnp.where(2 * pairs <= count, s[TILE:], NEGATIVE)], axis=0
                    )
                s_ref[c] = s
                part = jnp.max(s.reshape(32, 8, TILE), axis=0)
                top = part if top is None else jnp.maximum(top, part)
            top = jnp.max(top, axis=0, keepdims=True)
            total = None
            for c in range(pairs + 1):
                p = jnp.exp2(s_ref[c] - top)
                s_ref[c] = p
                part = jnp.sum(p.reshape(32, 8, TILE), axis=0)
                total = part if total is None else total + part
            scale = 1.0 / jnp.sum(total, axis=0, keepdims=True)
            out = None
            for c in range(pairs + 1):
                p = s_ref[c] * scale
                s_ref[c] = p
                p = p.astype(BF16)
                p_ref[c] = p
                part = dot_tn(p, values[c])
                out = part if out is None else out + part
            out_ref[i, 0] = out.astype(BF16)
            offset = jnp.sum((grad.astype(F32) * out).T, axis=0, keepdims=True)
            query_grad = None
            for c in range(pairs + 1):
                ds = (s_ref[c] * (dot_nt(values[c], grad) - offset)).astype(BF16)
                part = dot_tn(ds, keys[c])
                query_grad = part if query_grad is None else query_grad + part
                key_grad = dot_nn(ds, query)
                value_grad = dot_nn(p_ref[c], grad)
                if c == 0:
                    tk_acc[...] += key_grad
                    tv_acc[...] += value_grad
                else:
                    for e in (0, 1):
                        slot = slots[2 * (c - 1) + e]
                        dk_acc[slot] += key_grad[e * TILE : (e + 1) * TILE]
                        dv_acc[slot] += value_grad[e * TILE : (e + 1) * TILE]
            out_ref[i, 1] = (query_grad * FACTOR).astype(BF16)

        for pairs in range(1, KT // 2 + 1):

            @pl.when((count + 1) // 2 == pairs)
            def _():
                run(pairs)

        return carry

    lax.fori_loop(0, TILES, tile, 0)

    own_ref[:, 0] = dk_acc[:TILES]
    own_ref[:, 1] = dv_acc[:TILES]
    for g in range(GROUPS):
        for m in range(MOST):
            slot = TILES + g * MOST + m
            back_ref[g, 2 * m * TILE : (2 * m + 1) * TILE] = (dk_acc[slot] * FACTOR).astype(BF16)
            back_ref[g, (2 * m + 1) * TILE : (2 * m + 2) * TILE] = dv_acc[slot].astype(BF16)
        rows = slice(g * TROWS, (g + 1) * TROWS)
        at = MOST * 2 * TILE
        back_ref[g, at : at + TROWS] = tqg_ref[rows].astype(BF16)
        back_ref[g, at + TROWS : at + 2 * TROWS] = (tk_acc[rows] * FACTOR).astype(BF16)
        back_ref[g, at + 2 * TROWS : at + 3 * TROWS] = tv_acc[rows].astype(BF16)


def video(slot, count, n, x, got, tk, tv, tqg, tacc, dx):
    smem = pl.BlockSpec(memory_space=SMEM)
    text = pl.BlockSpec((TXT, HD), lambda j: (0, j))
    pair = (TILES, 2, TILE, HD)
    return pl.pallas_call(
        video_kernel,
        grid=(NH,),
        in_specs=[
            smem,
            smem,
            smem,
            pl.BlockSpec(pair, lambda j: (0, 0, 0, j)),
            pl.BlockSpec(pair, lambda j: (0, 1, 0, j)),
            pl.BlockSpec((SLOTS, 2, TILE, HD), lambda j: (0, 0, 0, j)),
            text,
            text,
            text,
            pl.BlockSpec((2, TXT, HD), lambda j: (0, 0, j)),
            pl.BlockSpec(pair, lambda j: (0, 0, 0, j)),
        ],
        out_specs=[
            pl.BlockSpec(pair, lambda j: (0, 0, 0, j)),
            pl.BlockSpec((GROUPS, BACK, HD), lambda j: (0, 0, j)),
            pl.BlockSpec(pair, lambda j: (0, 0, 0, j)),
        ],
        out_shape=[
            jax.ShapeDtypeStruct((TILES, 2, TILE, W), BF16),
            jax.ShapeDtypeStruct((GROUPS, BACK, W), BF16),
            jax.ShapeDtypeStruct((TILES, 2, TILE, W), F32),
        ],
        scratch_shapes=[
            pltpu.VMEM((CHUNKS, 256, HD), BF16),
            pltpu.VMEM((CHUNKS, 256, HD), BF16),
            pltpu.VMEM((CHUNKS, 256, TILE), F32),
            pltpu.VMEM((CHUNKS, 256, TILE), BF16),
            pltpu.VMEM((POOL, TILE, HD), F32),
            pltpu.VMEM((POOL, TILE, HD), F32),
            pltpu.VMEM((TXT, HD), F32),
            pltpu.VMEM((TXT, HD), F32),
            pltpu.VMEM((POOL, 2, TILE, HD), BF16),
        ],
        compiler_params=params(),
        cost_estimate=cost(12 * NH * TLOCAL * 1280 * HD, 24 << 20, NH * TLOCAL * 1280),
        name="video",
    )(slot, count, n, x, x, got, tk, tv, tqg, tacc, dx)


def combine_kernel(sel_ref, back_ref, own_ref, half_ref, out_ref, text_ref, acc):
    acc[:, 0] = own_ref[:, 0] * FACTOR
    acc[:, 1] = own_ref[:, 1]

    def add(g, carry):
        for m in range(MOST):
            at = sel_ref[g * MOST + m]
            part = back_ref[g, 2 * m * TILE : 2 * (m + 1) * TILE].astype(F32)
            acc[at] += part.reshape(2, TILE, HD)
        return carry

    lax.fori_loop(0, GROUPS, add, 0)
    out_ref[:, :2] = half_ref[...]
    out_ref[:, 2:] = acc[...].astype(BF16)
    text = None
    for g in range(GROUPS):
        part = back_ref[g, MOST * 2 * TILE :].astype(F32)
        text = part if text is None else text + part
    text_ref[...] = text.astype(BF16)


def combine(sel, back, own, half):
    pair = (TILES, 2, TILE, HD)
    return pl.pallas_call(
        combine_kernel,
        grid=(NH,),
        in_specs=[
            pl.BlockSpec(memory_space=SMEM),
            pl.BlockSpec((GROUPS, BACK, HD), lambda j: (0, 0, j)),
            pl.BlockSpec(pair, lambda j: (0, 0, 0, j)),
            pl.BlockSpec(pair, lambda j: (0, 0, 0, j)),
        ],
        out_specs=[
            pl.BlockSpec((TILES, 4, TILE, HD), lambda j: (0, 0, 0, j)),
            pl.BlockSpec((3 * TROWS, HD), lambda j: (0, j)),
        ],
        out_shape=[
            jax.ShapeDtypeStruct((TILES, 4, TILE, W), BF16),
            jax.ShapeDtypeStruct((3 * TROWS, W), BF16),
        ],
        scratch_shapes=[pltpu.VMEM(pair, F32)],
        compiler_params=params(),
        cost_estimate=cost(TLOCAL * W * 64, 16 << 20),
        name="combine",
    )(sel, back, own, half)


STEPS = ((1, 1), (2, 2), (4, 6), (8, 8))


def swapped(x, mask):
    return lax.ppermute(x, "seq", [(i, i ^ mask) for i in range(GROUPS)])


def tables(tile_list, tile_count, own):
    live = jnp.arange(KT)[None, :] < tile_count[:, None]
    listed = jnp.where(live, tile_list, -1)

    def ranked(wanted):
        before = jnp.arange(TILES)[:, None] < jnp.arange(TILES)[None, :]
        return jnp.sum(jnp.where(before[None], wanted[:, :, None], 0), axis=1)

    mine = own * TILES + jnp.arange(TILES)
    asked = jnp.any(
        listed.reshape(GROUPS, TILES * KT, 1) == mine[None, None, :], axis=1
    ).astype(jnp.int32)
    rank = ranked(asked)
    chosen = (asked[:, None, :] > 0) & (rank[:, None, :] == jnp.arange(MOST)[None, :, None])
    sel = jnp.sum(jnp.where(chosen, jnp.arange(TILES)[None, None, :], 0), axis=2).reshape(SLOTS)

    my_list = lax.dynamic_slice_in_dim(listed, own * TILES, TILES, 0).reshape(TILES * KT)
    hits = my_list[:, None] == jnp.arange(GROUPS * TILES)[None, :]
    needed = jnp.any(hits, axis=0).astype(jnp.int32).reshape(GROUPS, TILES)
    where_to = TILES + jnp.arange(GROUPS)[:, None] * MOST + jnp.minimum(ranked(needed), MOST - 1)
    local = jnp.arange(GROUPS)[:, None] == own
    where_to = jnp.where(local, jnp.arange(TILES)[None, :], where_to).reshape(GROUPS * TILES)
    slot = jnp.sum(jnp.where(hits, where_to[None, :], 0), axis=1)
    count = lax.dynamic_slice_in_dim(tile_count, own * TILES, TILES, 0)
    return sel.astype(jnp.int32), slot.astype(jnp.int32), count.astype(jnp.int32)


def body(
    video_query,
    video_key,
    video_value,
    video_grad,
    text_query,
    text_key,
    text_value,
    text_grad,
    tile_list,
    tile_count,
    text_mask,
):
    own = lax.axis_index("seq")
    x = lax.all_to_all(
        pack(video_key, video_value, video_query, video_grad), "head", 0, 0, tiled=True
    )
    sel, slot, count = tables(tile_list, tile_count, own)
    n = jnp.sum((text_mask > 0).astype(jnp.int32)).reshape(1)
    n_own = jnp.where(own == 0, n, 0)

    got = lax.all_to_all(
        pick(sel, x).reshape(GROUPS, MOST * 2 * TILE, W), "seq", 0, 0, tiled=True
    ).reshape(SLOTS, 2, TILE, W)

    part = text_forward(n_own, text_query, text_key, text_value, x)
    upper = [((own & bit) > 0).astype(jnp.int32).reshape(1) for bit, _ in STEPS]
    for flag, (_, mask) in zip(upper[:-1], STEPS[:-1]):
        part = text_merge(flag, part, swapped(part, mask))
    other = swapped(part, STEPS[-1][1])
    attended_text, tqg, tacc, dx = text_backward(
        n_own, upper[-1], part, other, text_query, text_key, text_value, text_grad, x
    )

    half, back, own_grads = video(slot, count, n, x, got, text_key, text_value, tqg, tacc, dx)
    back = lax.all_to_all(back, "seq", 0, 0, tiled=True)
    packed, text_rows = combine(sel, back, own_grads, half)

    gathered = text_rows.reshape(1, 3, TROWS, W)
    for bit, mask in STEPS:
        theirs = swapped(gathered, mask)
        first = jnp.concatenate([gathered, theirs], axis=0)
        second = jnp.concatenate([theirs, gathered], axis=0)
        gathered = jnp.where((own & bit) == 0, first, second)
    text_grads = jnp.transpose(gathered, (1, 0, 2, 3)).reshape(3, TXT, W)

    attended_video, video_query_grad, video_key_grad, video_value_grad = unpack(
        lax.all_to_all(packed, "head", 0, 0, tiled=True)
    )
    return (
        attended_video,
        video_query_grad,
        video_key_grad,
        video_value_grad,
        attended_text,
        text_grads[0],
        text_grads[1],
        text_grads[2],
    )


def solution(mesh):
    tokens, heads = P(("seq", "head"), None), P(None, "head")
    return jax.shard_map(
        body,
        mesh=mesh,
        in_specs=(tokens,) * 4 + (heads,) * 4 + (P(),) * 3,
        out_specs=(tokens,) * 4 + (heads,) * 4,
        check_vma=False,
    )
```

time: 834 us -> 391 us (0.47); the launches traced: 819 us -> 389 us
  local copies, waits for them, and re-layouts: 266 us -> 9.37 us
  other arithmetic: 145 us -> 4.42 us
  Pallas kernels: 0 us -> 90.3 us
  blocking collectives: 0 us -> 82.4 us
  matrix products: 67.1 us -> 0 us
  starting transfers between devices: 87.9 us -> 25.5 us
  waiting for transfers between devices: 237 us -> 176 us
  between operations: 14.9 us -> 1.4 us
    all_to_all x12 -> x3, waiting for transfers between devices: 237 us -> 34.7 us  [the longest x1 34.7 us: body(): lax.all_to_all(pack(video_key, video_value, video_query, video_grad), 'he...]
    ppermute x0 -> x8, waiting for transfers between devices: none -> 141 us  [swapped(): return lax.ppermute(x, 'seq', [(i, i ^ mask) for i in range(GROUPS)])]
    reshape x27 -> x1, local copies, waits for them, and re-layouts: 136 us -> 0.6 us  [tables(): jnp.sum(jnp.where(chosen, jnp.arange(TILES)[None, None, :], 0), axis=2)]
    scatter-add x6 -> x0, other arithmetic: 90.5 us -> none  [the longest x4 65.2 us: spread_grads(): pool_total.at[pool_slot].add(tile_part)]
    pallas_call x0 -> x10, Pallas kernels: none -> 90.3 us  [the longest x1 44 us: video(): pl.pallas_call(video_kernel, grid=(NH,), in_specs=[smem, smem, smem, pl.B...]
    all_to_all x0 -> x1, blocking collectives: none -> 82.4 us  [body(): back = lax.all_to_all(back, 'seq', 0, 0, tiled=True)]
    all_to_all x12 -> x3, starting transfers between devices: 87.8 us -> 20.2 us  [the longest x1 7.57 us: body(): lax.all_to_all(pack(video_key, video_value, video_query, video_grad), 'he...]
    dot_general x30 -> x0, matrix products: 67.1 us -> none  [the longest x4 7.57 us: split_product(): jnp.einsum(form, upper, data, preferred_element_type=jnp.float32)]
  transfers between devices with their start and end apart: 13 -> 11, of which waited for: 5 -> 9; matrix products, arithmetic and copies ran while one was open for 56% -> 2% of each run, Pallas kernels for 0% -> 6%
where the time goes in v1:
time: 391 us; the launch traced here: 389 us
  waiting for transfers between devices  176 us (45%)
  Pallas kernels  90.3 us (23%)
  blocking collectives  82.4 us (21%)
  starting transfers between devices  25.5 us (7%)
  local copies, waits for them, and re-layouts  9.37 us (2%)
  other arithmetic  4.42 us (1%)
    ppermute x8, waiting for transfers between devices, swapped(): return lax.ppermute(x, 'seq', [(i, i ^ mask) for i in range(GROUPS)])  141 us
    all_to_all x1, blocking collectives, body(): back = lax.all_to_all(back, 'seq', 0, 0, tiled=True)  82.4 us
    pallas_call x1, Pallas kernels, video(): pl.pallas_call(video_kernel, grid=(NH,), in_specs=[smem, smem, smem, pl.B...  44 us
    all_to_all x1, waiting for transfers between devices, body(): lax.all_to_all(pack(video_key, video_value, video_query, video_grad), 'he...  34.7 us
    pallas_call x1, Pallas kernels, text_backward(): pl.pallas_call(text_backward_kernel, grid=(1,), in_specs=[pl.BlockSpec(me...  9.46 us
  transfers between devices with their start and end apart: 11, of which 9 were waited for; matrix products, arithmetic and copies ran while one was open for 2% of the time, Pallas kernels for 6%

profile of v1, /device:TPU:6, one launch (start us, length us, event | category | flops | bytes accessed | tf_op | source)
XLA Modules:
  0.0 388.9 jit_solution(7876145011007968128)
XLA Ops:
  0.6 6.3 %pack.1 = bf16[8,4,128,384]{3,2,1,0:T(8,128)(2,1)} custom-call(bf16[128,3072]{1,0:T(8,128)(2,1)} %k_ref.1, bf16[128,3072]{1,0:T(8,128)(2,1)} %v_ref.1, bf16[128,3072]{1,0:T(8,128)(2,1)} %q_ref.1, bf16[128,3072]{1,0:T(8,128)(2,1)} %g_ref.1), custom_call_target="tpu_custom_call" | custom-call | bytes 6291456 | tf_op jit(solution)/shard_map/pack/pallas_call | solution.py:68
  7.0 7.6 %all-to-all-start = ((bf16[8,4,128,384]{3,2,1,0:T(8,128)(2,1)}), bf16[8,4,128,384]{3,2,1,0:T(8,128)(2,1)S(1)}, u32[]{:S(2)}, u32[]{:S(2)}) async-start(bf16[8,4,128,384]{3,2,1,0:T(8,128)(2,1)} %pack.1), calls=%async_computation | async-start | bytes 6291456 | tf_op jit(solution)/shard_map/all_to_all | solution.py:558
  14.6 0.1 copy.29
  14.9 0.1 fusion.1
  15.2 0.1 eq.69
  15.3 0.4 compare_reduce_fusion
  15.7 0.1 copy.30
  15.9 0.1 copy.31
  16.0 0.6 reshape.136.sel_ref
  16.6 34.7 %all-to-all-done.x_ref.kv_ref.qg_ref = bf16[8,4,128,384]{3,2,1,0:T(8,128)(2,1)S(1)} async-done(((bf16[8,4,128,384]{3,2,1,0:T(8,128)(2,1)}), bf16[8,4,128,384]{3,2,1,0:T(8,128)(2,1)S(1)}, u32[]{:S(2)}, u32[]{:S(2)}) %all-to-all-start) | async-done | bytes 3145760 | tf_op jit(solution)/shard_map/all_to_all | solution.py:558
  51.3 1.6 copy-done
  52.9 4.4 %pick.1 = bf16[32,2,128,384]{3,2,1,0:T(8,128)(2,1)} custom-call(s32[32]{0:T(128)} %reshape.136.sel_ref, bf16[8,4,128,384]{3,2,1,0:T(8,128)(2,1)} %copy-done), custom_call_target="tpu_custom_call" | custom-call | bytes 7864320 | tf_op jit(solution)/shard_map/pick/pallas_call | solution.py:111
  57.3 6.8 %all-to-all-start.1 = ((bf16[16,512,384]{2,1,0:T(8,128)(2,1)}), bf16[16,512,384]{2,1,0:T(8,128)(2,1)}, u32[]{:S(2)}, u32[]{:S(2)}) async-start(bf16[16,512,384]{2,1,0:T(8,128)(2,1)} %bitcast.14), calls=%async_computation.1 | async-start | bytes 12582912 | tf_op jit(solution)/shard_map/all_to_all | solution.py:565
  64.1 0.7 fusion.4
  65.4 5.1 %text_forward.1.a_ref = f32[256,512]{1,0:T(8,128)} custom-call(s32[1]{0:T(128)S(6)} %select_n.83.n_ref, bf16[256,384]{1,0:T(8,128)(2,1)} %tq_ref.3, bf16[256,384]{1,0:T(8,128)(2,1)} %tk_ref.5, bf16[256,384]{1,0:T(8,128)(2,1)} %tv_ref.5, bf16[8,4,128,384]{3,2,1,0:T(8,128)(2,1)} %copy-done), custom_call_target="tpu_custom_call" | custom-call | flops 503316480 | bytes 3145728 | tf_op jit(solution)/shard_map/text_forward/pallas_call | solution.py:178
  70.5 0.1 collective-permute-start
  70.6 2.0 collective-permute-done.b_ref
  72.7 0.8 copy-done.4
  73.4 2.5 text_merge.3.a_ref
  76.0 1.5 collective-permute-start.1
  77.4 72.1 %collective-permute-done.1.b_ref = f32[256,512]{1,0:T(8,128)S(1)} collective-permute-done((f32[256,512]{1,0:T(8,128)}, f32[256,512]{1,0:T(8,128)S(1)}, u32[]{:S(2)}, u32[]{:S(2)}) %collective-permute-start.1) | collective-permute-done | bytes 524320 | tf_op jit(solution)/shard_map/ppermute | solution.py:514
  149.5 0.8 copy-done.5
  150.3 2.5 text_merge.4.a_ref
  152.8 0.6 dynamic_slice.7.count_ref
  153.4 16.4 %collective-permute-done.2.b_ref = f32[256,512]{1,0:T(8,128)S(1)} collective-permute-done((f32[256,512]{1,0:T(8,128)}, f32[256,512]{1,0:T(8,128)S(1)}, u32[]{:S(2)}, u32[]{:S(2)}) %collective-permute-start.2) | collective-permute-done | bytes 524320 | tf_op jit(solution)/shard_map/ppermute | solution.py:514
  169.8 0.8 copy-done.3
  170.6 2.5 text_merge.5.a_ref
  173.3 0.1 select_n.80
  173.4 0.7 select_reduce_fusion.slot_ref
  174.1 13.2 %collective-permute-done.3.b_ref = f32[256,512]{1,0:T(8,128)S(1)} collective-permute-done((f32[256,512]{1,0:T(8,128)}, f32[256,512]{1,0:T(8,128)S(1)}, u32[]{:S(2)}, u32[]{:S(2)}) %collective-permute-start.3) | collective-permute-done | bytes 524320 | tf_op jit(solution)/shard_map/ppermute | solution.py:514
  187.2 0.8 copy-done.6
  188.0 9.5 %text_backward.1 = (bf16[256,384]{1,0:T(8,128)(2,1)}, f32[256,384]{1,0:T(8,128)}, f32[2,256,384]{2,1,0:T(8,128)}, f32[8,2,128,384]{3,2,1,0:T(8,128)}) custom-call(s32[1]{0:T(128)S(6)} %select_n.83.n_ref, s32[1]{0:T(128)} %bitcast.4.flag_ref, f32[256,512]{1,0:T(8,128)} %text_merge.5.a_ref, f32[256,512]{1,0:T(8,128)} %copy-done.6, bf16[256,384]{1,0:T(8,128)(2,1)} %tq_ref.3, ...), custom_call_target="tpu_custom_call" | custom-call | flops 1258291200 | bytes 8388608 | tf_op jit(solution)/shard_map/text_backward/pallas_call | solution.py:275
  197.5 44.0 %video.1 = (bf16[8,2,128,384]{3,2,1,0:T(8,128)(2,1)}, bf16[16,560,384]{2,1,0:T(8,128)(2,1)}, f32[8,2,128,384]{3,2,1,0:T(8,128)}) custom-call(s32[64]{0:T(128)} %select_reduce_fusion.slot_ref, s32[8]{0:T(128)} %dynamic_slice.7.count_ref, s32[1]{0:T(128)} %bitcast.n_ref, bf16[8,4,128,384]{3,2,1,0:T(8,128)(2,1)} %copy-done, bf16[8,4,128,384]{3,2,1,0:T(8,128)(2,1)} %copy-done, ...), custom_call_target="tpu_custom_call" | custom-call | flops 6039797760 | bytes 25165824 | tf_op jit(solution)/shard_map/video/pallas_call | solution.py:420
  241.4 82.4 %all_to_all.20.back_ref = bf16[16,560,384]{2,1,0:T(8,128)(2,1)} all-to-all(bf16[16,560,384]{2,1,0:T(8,128)(2,1)} %get-tuple-element.24), channel_id=1, replica_groups=mesh['seq'=16,'head'=8] {'seq'}, dimensions={0} | all-to-all | bytes 13762560 | tf_op jit(solution)/shard_map/all_to_all | solution.py:579
  323.8 7.3 %combine.1 = (bf16[8,4,128,384]{3,2,1,0:T(8,128)(2,1)}, bf16[48,384]{1,0:T(8,128)(2,1)}) custom-call(s32[32]{0:T(128)} %reshape.136.sel_ref, bf16[16,560,384]{2,1,0:T(8,128)(2,1)} %all_to_all.20.back_ref, f32[8,2,128,384]{3,2,1,0:T(8,128)} %get-tuple-element.25.own_ref, bf16[8,2,128,384]{3,2,1,0:T(8,128)(2,1)} %get-tuple-element.26.half_ref), custom_call_target="tpu_custom_call" | custom-call | flops 25165824 | bytes 16777216 | tf_op jit(solution)/shard_map/combine/pallas_call | solution.py:486
  331.1 5.8 %all-to-all-start.3 = ((bf16[8,4,128,384]{3,2,1,0:T(8,128)(2,1)}), bf16[8,4,128,384]{3,2,1,0:T(8,128)(2,1)S(1)}, u32[]{:S(2)}, u32[]{:S(2)}) async-start(bf16[8,4,128,384]{3,2,1,0:T(8,128)(2,1)} %get-tuple-element.27), calls=%async_computation.3 | async-start | bytes 6291456 | tf_op jit(solution)/shard_map/all_to_all | solution.py:591
  337.0 1.2 collective-permute-done.4
  338.2 0.6 collective-permute-start.5
  338.8 3.8 collective-permute-done.5
  342.7 1.6 collective-permute-start.6
  344.2 5.0 %collective-permute-done.6 = bf16[4,3,16,384]{3,2,1,0:T(8,128)(2,1)} collective-permute-done((bf16[4,3,16,384]{3,2,1,0:T(8,128)(2,1)S(1)}, bf16[4,3,16,384]{3,2,1,0:T(8,128)(2,1)}, u32[]{:S(2)}, u32[]{:S(2)}) %collective-permute-start.6) | collective-permute-done | bytes 147488 | tf_op jit(solution)/shard_map/ppermute | solution.py:514
  349.2 1.2 maximum_select_fusion.1
  350.4 1.5 collective-permute-start.7
  351.9 27.2 %collective-permute-done.7 = bf16[8,3,16,384]{3,2,1,0:T(8,128)(2,1)} collective-permute-done((bf16[8,3,16,384]{3,2,1,0:T(8,128)(2,1)S(1)}, bf16[8,3,16,384]{3,2,1,0:T(8,128)(2,1)}, u32[]{:S(2)}, u32[]{:S(2)}) %collective-permute-start.7) | collective-permute-done | bytes 294944 | tf_op jit(solution)/shard_map/ppermute | solution.py:514
  379.1 1.2 fusion
  380.3 0.8 fusion.5
  381.1 1.6 copy-done.1
  382.7 6.1 %unpack.1 = (bf16[128,3072]{1,0:T(8,128)(2,1)}, bf16[128,3072]{1,0:T(8,128)(2,1)}, bf16[128,3072]{1,0:T(8,128)(2,1)}, bf16[128,3072]{1,0:T(8,128)(2,1)}) custom-call(bf16[8,4,128,384]{3,2,1,0:T(8,128)(2,1)} %copy-done.1), custom_call_target="tpu_custom_call" | custom-call | bytes 6291456 | tf_op jit(solution)/shard_map/unpack/pallas_call | solution.py:87
  (39 shorter events, 0.7 us)
Async XLA Ops:
  7.0 7.6 %copy-start.8 = (s32[128,8]{0,1:T(8,128)S(1)}, s32[128,8]{0,1:T(8,128)}, u32[]{:S(2)}) copy-start(s32[128,8]{0,1:T(8,128)} %param.19) | copy-start | bytes 12292
  7.0 7.6 %copy-start.9 = (s32[128]{0:T(128)S(1)}, s32[128]{0:T(128)}, u32[]{:S(2)}) copy-start(s32[128]{0:T(128)} %param.20) | copy-start | bytes 1540
  7.0 44.3 %all-to-all-start = ((bf16[8,4,128,384]{3,2,1,0:T(8,128)(2,1)}), bf16[8,4,128,384]{3,2,1,0:T(8,128)(2,1)S(1)}, u32[]{:S(2)}, u32[]{:S(2)}) async-start(bf16[8,4,128,384]{3,2,1,0:T(8,128)(2,1)} %pack.1), calls=%async_computation | async-start | bytes 6291456 | tf_op jit(solution)/shard_map/all_to_all | solution.py:558
  51.3 1.6 copy-start
  57.3 6.8 %copy-start.10 = (s32[256]{0:T(256)S(1)}, s32[256]{0:T(256)}, u32[]{:S(2)}) copy-start(s32[256]{0:T(256)} %param.21) | copy-start | bytes 3076
  57.3 140.2 %all-to-all-start.1 = ((bf16[16,512,384]{2,1,0:T(8,128)(2,1)}), bf16[16,512,384]{2,1,0:T(8,128)(2,1)}, u32[]{:S(2)}, u32[]{:S(2)}) async-start(bf16[16,512,384]{2,1,0:T(8,128)(2,1)} %bitcast.14), calls=%async_computation.1 | async-start | bytes 12582912 | tf_op jit(solution)/shard_map/all_to_all | solution.py:565
  70.5 2.1 collective-permute-start
  72.6 0.8 copy-start.4
  76.0 73.5 %collective-permute-start.1 = (f32[256,512]{1,0:T(8,128)}, f32[256,512]{1,0:T(8,128)S(1)}, u32[]{:S(2)}, u32[]{:S(2)}) collective-permute-start(f32[256,512]{1,0:T(8,128)} %text_merge.3.a_ref), channel_id=1, source_target_pairs={{0,16},{8,24},{16,0},{24,8},{32,48},{40,56},{48,32},{56,40},{64,80... | collective-permute-start | bytes 1572872 | tf_op jit(solution)/shard_map/ppermute | solution.py:514
  149.5 0.8 copy-start.5
  152.8 17.0 %collective-permute-start.2 = (f32[256,512]{1,0:T(8,128)}, f32[256,512]{1,0:T(8,128)S(1)}, u32[]{:S(2)}, u32[]{:S(2)}) collective-permute-start(f32[256,512]{1,0:T(8,128)} %text_merge.4.a_ref), channel_id=1, source_target_pairs={{0,48},{8,56},{16,32},{24,40},{32,16},{40,24},{48,0},{56,8},{64,11... | collective-permute-start | bytes 1572872 | tf_op jit(solution)/shard_map/ppermute | solution.py:514
  169.8 0.8 copy-start.3
  173.2 14.1 %collective-permute-start.3 = (f32[256,512]{1,0:T(8,128)}, f32[256,512]{1,0:T(8,128)S(1)}, u32[]{:S(2)}, u32[]{:S(2)}) collective-permute-start(f32[256,512]{1,0:T(8,128)} %text_merge.5.a_ref), channel_id=1, source_target_pairs={{0,64},{8,72},{16,80},{24,88},{32,96},{40,104},{48,112},{56,120},{... | collective-permute-start | bytes 1572872 | tf_op jit(solution)/shard_map/ppermute | solution.py:514
  187.2 0.8 copy-start.6
  331.1 5.8 %copy-start.7 = (bf16[48,384]{1,0:T(8,128)(2,1)S(1)}, bf16[48,384]{1,0:T(8,128)(2,1)}, u32[]{:S(2)}) copy-start(bf16[48,384]{1,0:T(8,128)(2,1)} %get-tuple-element.33) | copy-start | bytes 110596
  331.1 50.0 %all-to-all-start.3 = ((bf16[8,4,128,384]{3,2,1,0:T(8,128)(2,1)}), bf16[8,4,128,384]{3,2,1,0:T(8,128)(2,1)S(1)}, u32[]{:S(2)}, u32[]{:S(2)}) async-start(bf16[8,4,128,384]{3,2,1,0:T(8,128)(2,1)} %get-tuple-element.27), calls=%async_computation.3 | async-start | bytes 6291456 | tf_op jit(solution)/shard_map/all_to_all | solution.py:591
  337.0 1.2 collective-permute-start.4
  338.2 4.4 %collective-permute-start.5 = (bf16[2,3,16,384]{3,2,1,0:T(8,128)(2,1)S(1)}, bf16[2,3,16,384]{3,2,1,0:T(8,128)(2,1)S(1)}, u32[]{:S(2)}, u32[]{:S(2)}) collective-permute-start(bf16[2,3,16,384]{3,2,1,0:T(8,128)(2,1)S(1)} %maximum_select_fusion.3), channel_id=1, source_target_pairs={{0,16},{8,24},{16,0},{24,8},{32,48},{40,56},{48,32},{56,40},{64,80... | collective-permute-start | bytes 221192 | tf_op jit(solution)/shard_map/ppermute | solution.py:514
  342.7 1.6 copy-start.2
  342.7 6.5 %collective-permute-start.6 = (bf16[4,3,16,384]{3,2,1,0:T(8,128)(2,1)S(1)}, bf16[4,3,16,384]{3,2,1,0:T(8,128)(2,1)}, u32[]{:S(2)}, u32[]{:S(2)}) collective-permute-start(bf16[4,3,16,384]{3,2,1,0:T(8,128)(2,1)S(1)} %maximum_select_fusion.2), channel_id=1, source_target_pairs={{0,48},{8,56},{16,32},{24,40},{32,16},{40,24},{48,0},{56,8},{64,11... | collective-permute-start | bytes 442376 | tf_op jit(solution)/shard_map/ppermute | solution.py:514
  350.4 28.7 %collective-permute-start.7 = (bf16[8,3,16,384]{3,2,1,0:T(8,128)(2,1)S(1)}, bf16[8,3,16,384]{3,2,1,0:T(8,128)(2,1)}, u32[]{:S(2)}, u32[]{:S(2)}) collective-permute-start(bf16[8,3,16,384]{3,2,1,0:T(8,128)(2,1)S(1)} %maximum_select_fusion.1), channel_id=1, source_target_pairs={{0,64},{8,72},{16,80},{24,88},{32,96},{40,104},{48,112},{56,120},{... | collective-permute-start | bytes 884744 | tf_op jit(solution)/shard_map/ppermute | solution.py:514
  381.1 1.6 copy-start.1

commit v2 on v1

v2 whole, which is shorter than its diff:
```python
import functools

import jax
import jax.numpy as jnp
from jax import lax
from jax.experimental import pallas as pl
from jax.experimental.pallas import tpu as pltpu
from jax.sharding import PartitionSpec as P

HD = 128
TXT = 256
TILE = 128
KT = 8
MOST = 2
GROUPS = 16
HEADS = 8
TILES = 8
NH = 3
W = NH * HD
SLOTS = GROUPS * MOST
POOL = TILES + SLOTS
TROWS = TXT // GROUPS
TLOCAL = TILES * TILE
TCHUNKS = TLOCAL // 256 + 1
PAIR_ROWS = MOST * 2 * TILE
SEND_FIRST = PAIR_ROWS + 2 * TROWS
SEND_REST = PAIR_ROWS + TROWS
BACK_REST = PAIR_ROWS + 3 * NH * TROWS
NF = 2
WF = NF * HD
WR = W - WF

NEGATIVE = -1e30
FACTOR = HD**-0.5
LOG2E = 1.4426950408889634
FACTOR2 = FACTOR * LOG2E
VMEM_LIMIT = 67043328

F32 = jnp.float32
BF16 = jnp.bfloat16
SMEM = pltpu.SMEM
ANY = pl.ANY


def dot_nt(a, b):
    return lax.dot_general(a, b, (((1,), (1,)), ((), ())), preferred_element_type=F32)


def dot_nn(a, b):
    return lax.dot_general(a, b, (((1,), (0,)), ((), ())), preferred_element_type=F32)


def dot_tn(a, b):
    return lax.dot_general(a, b, (((0,), (0,)), ((), ())), preferred_element_type=F32)


def params(**kw):
    return pltpu.CompilerParams(vmem_limit_bytes=VMEM_LIMIT, **kw)


def cost(flops, nbytes, exps=0):
    return pl.CostEstimate(
        flops=int(flops), bytes_accessed=int(nbytes), transcendentals=int(exps)
    )


def go(copies):
    for copy in copies:
        copy.start()
    return copies


def finish(copies):
    for copy in copies:
        copy.wait()


def columns(h):
    return pl.ds(h * W, W)


def pack_kernel(k_ref, v_ref, q_ref, g_ref, o_ref, rows, in_sems, out_sems):
    refs = (k_ref, v_ref, q_ref, g_ref)
    loads = go([pltpu.make_async_copy(refs[n], rows.at[n], in_sems.at[n]) for n in range(4)])
    stores = []
    for n in range(4):
        loads[n].wait()
        stores += go(
            [
                pltpu.make_async_copy(
                    rows.at[n, :, columns(h)], o_ref.at[h, n], out_sems.at[n, h]
                )
                for h in range(HEADS)
            ]
        )
    finish(stores)


def any_specs(n):
    return [pl.BlockSpec(memory_space=ANY)] * n


def pack(k, v, q, g):
    return pl.pallas_call(
        pack_kernel,
        in_specs=any_specs(4),
        out_specs=pl.BlockSpec(memory_space=ANY),
        out_shape=jax.ShapeDtypeStruct((HEADS, 4, TILE, W), BF16),
        scratch_shapes=[
            pltpu.VMEM((4, TILE, HEADS * W), BF16),
            pltpu.SemaphoreType.DMA((4,)),
            pltpu.SemaphoreType.DMA((4, HEADS)),
        ],
        compiler_params=params(),
        cost_estimate=cost(0, 8 * TILE * HEADS * W * 2),
        name="pack",
    )(k, v, q, g)


def unpack_kernel(x_ref, a_ref, b_ref, c_ref, d_ref, rows, in_sems, out_sems):
    refs = (a_ref, b_ref, c_ref, d_ref)
    loads = [
        go(
            [
                pltpu.make_async_copy(
                    x_ref.at[h, n], rows.at[n, :, columns(h)], in_sems.at[n, h]
                )
                for h in range(HEADS)
            ]
        )
        for n in range(4)
    ]
    stores = []
    for n in range(4):
        finish(loads[n])
        stores += go([pltpu.make_async_copy(rows.at[n], refs[n], out_sems.at[n])])
    finish(stores)


def unpack(x):
    return pl.pallas_call(
        unpack_kernel,
        in_specs=any_specs(1),
        out_specs=any_specs(4),
        out_shape=[jax.ShapeDtypeStruct((TILE, HEADS * W), BF16)] * 4,
        scratch_shapes=[
            pltpu.VMEM((4, TILE, HEADS * W), BF16),
            pltpu.SemaphoreType.DMA((4, HEADS)),
            pltpu.SemaphoreType.DMA((4,)),
        ],
        compiler_params=params(),
        cost_estimate=cost(0, 8 * TILE * HEADS * W * 2),
        name="unpack",
    )(x)


def picked(sel_ref, x_ref, o_ref, sems, lanes):
    return [
        pltpu.make_async_copy(
            x_ref.at[sel_ref[g * MOST + m], kv, :, lanes],
            o_ref.at[g, pl.ds((2 * m + kv) * TILE, TILE)],
            sems.at[g, 2 * m + kv],
        )
        for g in range(GROUPS)
        for m in range(MOST)
        for kv in range(2)
    ]


def pick_rest_kernel(sel_ref, x_ref, o_ref, sems):
    finish(go(picked(sel_ref, x_ref, o_ref, sems, pl.ds(WF, WR))))


def pick_rest(sel, x):
    return pl.pallas_call(
        pick_rest_kernel,
        grid=(1,),
        in_specs=[pl.BlockSpec(memory_space=SMEM), whole(LOCAL_KV)],
        out_specs=pl.BlockSpec(memory_space=ANY),
        out_shape=jax.ShapeDtypeStruct((GROUPS, SEND_REST, WR), BF16),
        scratch_shapes=[pltpu.SemaphoreType.DMA((GROUPS, 2 * MOST))],
        compiler_params=params(),
        cost_estimate=cost(0, (SLOTS + TILES) * 2 * TILE * WR * 2),
        name="pick_rest",
    )(sel, x)


def text_chunk(x_ref, text_ref, which, c, lanes):
    if c < TCHUNKS - 1:
        return x_ref[2 * c : 2 * c + 2, which, :, lanes].reshape(256, HD)
    return text_ref[:, lanes]


def head_lanes(j):
    return pl.ds(pl.multiple_of(j * HD, HD), HD)


def whole(shape):
    return pl.BlockSpec(shape, lambda i: (0,) * len(shape))


TEXT = (TXT, W)
LOCAL_KV = (TILES, 2, TILE, W)


def thirds(x):
    first = x.astype(BF16).astype(F32)
    second = (x - first).astype(BF16).astype(F32)
    return first, second, x - first - second


def put(lane, block, at, column):
    return jnp.where(lane == at, column, block)


def take(lane, block, low, high, j):
    hit = (lane >= low) & (lane < high) & (lane % 8 == j)
    return jnp.sum(jnp.where(hit, block, 0.0), axis=1, keepdims=True)


def send_first_kernel(
    sel_ref, n_ref, tq_ref, tk_ref, tv_ref, x_ref, o_ref, s_ref, part_ref, sems, part_sems
):
    tiles = go(picked(sel_ref, x_ref, o_ref, sems, pl.ds(0, WF)))
    live = lax.broadcasted_iota(jnp.int32, (TXT, TXT), 1) < n_ref[0]
    lane = lax.broadcasted_iota(jnp.int32, (TXT, HD), 1)
    stats = jnp.zeros((TXT, HD), F32)
    for j in range(NH):
        lanes = slice(j * HD, (j + 1) * HD)
        query = tq_ref[:, lanes]
        top = None
        for c in range(TCHUNKS):
            s = dot_nt(query, text_chunk(x_ref, tk_ref, 0, c, lanes)) * FACTOR2
            if c == TCHUNKS - 1:
                s = jnp.where(live, s, NEGATIVE)
            s_ref[c] = s
            top = s if top is None else jnp.maximum(top, s)
        top = jnp.max(top, axis=1, keepdims=True).astype(BF16).astype(F32)
        total, out = None, None
        for c in range(TCHUNKS):
            p = jnp.exp2(s_ref[c] - top)
            part = dot_nn(p.astype(BF16), text_chunk(x_ref, tv_ref, 1, c, lanes))
            total = p if total is None else total + p
            out = part if out is None else out + part
        total = jnp.sum(total, axis=1, keepdims=True)
        part_ref[j] = out.astype(BF16)
        stats = put(lane, stats, j, top)
        for n, third in enumerate(thirds(total)):
            stats = put(lane, stats, 8 * (n + 1) + j, third)
    part_ref[NH] = stats.astype(BF16)
    parts = go(
        [
            pltpu.make_async_copy(
                part_ref.at[n, pl.ds(g * TROWS, TROWS)],
                o_ref.at[g, pl.ds(PAIR_ROWS + n // 2 * TROWS, TROWS), pl.ds(n % 2 * HD, HD)],
                part_sems.at[g, n],
            )
            for g in range(GROUPS)
            for n in range(NH + 1)
        ]
    )
    finish(tiles + parts)


def send_first(sel, n, tq, tk, tv, x):
    return pl.pallas_call(
        send_first_kernel,
        grid=(1,),
        in_specs=[pl.BlockSpec(memory_space=SMEM)] * 2 + [whole(TEXT)] * 3 + [whole(LOCAL_KV)],
        out_specs=pl.BlockSpec(memory_space=ANY),
        out_shape=jax.ShapeDtypeStruct((GROUPS, SEND_FIRST, WF), BF16),
        scratch_shapes=[
            pltpu.VMEM((TCHUNKS, TXT, 256), F32),
            pltpu.VMEM((NH + 1, TXT, HD), BF16),
            pltpu.SemaphoreType.DMA((GROUPS, 2 * MOST)),
            pltpu.SemaphoreType.DMA((GROUPS, NH + 1)),
        ],
        compiler_params=params(),
        cost_estimate=cost(4 * NH * TXT * TCHUNKS * 256 * HD, 5 << 20, NH * TXT * 1280),
        name="send_first",
    )(sel, n, tq, tk, tv, x)


def text_stats_kernel(own_ref, got_ref, tg_ref, in_ref, o_ref, out_ref, parts, stats_ref, sem, sems):
    load = go([pltpu.make_async_copy(got_ref.at[:, pl.ds(PAIR_ROWS, 2 * TROWS)], parts, sem)])
    lane_all = lax.broadcasted_iota(jnp.int32, (TXT, HD), 1)
    lane = lax.broadcasted_iota(jnp.int32, (TROWS, HD), 1)
    mine = pl.ds(pl.multiple_of(own_ref[0] * TROWS, TROWS), TROWS)
    finish(load)
    received = parts[:, TROWS:, HD:].astype(F32).reshape(TXT, HD)
    stats = jnp.zeros((TROWS, HD), F32)
    for j in range(NH):
        lanes = slice(j * HD, (j + 1) * HD)
        tops = take(lane_all, received, 0, 8, j).reshape(GROUPS, TROWS, 1)
        totals = take(lane_all, received, 8, 32, j).reshape(GROUPS, TROWS, 1)
        top = jnp.max(tops, axis=0)
        scale = jnp.exp2(tops - top[None])
        total = jnp.sum(scale * totals, axis=0)
        part = parts[:, j // 2 * TROWS : (j // 2 + 1) * TROWS, j % 2 * HD : (j % 2 + 1) * HD]
        out = jnp.sum(scale * part.astype(F32), axis=0) / total
        out_ref[:, lanes] = out.astype(BF16)
        offset = jnp.sum(tg_ref[mine, lanes].astype(F32) * out, axis=1, keepdims=True)
        for n, third in enumerate(thirds(top + jnp.log2(total)) + thirds(offset)):
            stats = put(lane, stats, 8 * n + j, third)
    stats_ref[...] = stats.astype(BF16)
    finish(
        go(
            [
                pltpu.make_async_copy(
                    stats_ref, o_ref.at[g, pl.ds(PAIR_ROWS, TROWS)], sems.at[g]
                )
                for g in range(GROUPS)
            ]
        )
    )


def text_stats(own, got, tg, send):
    return pl.pallas_call(
        text_stats_kernel,
        grid=(1,),
        in_specs=[pl.BlockSpec(memory_space=SMEM)]
        + any_specs(1)
        + [whole(TEXT)]
        + any_specs(1),
        out_specs=[pl.BlockSpec(memory_space=ANY), whole((TROWS, W))],
        out_shape=[
            jax.ShapeDtypeStruct(send.shape, BF16),
            jax.ShapeDtypeStruct((TROWS, W), BF16),
        ],
        scratch_shapes=[
            pltpu.VMEM((GROUPS, 2 * TROWS, WF), BF16),
            pltpu.VMEM((TROWS, WR), BF16),
            pltpu.SemaphoreType.DMA,
            pltpu.SemaphoreType.DMA((GROUPS,)),
        ],
        input_output_aliases={3: 0},
        compiler_params=params(),
        cost_estimate=cost(TXT * W * 8, 1 << 19),
        name="text_stats",
    )(own, got, tg, send)


def text_backward_kernel(
    n_ref, got_ref, tq_ref, tk_ref, tv_ref, tg_ref, x_ref, tqg_ref, acc_ref, dx_ref, rows, sem
):
    load = go(
        [
            pltpu.make_async_copy(
                got_ref.at[:, pl.ds(PAIR_ROWS, TROWS), pl.ds(0, HD)], rows, sem
            )
        ]
    )
    live = lax.broadcasted_iota(jnp.int32, (TXT, TXT), 1) < n_ref[0]
    lane = lax.broadcasted_iota(jnp.int32, (TXT, HD), 1)
    finish(load)

    def head(j, carry):
        lanes = head_lanes(j)
        stats = rows[...].astype(F32).reshape(TXT, HD)
        log_total = take(lane, stats, 0, 24, j)
        offset = take(lane, stats, 24, 48, j)
        query, grad = tq_ref[:, lanes], tg_ref[:, lanes]
        query_grad = None
        for c in range(TCHUNKS):
            key = text_chunk(x_ref, tk_ref, 0, c, lanes)
            value = text_chunk(x_ref, tv_ref, 1, c, lanes)
            s = dot_nt(query, key) * FACTOR2
            if c == TCHUNKS - 1:
                s = jnp.where(live, s, NEGATIVE)
            p = jnp.exp2(s - log_total)
            ds = (p * (dot_nt(grad, value) - offset)).astype(BF16)
            p = p.astype(BF16)
            part = dot_nn(ds, key)
            query_grad = part if query_grad is None else query_grad + part
            key_grad = dot_tn(ds, query)
            value_grad = dot_tn(p, grad)
            if c < TCHUNKS - 1:
                dx_ref[2 * c : 2 * c + 2, 0, :, lanes] = key_grad.reshape(2, TILE, HD)
                dx_ref[2 * c : 2 * c + 2, 1, :, lanes] = value_grad.reshape(2, TILE, HD)
            else:
                acc_ref[0, :, lanes] = key_grad
                acc_ref[1, :, lanes] = value_grad
        tqg_ref[:, lanes] = query_grad * FACTOR
        return carry

    lax.fori_loop(0, NH, head, 0)


def text_backward(n, got, tq, tk, tv, tg, x):
    return pl.pallas_call(
        text_backward_kernel,
        grid=(1,),
        in_specs=[pl.BlockSpec(memory_space=SMEM)]
        + any_specs(1)
        + [whole(TEXT)] * 4
        + [whole(LOCAL_KV)],
        out_specs=[whole(TEXT), whole((2, TXT, W)), whole(LOCAL_KV)],
        out_shape=[
            jax.ShapeDtypeStruct(TEXT, F32),
            jax.ShapeDtypeStruct((2, TXT, W), F32),
            jax.ShapeDtypeStruct(LOCAL_KV, F32),
        ],
        scratch_shapes=[
            pltpu.VMEM((GROUPS, TROWS, HD), BF16),
            pltpu.SemaphoreType.DMA,
        ],
        compiler_params=params(),
        cost_estimate=cost(10 * NH * TXT * TCHUNKS * 256 * HD, 8 << 20, NH * TXT * 1280),
        name="text_backward",
    )(n, got, tq, tk, tv, tg, x)


CHUNKS = KT // 2 + 1


def video_kernel(first, slot_ref, count_ref, n_ref, kv_ref, qg_ref, got_ref, tk_ref, tv_ref, *refs):
    if first:
        out_ref, back_ref, own_ref, text_ref = refs[:4]
        refs = refs[4:]
    else:
        tqg_ref, tacc_ref, text0_ref, out_ref, back_ref, own_ref = refs[:6]
        refs = refs[6:]
    keys, values, s_ref, p_ref, dk_acc, dv_acc, tk_acc, tv_acc, pool = refs
    pool[:TILES] = kv_ref[...]
    pool[TILES:] = got_ref[...].reshape(SLOTS, 2, TILE, HD)
    keys[0] = tk_ref[...]
    values[0] = tv_ref[...]
    dk_acc[...] = jnp.zeros((POOL, TILE, HD), F32)
    dv_acc[...] = jnp.zeros((POOL, TILE, HD), F32)
    if first:
        tk_acc[...] = jnp.zeros((TXT, HD), F32)
        tv_acc[...] = jnp.zeros((TXT, HD), F32)
    else:
        tk_acc[...] = tacc_ref[0, :, WF:]
        tv_acc[...] = tacc_ref[1, :, WF:]
    text_live = lax.broadcasted_iota(jnp.int32, (TXT, TILE), 0) < n_ref[0]

    def tile(i, carry):
        count = count_ref[i]
        query, grad = qg_ref[i, 0], qg_ref[i, 1]

        def run(pairs):
            slots = [slot_ref[i * KT + e] for e in range(2 * pairs)]
            for e in range(2 * pairs):
                half = pl.ds((e % 2) * TILE, TILE)
                keys[1 + e // 2, half] = pool[slots[e], 0]
                values[1 + e // 2, half] = pool[slots[e], 1]
            top = None
            for c in range(pairs + 1):
                s = dot_nt(keys[c], query) * FACTOR2
                if c == 0:
                    s = jnp.where(text_live, s, NEGATIVE)
                elif c == pairs:
                    s = jnp.concatenate(
                        [s[:TILE], jnp.where(2 * pairs <= count, s[TILE:], NEGATIVE)], axis=0
                    )
                s_ref[c] = s
                part = jnp.max(s.reshape(32, 8, TILE), axis=0)
                top = part if top is None else jnp.maximum(top, part)
            top = jnp.max(top, axis=0, keepdims=True)
            total = None
            for c in range(pairs + 1):
                p = jnp.exp2(s_ref[c] - top)
                s_ref[c] = p
                part = jnp.sum(p.reshape(32, 8, TILE), axis=0)
                total = part if total is None else total + part
            scale = 1.0 / jnp.sum(total, axis=0, keepdims=True)
            out = None
            for c in range(pairs + 1):
                p = s_ref[c] * scale
                s_ref[c] = p
                p = p.astype(BF16)
                p_ref[c] = p
                part = dot_tn(p, values[c])
                out = part if out is None else out + part
            out_ref[i, 0] = out.astype(BF16)
            offset = jnp.sum((grad.astype(F32) * out).T, axis=0, keepdims=True)
            query_grad = None
            for c in range(pairs + 1):
                ds = (s_ref[c] * (dot_nt(values[c], grad) - offset)).astype(BF16)
                part = dot_tn(ds, keys[c])
                query_grad = part if query_grad is None else query_grad + part
                key_grad = dot_nn(ds, query)
                value_grad = dot_nn(p_ref[c], grad)
                if c == 0:
                    tk_acc[...] += key_grad
                    tv_acc[...] += value_grad
                else:
                    for e in (0, 1):
                        slot = slots[2 * (c - 1) + e]
                        dk_acc[slot] += key_grad[e * TILE : (e + 1) * TILE]
                        dv_acc[slot] += value_grad[e * TILE : (e + 1) * TILE]
            out_ref[i, 1] = (query_grad * FACTOR).astype(BF16)

        for pairs in range(1, KT // 2 + 1):

            @pl.when((count + 1) // 2 == pairs)
            def _():
                run(pairs)

        return carry

    lax.fori_loop(0, TILES, tile, 0)

    own_ref[:, 0] = dk_acc[:TILES]
    own_ref[:, 1] = dv_acc[:TILES]
    for g in range(GROUPS):
        for m in range(MOST):
            slot = TILES + g * MOST + m
            back_ref[g, 2 * m * TILE : (2 * m + 1) * TILE] = (dk_acc[slot] * FACTOR).astype(BF16)
            back_ref[g, (2 * m + 1) * TILE : (2 * m + 2) * TILE] = dv_acc[slot].astype(BF16)
    if first:
        text_ref[0] = tk_acc[...]
        text_ref[1] = tv_acc[...]
        return

    def store(n, values):
        at = PAIR_ROWS + n * TROWS
        back_ref[:, at : at + TROWS] = values.reshape(GROUPS, TROWS, HD).astype(BF16)

    for h in range(NH):
        lanes = slice(h * HD, (h + 1) * HD)
        if h < NF:
            key_grad = tacc_ref[0, :, lanes] + text0_ref[0, :, lanes]
            value_grad = tacc_ref[1, :, lanes] + text0_ref[1, :, lanes]
        else:
            key_grad, value_grad = tk_acc[...], tv_acc[...]
        store(h, tqg_ref[:, lanes])
        store(NH + h, key_grad * FACTOR)
        store(2 * NH + h, value_grad)


def video(first, slot, count, n, x, got, tk, tv, *text):
    base, heads = (0, NF) if first else (NF, NH - NF)
    rows = PAIR_ROWS if first else BACK_REST
    width = heads * HD
    smem = pl.BlockSpec(memory_space=SMEM)
    per_head = pl.BlockSpec((TXT, HD), lambda j: (0, base + j))
    pair = (TILES, 2, TILE, HD)
    in_specs = [
        smem,
        smem,
        smem,
        pl.BlockSpec(pair, lambda j: (0, 0, 0, base + j)),
        pl.BlockSpec(pair, lambda j: (0, 1, 0, base + j)),
        pl.BlockSpec((GROUPS, PAIR_ROWS, HD), lambda j: (0, 0, j)),
        per_head,
        per_head,
    ]
    out_specs = [
        pl.BlockSpec(pair, lambda j: (0, 0, 0, j)),
        pl.BlockSpec((GROUPS, rows, HD), lambda j: (0, 0, j)),
        pl.BlockSpec(pair, lambda j: (0, 0, 0, j)),
    ]
    out_shape = [
        jax.ShapeDtypeStruct((TILES, 2, TILE, width), BF16),
        jax.ShapeDtypeStruct((GROUPS, rows, width), BF16),
        jax.ShapeDtypeStruct((TILES, 2, TILE, width), F32),
    ]
    if first:
        out_specs.append(pl.BlockSpec((2, TXT, HD), lambda j: (0, 0, j)))
        out_shape.append(jax.ShapeDtypeStruct((2, TXT, WF), F32))
    else:
        in_specs += [whole(TEXT), whole((2, TXT, W)), whole((2, TXT, WF))]
    return pl.pallas_call(
        functools.partial(video_kernel, first),
        grid=(heads,),
        in_specs=in_specs,
        out_specs=out_specs,
        out_shape=out_shape,
        scratch_shapes=[
            pltpu.VMEM((CHUNKS, 256, HD), BF16),
            pltpu.VMEM((CHUNKS, 256, HD), BF16),
            pltpu.VMEM((CHUNKS, 256, TILE), F32),
            pltpu.VMEM((CHUNKS, 256, TILE), BF16),
            pltpu.VMEM((POOL, TILE, HD), F32),
            pltpu.VMEM((POOL, TILE, HD), F32),
            pltpu.VMEM((TXT, HD), F32),
            pltpu.VMEM((TXT, HD), F32),
            pltpu.VMEM((POOL, 2, TILE, HD), BF16),
        ],
        compiler_params=params(),
        cost_estimate=cost(
            12 * heads * TLOCAL * 1280 * HD, heads * (8 << 20), heads * TLOCAL * 1280
        ),
        name="video_first" if first else "video_rest",
    )(slot, count, n, x, x, got, tk, tv, *text)


def combine_kernel(sel_ref, back_ref, own_ref, dx_ref, half_ref, *refs):
    out_ref, acc = refs[-2:]
    acc[:, 0] = (own_ref[:, 0] + dx_ref[:, 0]) * FACTOR
    acc[:, 1] = own_ref[:, 1] + dx_ref[:, 1]

    def add(g, carry):
        for m in range(MOST):
            at = sel_ref[g * MOST + m]
            part = back_ref[g, 2 * m * TILE : 2 * (m + 1) * TILE].astype(F32)
            acc[at] += part.reshape(2, TILE, HD)
        return carry

    lax.fori_loop(0, GROUPS, add, 0)
    out_ref[:, :2] = half_ref[...]
    out_ref[:, 2:] = acc[...].astype(BF16)


def combine(first, sel, back, own, dx, half, *packed):
    base, heads = (0, NF) if first else (NF, NH - NF)
    pair = (TILES, 2, TILE, HD)
    return pl.pallas_call(
        combine_kernel,
        grid=(heads,),
        in_specs=[
            pl.BlockSpec(memory_space=SMEM),
            pl.BlockSpec((GROUPS, PAIR_ROWS, HD), lambda j: (0, 0, j)),
            pl.BlockSpec(pair, lambda j: (0, 0, 0, j)),
            pl.BlockSpec(pair, lambda j: (0, 0, 0, base + j)),
            pl.BlockSpec(pair, lambda j: (0, 0, 0, j)),
        ]
        + any_specs(len(packed)),
        out_specs=pl.BlockSpec((TILES, 4, TILE, HD), lambda j: (0, 0, 0, base + j)),
        out_shape=jax.ShapeDtypeStruct((TILES, 4, TILE, W), BF16),
        scratch_shapes=[pltpu.VMEM(pair, F32)],
        input_output_aliases={5: 0} if packed else {},
        compiler_params=params(),
        cost_estimate=cost(heads * TLOCAL * HD * 64, heads * (5 << 20)),
        name="combine_first" if first else "combine_rest",
    )(sel, back, own, dx, half, *packed)


def text_sum_kernel(back_ref, out_ref, o_ref, rows, sem):
    load = [pltpu.make_async_copy(back_ref.at[:, pl.ds(PAIR_ROWS, 3 * NH * TROWS)], rows, sem)]
    finish(go(load))
    total = jnp.sum(rows[...].astype(F32), axis=0).astype(BF16)
    o_ref[0] = out_ref[...]
    for n in range(3 * NH):
        h = n % NH
        o_ref[n // NH + 1, :, h * HD : (h + 1) * HD] = total[n * TROWS : (n + 1) * TROWS]


def text_sum(back, out):
    return pl.pallas_call(
        text_sum_kernel,
        grid=(1,),
        in_specs=any_specs(1) + [whole((TROWS, W))],
        out_specs=whole((4, TROWS, W)),
        out_shape=jax.ShapeDtypeStruct((4, TROWS, W), BF16),
        scratch_shapes=[
            pltpu.VMEM((GROUPS, 3 * NH * TROWS, WR), BF16),
            pltpu.SemaphoreType.DMA,
        ],
        compiler_params=params(),
        cost_estimate=cost(GROUPS * 9 * TROWS * WR, 1 << 20),
        name="text_sum",
    )(back, out)


STEPS = ((1, 1), (2, 2), (4, 6), (8, 8))


def swapped(x, mask):
    return lax.ppermute(x, "seq", [(i, i ^ mask) for i in range(GROUPS)])


def tables(tile_list, tile_count, own):
    live = jnp.arange(KT)[None, :] < tile_count[:, None]
    listed = jnp.where(live, tile_list, -1)

    def ranked(wanted):
        before = jnp.arange(TILES)[:, None] < jnp.arange(TILES)[None, :]
        return jnp.sum(jnp.where(before[None], wanted[:, :, None], 0), axis=1)

    mine = own * TILES + jnp.arange(TILES)
    asked = jnp.any(
        listed.reshape(GROUPS, TILES * KT, 1) == mine[None, None, :], axis=1
    ).astype(jnp.int32)
    rank = ranked(asked)
    chosen = (asked[:, None, :] > 0) & (rank[:, None, :] == jnp.arange(MOST)[None, :, None])
    sel = jnp.sum(jnp.where(chosen, jnp.arange(TILES)[None, None, :], 0), axis=2).reshape(SLOTS)

    my_list = lax.dynamic_slice_in_dim(listed, own * TILES, TILES, 0).reshape(TILES * KT)
    hits = my_list[:, None] == jnp.arange(GROUPS * TILES)[None, :]
    needed = jnp.any(hits, axis=0).astype(jnp.int32).reshape(GROUPS, TILES)
    where_to = TILES + jnp.arange(GROUPS)[:, None] * MOST + jnp.minimum(ranked(needed), MOST - 1)
    local = jnp.arange(GROUPS)[:, None] == own
    where_to = jnp.where(local, jnp.arange(TILES)[None, :], where_to).reshape(GROUPS * TILES)
    slot = jnp.sum(jnp.where(hits, where_to[None, :], 0), axis=1)
    count = lax.dynamic_slice_in_dim(tile_count, own * TILES, TILES, 0)
    return sel.astype(jnp.int32), slot.astype(jnp.int32), count.astype(jnp.int32)


def body(
    video_query,
    video_key,
    video_value,
    video_grad,
    text_query,
    text_key,
    text_value,
    text_grad,
    tile_list,
    tile_count,
    text_mask,
):
    own = lax.axis_index("seq")
    x = lax.all_to_all(
        pack(video_key, video_value, video_query, video_grad), "head", 0, 0, tiled=True
    )
    sel, slot, count = tables(tile_list, tile_count, own)
    n = jnp.sum((text_mask > 0).astype(jnp.int32)).reshape(1)
    n_own = jnp.where(own == 0, n, 0)
    text = (text_query, text_key, text_value)

    send = send_first(sel, n_own, *text, x)
    got0 = lax.all_to_all(send, "seq", 0, 0, tiled=True)
    send, text_out = text_stats(own.reshape(1), got0, text_grad, pick_rest(sel, x))
    got = lax.all_to_all(send, "seq", 0, 0, tiled=True)
    half0, back0, own0, text0 = video(
        True, slot, count, n, x, got0, text_key, text_value
    )
    back0 = lax.all_to_all(back0, "seq", 0, 0, tiled=True)
    tqg, tacc, dx = text_backward(n_own, got, *text, text_grad, x)
    half, back, own_grads = video(
        False, slot, count, n, x, got, text_key, text_value, tqg, tacc, text0
    )
    back = lax.all_to_all(back, "seq", 0, 0, tiled=True)
    packed = combine(True, sel, back0, own0, dx, half0)
    packed = combine(False, sel, back, own_grads, dx, half, packed)

    gathered = text_sum(back, text_out)[None]
    for bit, mask in STEPS:
        theirs = swapped(gathered, mask)
        first = jnp.concatenate([gathered, theirs], axis=0)
        second = jnp.concatenate([theirs, gathered], axis=0)
        gathered = jnp.where((own & bit) == 0, first, second)
    text_rows = jnp.transpose(gathered, (1, 0, 2, 3)).reshape(4, TXT, W)

    attended_video, video_query_grad, video_key_grad, video_value_grad = unpack(
        lax.all_to_all(packed, "head", 0, 0, tiled=True)
    )
    return (
        attended_video,
        video_query_grad,
        video_key_grad,
        video_value_grad,
        text_rows[0],
        text_rows[1],
        text_rows[2],
        text_rows[3],
    )


def solution(mesh):
    tokens, heads = P(("seq", "head"), None), P(None, "head")
    return jax.shard_map(
        body,
        mesh=mesh,
        in_specs=(tokens,) * 4 + (heads,) * 4 + (P(),) * 3,
        out_specs=(tokens,) * 4 + (heads,) * 4,
        check_vma=False,
    )
```

time: 391 us -> 339 us (0.87)
  blocking collectives: 82.4 us -> 0 us
  starting transfers between devices: 25.5 us -> 62.9 us
  local copies, waits for them, and re-layouts: 9.37 us -> 3.52 us
  waiting for transfers between devices: 176 us -> 172 us
    ppermute x8 -> x4, waiting for transfers between devices: 141 us -> 30.5 us  [swapped(): return lax.ppermute(x, 'seq', [(i, i ^ mask) for i in range(GROUPS)])]
    all_to_all x1 -> x4, waiting for transfers between devices: 0.01 us -> 109 us  [the longest x1 54.9 us: body(): got0 = lax.all_to_all(send, 'seq', 0, 0, tiled=True)]
    all_to_all x1 -> x0, blocking collectives: 82.4 us -> none  [body(): back = lax.all_to_all(back, 'seq', 0, 0, tiled=True)]
    all_to_all x1 -> x4, starting transfers between devices: 6.8 us -> 39.8 us  [the longest x1 13.3 us: body(): got = lax.all_to_all(send, 'seq', 0, 0, tiled=True)]
    unnamed x22 -> x14, local copies, waits for them, and re-layouts: 6.45 us -> 0.46 us
    ppermute x8 -> x4, starting transfers between devices: 5.28 us -> 9.8 us  [swapped(): return lax.ppermute(x, 'seq', [(i, i ^ mask) for i in range(GROUPS)])]
    pallas_call x9 -> x10, Pallas kernels: 80.8 us -> 80.3 us  [the longest x2 49.2 us: video(): pl.pallas_call(functools.partial(video_kernel, first), grid=(heads,), in_...]
  transfers between devices with their start and end apart: 11 -> 10, of which waited for: 9 -> 8; matrix products, arithmetic and copies ran while one was open for 2% -> 2% of each run, Pallas kernels for 6% -> 21%
where the time goes in v2:
time: 339 us; the launch traced here: 334 us
  waiting for transfers between devices  172 us (51%)
  Pallas kernels  90.5 us (27%)
  starting transfers between devices  62.9 us (19%)
  other arithmetic  3.71 us (1%)
  local copies, waits for them, and re-layouts  3.52 us (1%)
    all_to_all x1, waiting for transfers between devices, body(): got0 = lax.all_to_all(send, 'seq', 0, 0, tiled=True)  54.9 us
    pallas_call x2, Pallas kernels, video(): pl.pallas_call(functools.partial(video_kernel, first), grid=(heads,), in_...  49.2 us
    all_to_all x1, waiting for transfers between devices, body(): lax.all_to_all(pack(video_key, video_value, video_query, video_grad), 'he...  32.6 us
    ppermute x4, waiting for transfers between devices, swapped(): return lax.ppermute(x, 'seq', [(i, i ^ mask) for i in range(GROUPS)])  30.5 us
    all_to_all x1, waiting for transfers between devices, body(): back = lax.all_to_all(back, 'seq', 0, 0, tiled=True)  28 us
    all_to_all x1, waiting for transfers between devices, body(): back0 = lax.all_to_all(back0, 'seq', 0, 0, tiled=True)  25.9 us
    all_to_all x1, starting transfers between devices, body(): got = lax.all_to_all(send, 'seq', 0, 0, tiled=True)  13.3 us
    all_to_all x1, starting transfers between devices, body(): back = lax.all_to_all(back, 'seq', 0, 0, tiled=True)  13.1 us
  transfers between devices with their start and end apart: 10, of which 8 were waited for; matrix products, arithmetic and copies ran while one was open for 2% of the time, Pallas kernels for 21%

profile of v2, /device:TPU:6, one launch (start us, length us, event | category | flops | bytes accessed | tf_op | source)
XLA Modules:
  0.0 334.1 jit_solution(5872655879300840015)
XLA Ops:
  0.6 3.2 pack.1
  3.9 7.6 %all-to-all-start = ((bf16[8,4,128,384]{3,2,1,0:T(8,128)(2,1)}), bf16[8,4,128,384]{3,2,1,0:T(8,128)(2,1)}, u32[]{:S(2)}, u32[]{:S(2)}) async-start(bf16[8,4,128,384]{3,2,1,0:T(8,128)(2,1)} %pack.1), calls=%async_computation | async-start | bytes 6291456 | tf_op jit(solution)/shard_map/all_to_all | solution.py:707
  11.5 0.1 copy.31
  11.6 0.1 copy.34
  11.7 0.1 eq.76
  11.8 0.1 fusion.1
  11.9 0.4 copy-done.4
  12.3 0.1 reshape.115
  12.5 0.1 eq.69
  12.6 0.4 compare_reduce_fusion
  13.0 0.1 copy.32
  13.1 0.7 select_reduce_fusion.1
  13.8 0.1 copy.33
  13.9 0.6 reshape.112.sel_ref
  14.5 0.6 fusion.4
  15.7 32.6 %all-to-all-done.x_ref.kv_ref.qg_ref = bf16[8,4,128,384]{3,2,1,0:T(8,128)(2,1)} async-done(((bf16[8,4,128,384]{3,2,1,0:T(8,128)(2,1)}), bf16[8,4,128,384]{3,2,1,0:T(8,128)(2,1)}, u32[]{:S(2)}, u32[]{:S(2)}) %all-to-all-start) | async-done | bytes 3145760 | tf_op jit(solution)/shard_map/all_to_all | solution.py:707
  48.3 5.8 %send_first.1 = bf16[16,544,256]{2,1,0:T(8,128)(2,1)} custom-call(s32[32]{0:T(128)} %reshape.112.sel_ref, s32[1]{0:T(128)S(6)} %select_n.83.n_ref, bf16[256,384]{1,0:T(8,128)(2,1)} %tq_ref.3, bf16[256,384]{1,0:T(8,128)(2,1)} %tk_ref.7, bf16[256,384]{1,0:T(8,128)(2,1)} %tv_ref.7, bf16[8,4,128,384]{3,2,1,0:T(8,128)(2,1)} %all-to-all-done.x_ref.kv_ref.qg_ref), custom_call_target="tpu_custom_call" | custom-call | flops 503316480 | bytes 5242880 | tf_op jit(solution)/shard_map/send_first/pallas_call | solution.py:266
  54.0 6.8 %all-to-all-start.1 = ((bf16[16,544,256]{2,1,0:T(8,128)(2,1)}), bf16[16,544,256]{2,1,0:T(8,128)(2,1)}, u32[]{:S(2)}, u32[]{:S(2)}) async-start(bf16[16,544,256]{2,1,0:T(8,128)(2,1)} %send_first.1), calls=%async_computation.1 | async-start | bytes 8912896 | tf_op jit(solution)/shard_map/all_to_all | solution.py:716
  60.8 3.4 %pick_rest.1.in_ref = bf16[16,528,128]{2,1,0:T(8,128)(2,1)} custom-call(s32[32]{0:T(128)} %reshape.112.sel_ref, bf16[8,4,128,384]{3,2,1,0:T(8,128)(2,1)} %all-to-all-done.x_ref.kv_ref.qg_ref), custom_call_target="tpu_custom_call" | custom-call | bytes 2621440 | tf_op jit(solution)/shard_map/pick_rest/pallas_call | solution.py:175
  64.2 54.9 %all-to-all-done.1.got_ref = bf16[16,544,256]{2,1,0:T(8,128)(2,1)} async-done(((bf16[16,544,256]{2,1,0:T(8,128)(2,1)}), bf16[16,544,256]{2,1,0:T(8,128)(2,1)}, u32[]{:S(2)}, u32[]{:S(2)}) %all-to-all-start.1) | async-done | bytes 4456480 | tf_op jit(solution)/shard_map/all_to_all | solution.py:716
  119.1 3.7 %text_stats.1 = (bf16[16,528,128]{2,1,0:T(8,128)(2,1)}, bf16[16,384]{1,0:T(8,128)(2,1)}) custom-call(s32[1]{0:T(128)} %bitcast.1.own_ref, bf16[16,544,256]{2,1,0:T(8,128)(2,1)} %all-to-all-done.1.got_ref, bf16[256,384]{1,0:T(8,128)(2,1)} %tg_ref.3, bf16[16,528,128]{2,1,0:T(8,128)(2,1)} %pick_rest.1.in_ref), custom_call_target="tpu_custom_call", output_to_operand_aliasing={{0}: (3, {})} | custom-call | flops 786432 | bytes 524288 | tf_op jit(solution)/shard_map/text_stats/pallas_call | solution.py:319
  122.8 13.3 %all-to-all-start.2 = ((bf16[16,528,128]{2,1,0:T(8,128)(2,1)}), bf16[16,528,128]{2,1,0:T(8,128)(2,1)}, u32[]{:S(2)}, u32[]{:S(2)}) async-start(bf16[16,528,128]{2,1,0:T(8,128)(2,1)} %get-tuple-element.24), calls=%async_computation.2 | async-start | bytes 4325376 | tf_op jit(solution)/shard_map/all_to_all | solution.py:718
  136.1 0.7 dynamic_slice.7.count_ref
  136.9 0.1 select_n.80
  137.0 0.7 select_reduce_fusion.slot_ref
  137.7 31.0 %video_first.1 = (bf16[8,2,128,256]{3,2,1,0:T(8,128)(2,1)}, bf16[16,512,256]{2,1,0:T(8,128)(2,1)}, f32[8,2,128,256]{3,2,1,0:T(8,128)}, f32[2,256,256]{2,1,0:T(8,128)}) custom-call(s32[64]{0:T(128)} %select_reduce_fusion.slot_ref, s32[8]{0:T(128)} %dynamic_slice.7.count_ref, s32[1]{0:T(128)} %bitcast.n_ref, ...), custom_call_target="tpu_custom_call" | custom-call | flops 4026531840 | bytes 16777216 | tf_op jit(solution)/shard_map/video_first/pallas_call | solution.py:566
  168.7 6.6 %all-to-all-start.4 = ((bf16[16,512,256]{2,1,0:T(8,128)(2,1)}), bf16[16,512,256]{2,1,0:T(8,128)(2,1)}, u32[]{:S(2)}, u32[]{:S(2)}) async-start(bf16[16,512,256]{2,1,0:T(8,128)(2,1)} %get-tuple-element.32), calls=%async_computation.4 | async-start | bytes 8388608 | tf_op jit(solution)/shard_map/all_to_all | solution.py:722
  175.4 10.2 %text_backward.1 = (f32[256,384]{1,0:T(8,128)}, f32[2,256,384]{2,1,0:T(8,128)}, f32[8,2,128,384]{3,2,1,0:T(8,128)}) custom-call(s32[1]{0:T(128)S(6)} %select_n.83.n_ref, bf16[16,528,128]{2,1,0:T(8,128)(2,1)} %all-to-all-done.2.got_ref, bf16[256,384]{1,0:T(8,128)(2,1)} %tq_ref.3, bf16[256,384]{1,0:T(8,128)(2,1)} %tk_ref.7, bf16[256,384]{1,0:T(8,128)(2,1)} %tv_ref.7, ...), custom_call_target="tpu_custom_call" | custom-call | flops 1258291200 | bytes 8388608 | tf_op jit(solution)/shard_map/text_backward/pallas_call | solution.py:391
  185.5 18.2 %video_rest.1 = (bf16[8,2,128,128]{3,2,1,0:T(8,128)(2,1)}, bf16[16,656,128]{2,1,0:T(8,128)(2,1)}, f32[8,2,128,128]{3,2,1,0:T(8,128)}) custom-call(s32[64]{0:T(128)} %select_reduce_fusion.slot_ref, s32[8]{0:T(128)} %dynamic_slice.7.count_ref, s32[1]{0:T(128)} %bitcast.n_ref, bf16[8,4,128,384]{3,2,1,0:T(8,128)(2,1)} %all-to-all-done.x_ref.kv_ref.qg_ref, ...), custom_call_target="tpu_custom_call" | custom-call | flops 2013265920 | bytes 8388608 | tf_op jit(solution)/shard_map/video_rest/pallas_call | solution.py:566
  203.7 25.9 %all-to-all-done.4.back_ref = bf16[16,512,256]{2,1,0:T(8,128)(2,1)} async-done(((bf16[16,512,256]{2,1,0:T(8,128)(2,1)}), bf16[16,512,256]{2,1,0:T(8,128)(2,1)}, u32[]{:S(2)}, u32[]{:S(2)}) %all-to-all-start.4) | async-done | bytes 4194336 | tf_op jit(solution)/shard_map/all_to_all | solution.py:722
  229.6 13.1 %all-to-all-start.3 = ((bf16[16,656,128]{2,1,0:T(8,128)(2,1)}), bf16[16,656,128]{2,1,0:T(8,128)(2,1)}, u32[]{:S(2)}, u32[]{:S(2)}) async-start(bf16[16,656,128]{2,1,0:T(8,128)(2,1)} %get-tuple-element.28), calls=%async_computation.3 | async-start | bytes 5373952 | tf_op jit(solution)/shard_map/all_to_all | solution.py:727
  242.6 5.5 %combine_first.1.refs_0_ = bf16[8,4,128,384]{3,2,1,0:T(8,128)(2,1)} custom-call(s32[32]{0:T(128)} %reshape.112.sel_ref, bf16[16,512,256]{2,1,0:T(8,128)(2,1)} %all-to-all-done.4.back_ref, f32[8,2,128,256]{3,2,1,0:T(8,128)} %get-tuple-element.33.own_ref, f32[8,2,128,384]{3,2,1,0:T(8,128)} %get-tuple-element.30.dx_ref, ...), custom_call_target="tpu_custom_call" | custom-call | flops 16777216 | bytes 10485760 | tf_op jit(solution)/shard_map/combine_first/pallas_call | solution.py:611
  248.1 28.0 %all-to-all-done.3.back_ref = bf16[16,656,128]{2,1,0:T(8,128)(2,1)} async-done(((bf16[16,656,128]{2,1,0:T(8,128)(2,1)}), bf16[16,656,128]{2,1,0:T(8,128)(2,1)}, u32[]{:S(2)}, u32[]{:S(2)}) %all-to-all-start.3) | async-done | bytes 2687008 | tf_op jit(solution)/shard_map/all_to_all | solution.py:727
  276.1 4.1 %combine_rest.1 = bf16[8,4,128,384]{3,2,1,0:T(8,128)(2,1)} custom-call(s32[32]{0:T(128)} %reshape.112.sel_ref, bf16[16,656,128]{2,1,0:T(8,128)(2,1)} %all-to-all-done.3.back_ref, f32[8,2,128,128]{3,2,1,0:T(8,128)} %get-tuple-element.29.own_ref, f32[8,2,128,384]{3,2,1,0:T(8,128)} %get-tuple-element.30.dx_ref, ...), custom_call_target="tpu_custom_call", output_to_operand_aliasing={{}: (5, {})} | custom-call | flops 8388608 | bytes 5242880 | tf_op jit(solution)/shard_map/combine_rest/pallas_call | solution.py:611
  280.2 5.7 %all-to-all-start.5 = ((bf16[8,4,128,384]{3,2,1,0:T(8,128)(2,1)}), bf16[8,4,128,384]{3,2,1,0:T(8,128)(2,1)}, u32[]{:S(2)}, u32[]{:S(2)}) async-start(bf16[8,4,128,384]{3,2,1,0:T(8,128)(2,1)} %combine_rest.1), calls=%async_computation.5 | async-start | bytes 6291456 | tf_op jit(solution)/shard_map/all_to_all | solution.py:740
  285.9 2.5 text_sum.1
  288.3 0.1 collective-permute-start
  288.4 1.4 collective-permute-done
  289.9 0.9 maximum_select_fusion.3
  290.8 3.8 %collective-permute-start.1 = (bf16[2,4,16,384]{3,2,1,0:T(8,128)(2,1)S(1)}, bf16[2,4,16,384]{3,2,1,0:T(8,128)(2,1)S(1)}, u32[]{:S(2)}, u32[]{:S(2)}) collective-permute-start(bf16[2,4,16,384]{3,2,1,0:T(8,128)(2,1)S(1)} %maximum_select_fusion.3), channel_id=1, source_target_pairs={{0,16},{8,24},{16,0},{24,8},{32,48},{40,56},{48,32},{56,40},{64,80... | collective-permute-start | bytes 294920 | tf_op jit(solution)/shard_map/ppermute | solution.py:663
  294.6 3.1 collective-permute-done.1
  297.7 5.3 %collective-permute-start.2 = (bf16[4,4,16,384]{3,2,1,0:T(8,128)(2,1)S(1)}, bf16[4,4,16,384]{3,2,1,0:T(8,128)(2,1)S(1)}, u32[]{:S(2)}, u32[]{:S(2)}) collective-permute-start(bf16[4,4,16,384]{3,2,1,0:T(8,128)(2,1)S(1)} %maximum_select_fusion.2), channel_id=1, source_target_pairs={{0,48},{8,56},{16,32},{24,40},{32,16},{40,24},{48,0},{56,8},{64,11... | collective-permute-start | bytes 589832 | tf_op jit(solution)/shard_map/ppermute | solution.py:663
  303.1 4.5 %collective-permute-done.2 = bf16[4,4,16,384]{3,2,1,0:T(8,128)(2,1)S(1)} collective-permute-done((bf16[4,4,16,384]{3,2,1,0:T(8,128)(2,1)S(1)}, bf16[4,4,16,384]{3,2,1,0:T(8,128)(2,1)S(1)}, u32[]{:S(2)}, u32[]{:S(2)}) %collective-permute-start.2) | collective-permute-done | bytes 196640 | tf_op jit(solution)/shard_map/ppermute | solution.py:663
  307.6 0.6 collective-permute-start.3
  308.2 21.5 %collective-permute-done.3 = bf16[8,4,16,384]{3,2,1,0:T(8,128)(2,1)S(1)} collective-permute-done((bf16[8,4,16,384]{3,2,1,0:T(8,128)(2,1)S(1)}, bf16[8,4,16,384]{3,2,1,0:T(8,128)(2,1)S(1)}, u32[]{:S(2)}, u32[]{:S(2)}) %collective-permute-start.3) | collective-permute-done | bytes 393248 | tf_op jit(solution)/shard_map/ppermute | solution.py:663
  329.7 0.1 fusion
  329.9 0.9 fusion.5
  330.8 3.2 unpack.1
  (29 shorter events, 0.4 us)
Async XLA Ops:
  3.8 7.6 %copy-start.1 = (s32[128,8]{0,1:T(8,128)S(1)}, s32[128,8]{0,1:T(8,128)}, u32[]{:S(2)}) copy-start(s32[128,8]{0,1:T(8,128)} %param.19) | copy-start | bytes 12292
  3.8 7.6 %copy-start.2 = (s32[128]{0:T(128)S(1)}, s32[128]{0:T(128)}, u32[]{:S(2)}) copy-start(s32[128]{0:T(128)} %param.20) | copy-start | bytes 1540
  3.8 10.6 %copy-start.6 = (s32[256]{0:T(256)S(1)}, s32[256]{0:T(256)}, u32[]{:S(2)}) copy-start(s32[256]{0:T(256)} %param.21) | copy-start | bytes 3076
  3.9 44.4 %all-to-all-start = ((bf16[8,4,128,384]{3,2,1,0:T(8,128)(2,1)}), bf16[8,4,128,384]{3,2,1,0:T(8,128)(2,1)}, u32[]{:S(2)}, u32[]{:S(2)}) async-start(bf16[8,4,128,384]{3,2,1,0:T(8,128)(2,1)} %pack.1), calls=%async_computation | async-start | bytes 6291456 | tf_op jit(solution)/shard_map/all_to_all | solution.py:707
  11.8 0.5 copy-start.4
  54.0 65.1 %all-to-all-start.1 = ((bf16[16,544,256]{2,1,0:T(8,128)(2,1)}), bf16[16,544,256]{2,1,0:T(8,128)(2,1)}, u32[]{:S(2)}, u32[]{:S(2)}) async-start(bf16[16,544,256]{2,1,0:T(8,128)(2,1)} %send_first.1), calls=%async_computation.1 | async-start | bytes 8912896 | tf_op jit(solution)/shard_map/all_to_all | solution.py:716
  122.8 13.4 %copy-start.3 = (s32[128]{0:T(128)S(1)}, s32[128]{0:T(128)}, u32[]{:S(2)}) copy-start(s32[128]{0:T(128)} %param.20) | copy-start | bytes 1540
  122.8 14.0 %copy-start = (s32[16,8]{0,1:T(8,128)S(1)}, s32[16,8]{0,1:T(8,128)}, u32[]{:S(2)}) copy-start(s32[16,8]{0,1:T(8,128)} %get-tuple-element.40) | copy-start | bytes 1540
  122.8 14.2 %copy-start.5 = (s32[64]{0:T(128)S(1)}, s32[64]{0:T(128)}, u32[]{:S(2)}) copy-start(s32[64]{0:T(128)} %copy-done.4) | copy-start | bytes 772
  122.8 45.9 %all-to-all-start.2 = ((bf16[16,528,128]{2,1,0:T(8,128)(2,1)}), bf16[16,528,128]{2,1,0:T(8,128)(2,1)}, u32[]{:S(2)}, u32[]{:S(2)}) async-start(bf16[16,528,128]{2,1,0:T(8,128)(2,1)} %get-tuple-element.24), calls=%async_computation.2 | async-start | bytes 4325376 | tf_op jit(solution)/shard_map/all_to_all | solution.py:718
  168.7 60.8 %all-to-all-start.4 = ((bf16[16,512,256]{2,1,0:T(8,128)(2,1)}), bf16[16,512,256]{2,1,0:T(8,128)(2,1)}, u32[]{:S(2)}, u32[]{:S(2)}) async-start(bf16[16,512,256]{2,1,0:T(8,128)(2,1)} %get-tuple-element.32), calls=%async_computation.4 | async-start | bytes 8388608 | tf_op jit(solution)/shard_map/all_to_all | solution.py:722
  229.6 46.5 %all-to-all-start.3 = ((bf16[16,656,128]{2,1,0:T(8,128)(2,1)}), bf16[16,656,128]{2,1,0:T(8,128)(2,1)}, u32[]{:S(2)}, u32[]{:S(2)}) async-start(bf16[16,656,128]{2,1,0:T(8,128)(2,1)} %get-tuple-element.28), calls=%async_computation.3 | async-start | bytes 5373952 | tf_op jit(solution)/shard_map/all_to_all | solution.py:727
  280.2 50.6 %all-to-all-start.5 = ((bf16[8,4,128,384]{3,2,1,0:T(8,128)(2,1)}), bf16[8,4,128,384]{3,2,1,0:T(8,128)(2,1)}, u32[]{:S(2)}, u32[]{:S(2)}) async-start(bf16[8,4,128,384]{3,2,1,0:T(8,128)(2,1)} %combine_rest.1), calls=%async_computation.5 | async-start | bytes 6291456 | tf_op jit(solution)/shard_map/all_to_all | solution.py:740
  288.3 1.5 collective-permute-start
  290.8 6.9 %collective-permute-start.1 = (bf16[2,4,16,384]{3,2,1,0:T(8,128)(2,1)S(1)}, bf16[2,4,16,384]{3,2,1,0:T(8,128)(2,1)S(1)}, u32[]{:S(2)}, u32[]{:S(2)}) collective-permute-start(bf16[2,4,16,384]{3,2,1,0:T(8,128)(2,1)S(1)} %maximum_select_fusion.3), channel_id=1, source_target_pairs={{0,16},{8,24},{16,0},{24,8},{32,48},{40,56},{48,32},{56,40},{64,80... | collective-permute-start | bytes 294920 | tf_op jit(solution)/shard_map/ppermute | solution.py:663
  297.7 9.8 %collective-permute-start.2 = (bf16[4,4,16,384]{3,2,1,0:T(8,128)(2,1)S(1)}, bf16[4,4,16,384]{3,2,1,0:T(8,128)(2,1)S(1)}, u32[]{:S(2)}, u32[]{:S(2)}) collective-permute-start(bf16[4,4,16,384]{3,2,1,0:T(8,128)(2,1)S(1)} %maximum_select_fusion.2), channel_id=1, source_target_pairs={{0,48},{8,56},{16,32},{24,40},{32,16},{40,24},{48,0},{56,8},{64,11... | collective-permute-start | bytes 589832 | tf_op jit(solution)/shard_map/ppermute | solution.py:663
  307.6 22.1 %collective-permute-start.3 = (bf16[8,4,16,384]{3,2,1,0:T(8,128)(2,1)S(1)}, bf16[8,4,16,384]{3,2,1,0:T(8,128)(2,1)S(1)}, u32[]{:S(2)}, u32[]{:S(2)}) collective-permute-start(bf16[8,4,16,384]{3,2,1,0:T(8,128)(2,1)S(1)} %maximum_select_fusion.1), channel_id=1, source_target_pairs={{0,64},{8,72},{16,80},{24,88},{32,96},{40,104},{48,112},{56,120},{... | collective-permute-start | bytes 1179656 | tf_op jit(solution)/shard_map/ppermute | solution.py:663

commit v3 on v2

--- a/solution.py
+++ b/solution.py
@@ -167,24 +167,6 @@
     ]
 
 
-def pick_rest_kernel(sel_ref, x_ref, o_ref, sems):
-    finish(go(picked(sel_ref, x_ref, o_ref, sems, pl.ds(WF, WR))))
-
-
-def pick_rest(sel, x):
-    return pl.pallas_call(
-        pick_rest_kernel,
-        grid=(1,),
-        in_specs=[pl.BlockSpec(memory_space=SMEM), whole(LOCAL_KV)],
-        out_specs=pl.BlockSpec(memory_space=ANY),
-        out_shape=jax.ShapeDtypeStruct((GROUPS, SEND_REST, WR), BF16),
-        scratch_shapes=[pltpu.SemaphoreType.DMA((GROUPS, 2 * MOST))],
-        compiler_params=params(),
-        cost_estimate=cost(0, (SLOTS + TILES) * 2 * TILE * WR * 2),
-        name="pick_rest",
-    )(sel, x)
-
-
 def text_chunk(x_ref, text_ref, which, c, lanes):
     if c < TCHUNKS - 1:
         return x_ref[2 * c : 2 * c + 2, which, :, lanes].reshape(256, HD)
@@ -218,10 +200,23 @@
     return jnp.sum(jnp.where(hit, block, 0.0), axis=1, keepdims=True)
 
 
-def send_first_kernel(
-    sel_ref, n_ref, tq_ref, tk_ref, tv_ref, x_ref, o_ref, s_ref, part_ref, sems, part_sems
+def send_kernel(
+    sel_ref,
+    n_ref,
+    tq_ref,
+    tk_ref,
+    tv_ref,
+    x_ref,
+    o_ref,
+    rest_ref,
+    s_ref,
+    part_ref,
+    sems,
+    rest_sems,
+    part_sems,
 ):
     tiles = go(picked(sel_ref, x_ref, o_ref, sems, pl.ds(0, WF)))
+    tiles += go(picked(sel_ref, x_ref, rest_ref, rest_sems, pl.ds(WF, WR)))
     live = lax.broadcasted_iota(jnp.int32, (TXT, TXT), 1) < n_ref[0]
     lane = lax.broadcasted_iota(jnp.int32, (TXT, HD), 1)
     stats = jnp.zeros((TXT, HD), F32)
@@ -262,22 +257,26 @@
     finish(tiles + parts)
 
 
-def send_first(sel, n, tq, tk, tv, x):
+def send(sel, n, tq, tk, tv, x):
     return pl.pallas_call(
-        send_first_kernel,
+        send_kernel,
         grid=(1,),
         in_specs=[pl.BlockSpec(memory_space=SMEM)] * 2 + [whole(TEXT)] * 3 + [whole(LOCAL_KV)],
-        out_specs=pl.BlockSpec(memory_space=ANY),
-        out_shape=jax.ShapeDtypeStruct((GROUPS, SEND_FIRST, WF), BF16),
+        out_specs=any_specs(2),
+        out_shape=[
+            jax.ShapeDtypeStruct((GROUPS, SEND_FIRST, WF), BF16),
+            jax.ShapeDtypeStruct((GROUPS, SEND_REST, WR), BF16),
+        ],
         scratch_shapes=[
             pltpu.VMEM((TCHUNKS, TXT, 256), F32),
             pltpu.VMEM((NH + 1, TXT, HD), BF16),
             pltpu.SemaphoreType.DMA((GROUPS, 2 * MOST)),
+            pltpu.SemaphoreType.DMA((GROUPS, 2 * MOST)),
             pltpu.SemaphoreType.DMA((GROUPS, NH + 1)),
         ],
         compiler_params=params(),
         cost_estimate=cost(4 * NH * TXT * TCHUNKS * 256 * HD, 5 << 20, NH * TXT * 1280),
-        name="send_first",
+        name="send",
     )(sel, n, tq, tk, tv, x)
 
 
@@ -414,84 +413,125 @@
 CHUNKS = KT // 2 + 1
 
 
-def video_kernel(first, slot_ref, count_ref, n_ref, kv_ref, qg_ref, got_ref, tk_ref, tv_ref, *refs):
+def video_kernel(
+    first, slot_ref, count_ref, n_ref, x_ref, got_ref, tk_ref, tv_ref, *refs
+):
     if first:
         out_ref, back_ref, own_ref, text_ref = refs[:4]
         refs = refs[4:]
     else:
         tqg_ref, tacc_ref, text0_ref, out_ref, back_ref, own_ref = refs[:6]
         refs = refs[6:]
-    keys, values, s_ref, p_ref, dk_acc, dv_acc, tk_acc, tv_acc, pool = refs
-    pool[:TILES] = kv_ref[...]
-    pool[TILES:] = got_ref[...].reshape(SLOTS, 2, TILE, HD)
-    keys[0] = tk_ref[...]
-    values[0] = tv_ref[...]
-    dk_acc[...] = jnp.zeros((POOL, TILE, HD), F32)
-    dv_acc[...] = jnp.zeros((POOL, TILE, HD), F32)
+    keys, values, s_ref, p_ref, dk_acc, dv_acc, tk_acc, tv_acc, pool, qg, stage = refs[:11]
+    kv_sems, got_sems, qg_sem, back_sems, own_sems = refs[11:]
+    base, heads = (0, NF) if first else (NF, NH - NF)
+    mine = slice(base * HD, (base + heads) * HD)
+    lanes = pl.ds(base * HD, heads * HD)
+
+    def pool_rows(slot, kv):
+        return pl.ds(pl.multiple_of((2 * slot + kv) * TILE, TILE), TILE)
+
+    loads = [
+        pltpu.make_async_copy(
+            x_ref.at[t, kv, :, lanes], pool.at[pool_rows(t, kv)], kv_sems.at[t, kv]
+        )
+        for t in range(TILES)
+        for kv in range(2)
+    ]
+    loads.append(pltpu.make_async_copy(x_ref.at[:, pl.ds(2, 2), :, lanes], qg, qg_sem))
+    loads += [
+        pltpu.make_async_copy(
+            got_ref.at[g, pl.ds(0, PAIR_ROWS)],
+            pool.at[pl.ds(2 * TILES * TILE + g * PAIR_ROWS, PAIR_ROWS)],
+            got_sems.at[g],
+        )
+        for g in range(GROUPS)
+    ]
+    go(loads)
+    keys[0] = tk_ref[:, mine]
+    values[0] = tv_ref[:, mine]
+
+    def clear(slot, carry):
+        dk_acc[slot] = jnp.zeros((TILE, heads * HD), F32)
+        dv_acc[slot] = jnp.zeros((TILE, heads * HD), F32)
+        return carry
+
+    lax.fori_loop(0, POOL, clear, 0)
     if first:
-        tk_acc[...] = jnp.zeros((TXT, HD), F32)
-        tv_acc[...] = jnp.zeros((TXT, HD), F32)
+        tk_acc[...] = jnp.zeros((TXT, heads * HD), F32)
+        tv_acc[...] = jnp.zeros((TXT, heads * HD), F32)
     else:
-        tk_acc[...] = tacc_ref[0, :, WF:]
-        tv_acc[...] = tacc_ref[1, :, WF:]
+        tk_acc[...] = tacc_ref[0, :, mine]
+        tv_acc[...] = tacc_ref[1, :, mine]
     text_live = lax.broadcasted_iota(jnp.int32, (TXT, TILE), 0) < n_ref[0]
+    finish(loads)
+    cuts = [slice(h * HD, (h + 1) * HD) for h in range(heads)]
 
     def tile(i, carry):
         count = count_ref[i]
-        query, grad = qg_ref[i, 0], qg_ref[i, 1]
 
         def run(pairs):
             slots = [slot_ref[i * KT + e] for e in range(2 * pairs)]
             for e in range(2 * pairs):
                 half = pl.ds((e % 2) * TILE, TILE)
-                keys[1 + e // 2, half] = pool[slots[e], 0]
-                values[1 + e // 2, half] = pool[slots[e], 1]
-            top = None
-            for c in range(pairs + 1):
-                s = dot_nt(keys[c], query) * FACTOR2
-                if c == 0:
-                    s = jnp.where(text_live, s, NEGATIVE)
-                elif c == pairs:
-                    s = jnp.concatenate(
-                        [s[:TILE], jnp.where(2 * pairs <= count, s[TILE:], NEGATIVE)], axis=0
-                    )
-                s_ref[c] = s
-                part = jnp.max(s.reshape(32, 8, TILE), axis=0)
-                top = part if top is None else jnp.maximum(top, part)
-            top = jnp.max(top, axis=0, keepdims=True)
-            total = None
-            for c in range(pairs + 1):
-                p = jnp.exp2(s_ref[c] - top)
-                s_ref[c] = p
-                part = jnp.sum(p.reshape(32, 8, TILE), axis=0)
-                total = part if total is None else total + part
-            scale = 1.0 / jnp.sum(total, axis=0, keepdims=True)
-            out = None
-            for c in range(pairs + 1):
-                p = s_ref[c] * scale
-                s_ref[c] = p
-                p = p.astype(BF16)
-                p_ref[c] = p
-                part = dot_tn(p, values[c])
-                out = part if out is None else out + part
-            out_ref[i, 0] = out.astype(BF16)
-            offset = jnp.sum((grad.astype(F32) * out).T, axis=0, keepdims=True)
-            query_grad = None
-            for c in range(pairs + 1):
-                ds = (s_ref[c] * (dot_nt(values[c], grad) - offset)).astype(BF16)
-                part = dot_tn(ds, keys[c])
-                query_grad = part if query_grad is None else query_grad + part
-                key_grad = dot_nn(ds, query)
-                value_grad = dot_nn(p_ref[c], grad)
-                if c == 0:
-                    tk_acc[...] += key_grad
-                    tv_acc[...] += value_grad
-                else:
-                    for e in (0, 1):
-                        slot = slots[2 * (c - 1) + e]
-                        dk_acc[slot] += key_grad[e * TILE : (e + 1) * TILE]
-                        dv_acc[slot] += value_grad[e * TILE : (e + 1) * TILE]
-            out_ref[i, 1] = (query_grad * FACTOR).astype(BF16)
+                keys[1 + e // 2, half] = pool[pool_rows(slots[e], 0)]
+                values[1 + e // 2, half] = pool[pool_rows(slots[e], 1)]
+            query = [qg[i, 0, :, cut] for cut in cuts]
+            grad = [qg[i, 1, :, cut] for cut in cuts]
+            tops, scales, offsets = [], [], []
+            for h, cut in enumerate(cuts):
+                top = None
+                for c in range(pairs + 1):
+                    s = dot_nt(keys[c, :, cut], query[h]) * FACTOR2
+                    if c == 0:
+                        s = jnp.where(text_live, s, NEGATIVE)
+                    elif c == pairs:
+                        dead = jnp.where(2 * pairs <= count, s[TILE:], NEGATIVE)
+                        s = jnp.concatenate([s[:TILE], dead], axis=0)
+                    s_ref[h, c] = s
+                    part = jnp.max(s.reshape(32, 8, TILE), axis=0)
+                    top = part if top is None else jnp.maximum(top, part)
+                tops.append(jnp.max(top, axis=0, keepdims=True))
+            for h, cut in enumerate(cuts):
+                total = None
+                for c in range(pairs + 1):
+                    p = jnp.exp2(s_ref[h, c] - tops[h])
+                    s_ref[h, c] = p
+                    part = jnp.sum(p.reshape(32, 8, TILE), axis=0)
+                    total = part if total is None else total + part
+                scales.append(1.0 / jnp.sum(total, axis=0, keepdims=True))
+            for h, cut in enumerate(cuts):
+                out = None
+                for c in range(pairs + 1):
+                    p = s_ref[h, c] * scales[h]
+                    s_ref[h, c] = p
+                    p = p.astype(BF16)
+                    p_ref[h, c] = p
+                    part = dot_tn(p, values[c, :, cut])
+                    out = part if out is None else out + part
+                out_ref[i, 0, :, cut] = out.astype(BF16)
+                offsets.append(
+                    jnp.sum((grad[h].astype(F32) * out).T, axis=0, keepdims=True)
+                )
+            for h, cut in enumerate(cuts):
+                query_grad = None
+                for c in range(pairs + 1):
+                    dp = dot_nt(values[c, :, cut], grad[h])
+                    ds = (s_ref[h, c] * (dp - offsets[h])).astype(BF16)
+                    part = dot_tn(ds, keys[c, :, cut])
+                    query_grad = part if query_grad is None else query_grad + part
+                    key_grad = dot_nn(ds, query[h])
+                    value_grad = dot_nn(p_ref[h, c], grad[h])
+                    if c == 0:
+                        tk_acc[:, cut] += key_grad
+                        tv_acc[:, cut] += value_grad
+                    else:
+                        for e in (0, 1):
+                            slot = slots[2 * (c - 1) + e]
+                            rows = slice(e * TILE, (e + 1) * TILE)
+                            dk_acc[slot, :, cut] += key_grad[rows]
+                            dv_acc[slot, :, cut] += value_grad[rows]
+                out_ref[i, 1, :, cut] = (query_grad * FACTOR).astype(BF16)
 
         for pairs in range(1, KT // 2 + 1):
 
@@ -503,89 +543,87 @@
 
     lax.fori_loop(0, TILES, tile, 0)
 
-    own_ref[:, 0] = dk_acc[:TILES]
-    own_ref[:, 1] = dv_acc[:TILES]
+    stores = go(
+        [
+            pltpu.make_async_copy(acc.at[pl.ds(0, TILES)], own_ref.at[:, n], own_sems.at[n])
+            for n, acc in enumerate((dk_acc, dv_acc))
+        ]
+    )
+    if first:
+        text_ref[0] = tk_acc[...]
+        text_ref[1] = tv_acc[...]
+    else:
+
+        def store(n, values):
+            at = PAIR_ROWS + n * TROWS
+            stage[:, at : at + TROWS] = values.reshape(GROUPS, TROWS, HD).astype(BF16)
+
+        for h in range(NH):
+            cut = slice(h * HD, (h + 1) * HD)
+            if h < NF:
+                key_grad = tacc_ref[0, :, cut] + text0_ref[0, :, cut]
+                value_grad = tacc_ref[1, :, cut] + text0_ref[1, :, cut]
+            else:
+                key_grad, value_grad = tk_acc[...], tv_acc[...]
+            store(h, tqg_ref[:, cut])
+            store(NH + h, key_grad * FACTOR)
+            store(2 * NH + h, value_grad)
     for g in range(GROUPS):
         for m in range(MOST):
             slot = TILES + g * MOST + m
-            back_ref[g, 2 * m * TILE : (2 * m + 1) * TILE] = (dk_acc[slot] * FACTOR).astype(BF16)
-            back_ref[g, (2 * m + 1) * TILE : (2 * m + 2) * TILE] = dv_acc[slot].astype(BF16)
-    if first:
-        text_ref[0] = tk_acc[...]
-        text_ref[1] = tv_acc[...]
-        return
-
-    def store(n, values):
-        at = PAIR_ROWS + n * TROWS
-        back_ref[:, at : at + TROWS] = values.reshape(GROUPS, TROWS, HD).astype(BF16)
-
-    for h in range(NH):
-        lanes = slice(h * HD, (h + 1) * HD)
-        if h < NF:
-            key_grad = tacc_ref[0, :, lanes] + text0_ref[0, :, lanes]
-            value_grad = tacc_ref[1, :, lanes] + text0_ref[1, :, lanes]
-        else:
-            key_grad, value_grad = tk_acc[...], tv_acc[...]
-        store(h, tqg_ref[:, lanes])
-        store(NH + h, key_grad * FACTOR)
-        store(2 * NH + h, value_grad)
+            stage[g, 2 * m * TILE : (2 * m + 1) * TILE] = (dk_acc[slot] * FACTOR).astype(BF16)
+            stage[g, (2 * m + 1) * TILE : (2 * m + 2) * TILE] = dv_acc[slot].astype(BF16)
+        stores += go([pltpu.make_async_copy(stage.at[g], back_ref.at[g], back_sems.at[g])])
+    finish(stores)
 
 
 def video(first, slot, count, n, x, got, tk, tv, *text):
-    base, heads = (0, NF) if first else (NF, NH - NF)
+    heads = NF if first else NH - NF
     rows = PAIR_ROWS if first else BACK_REST
     width = heads * HD
-    smem = pl.BlockSpec(memory_space=SMEM)
-    per_head = pl.BlockSpec((TXT, HD), lambda j: (0, base + j))
-    pair = (TILES, 2, TILE, HD)
-    in_specs = [
-        smem,
-        smem,
-        smem,
-        pl.BlockSpec(pair, lambda j: (0, 0, 0, base + j)),
-        pl.BlockSpec(pair, lambda j: (0, 1, 0, base + j)),
-        pl.BlockSpec((GROUPS, PAIR_ROWS, HD), lambda j: (0, 0, j)),
-        per_head,
-        per_head,
-    ]
-    out_specs = [
-        pl.BlockSpec(pair, lambda j: (0, 0, 0, j)),
-        pl.BlockSpec((GROUPS, rows, HD), lambda j: (0, 0, j)),
-        pl.BlockSpec(pair, lambda j: (0, 0, 0, j)),
-    ]
+    pair = (TILES, 2, TILE, width)
+    in_specs = [pl.BlockSpec(memory_space=SMEM)] * 3 + any_specs(2) + [whole(TEXT)] * 2
+    out_specs = [whole(pair)] + any_specs(2)
     out_shape = [
-        jax.ShapeDtypeStruct((TILES, 2, TILE, width), BF16),
+        jax.ShapeDtypeStruct(pair, BF16),
         jax.ShapeDtypeStruct((GROUPS, rows, width), BF16),
-        jax.ShapeDtypeStruct((TILES, 2, TILE, width), F32),
+        jax.ShapeDtypeStruct(pair, F32),
     ]
     if first:
-        out_specs.append(pl.BlockSpec((2, TXT, HD), lambda j: (0, 0, j)))
+        out_specs.append(whole((2, TXT, WF)))
         out_shape.append(jax.ShapeDtypeStruct((2, TXT, WF), F32))
     else:
         in_specs += [whole(TEXT), whole((2, TXT, W)), whole((2, TXT, WF))]
     return pl.pallas_call(
         functools.partial(video_kernel, first),
-        grid=(heads,),
+        grid=(1,),
         in_specs=in_specs,
         out_specs=out_specs,
         out_shape=out_shape,
         scratch_shapes=[
-            pltpu.VMEM((CHUNKS, 256, HD), BF16),
-            pltpu.VMEM((CHUNKS, 256, HD), BF16),
-            pltpu.VMEM((CHUNKS, 256, TILE), F32),
-            pltpu.VMEM((CHUNKS, 256, TILE), BF16),
-            pltpu.VMEM((POOL, TILE, HD), F32),
-            pltpu.VMEM((POOL, TILE, HD), F32),
-            pltpu.VMEM((TXT, HD), F32),
-            pltpu.VMEM((TXT, HD), F32),
-            pltpu.VMEM((POOL, 2, TILE, HD), BF16),
+            pltpu.VMEM((CHUNKS, 256, width), BF16),
+            pltpu.VMEM((CHUNKS, 256, width), BF16),
+            pltpu.VMEM((heads, CHUNKS, 256, TILE), F32),
+            pltpu.VMEM((heads, CHUNKS, 256, TILE), BF16),
+            pltpu.VMEM((POOL, TILE, width), F32),
+            pltpu.VMEM((POOL, TILE, width), F32),
+            pltpu.VMEM((TXT, width), F32),
+            pltpu.VMEM((TXT, width), F32),
+            pltpu.VMEM((POOL * 2 * TILE, width), BF16),
+            pltpu.VMEM(pair, BF16),
+            pltpu.VMEM((GROUPS, rows, width), BF16),
+            pltpu.SemaphoreType.DMA((TILES, 2)),
+            pltpu.SemaphoreType.DMA((GROUPS,)),
+            pltpu.SemaphoreType.DMA,
+            pltpu.SemaphoreType.DMA((GROUPS,)),
+            pltpu.SemaphoreType.DMA((2,)),
         ],
         compiler_params=params(),
         cost_estimate=cost(
             12 * heads * TLOCAL * 1280 * HD, heads * (8 << 20), heads * TLOCAL * 1280
         ),
         name="video_first" if first else "video_rest",
-    )(slot, count, n, x, x, got, tk, tv, *text)
+    )(slot, count, n, x, got, tk, tv, *text)
 
 
 def combine_kernel(sel_ref, back_ref, own_ref, dx_ref, half_ref, *refs):
@@ -710,12 +748,13 @@
     sel, slot, count = tables(tile_list, tile_count, own)
     n = jnp.sum((text_mask > 0).astype(jnp.int32)).reshape(1)
     n_own = jnp.where(own == 0, n, 0)
+    sel, slot, count, n, n_own = lax.optimization_barrier((sel, slot, count, n, n_own))
     text = (text_query, text_key, text_value)
 
-    send = send_first(sel, n_own, *text, x)
-    got0 = lax.all_to_all(send, "seq", 0, 0, tiled=True)
-    send, text_out = text_stats(own.reshape(1), got0, text_grad, pick_rest(sel, x))
-    got = lax.all_to_all(send, "seq", 0, 0, tiled=True)
+    send0, send1 = send(sel, n_own, *text, x)
+    got0 = lax.all_to_all(send0, "seq", 0, 0, tiled=True)
+    send1, text_out = text_stats(own.reshape(1), got0, text_grad, send1)
+    got = lax.all_to_all(send1, "seq", 0, 0, tiled=True)
     half0, back0, own0, text0 = video(
         True, slot, count, n, x, got0, text_key, text_value
     )

time: 339 us -> 322 us (0.950)
  blocking collectives: 0 us -> 58.6 us
  waiting for transfers between devices: 172 us -> 119 us
  starting transfers between devices: 62.9 us -> 49.6 us
  Pallas kernels: 90.5 us -> 82 us
    all_to_all x0 -> x1, blocking collectives: none -> 58.6 us  [body(): got0 = lax.all_to_all(send0, 'seq', 0, 0, tiled=True)]
    all_to_all x2 -> x1, waiting for transfers between devices: 54.9 us -> 2.84 us  [body(): got = lax.all_to_all(send1, 'seq', 0, 0, tiled=True)]
    all_to_all x2 -> x1, starting transfers between devices: 20.1 us -> 5.57 us  [body(): got = lax.all_to_all(send1, 'seq', 0, 0, tiled=True)]
    pallas_call x4 -> x3, Pallas kernels: 58.3 us -> 50 us  [the longest x2 43 us: video(): pl.pallas_call(functools.partial(video_kernel, first), grid=(1,), in_spec...]
  transfers between devices with their start and end apart: 10 -> 9, of which waited for: 8 -> 8; matrix products, arithmetic and copies ran while one was open for 2% -> 2% of each run, Pallas kernels for 21% -> 19%
where the time goes in v3:
time: 322 us; the launch traced here: 317 us
  waiting for transfers between devices  119 us (37%)
  Pallas kernels  82 us (25%)
  blocking collectives  58.6 us (18%)
  starting transfers between devices  49.6 us (15%)
    all_to_all x1, blocking collectives, body(): got0 = lax.all_to_all(send0, 'seq', 0, 0, tiled=True)  58.6 us
    pallas_call x2, Pallas kernels, video(): pl.pallas_call(functools.partial(video_kernel, first), grid=(1,), in_spec...  43 us
    all_to_all x1, waiting for transfers between devices, body(): lax.all_to_all(pack(video_key, video_value, video_query, video_grad), 'he...  32 us
    ppermute x4, waiting for transfers between devices, swapped(): return lax.ppermute(x, 'seq', [(i, i ^ mask) for i in range(GROUPS)])  30.5 us
    all_to_all x1, waiting for transfers between devices, body(): back = lax.all_to_all(back, 'seq', 0, 0, tiled=True)  28.1 us
    all_to_all x1, waiting for transfers between devices, body(): back0 = lax.all_to_all(back0, 'seq', 0, 0, tiled=True)  25.9 us
    all_to_all x1, starting transfers between devices, body(): back = lax.all_to_all(back, 'seq', 0, 0, tiled=True)  13.1 us
    pallas_call x1, Pallas kernels, text_backward(): pl.pallas_call(text_backward_kernel, grid=(1,), in_specs=[pl.BlockSpec(me...  10.2 us
  transfers between devices with their start and end apart: 9, of which 8 were waited for; matrix products, arithmetic and copies ran while one was open for 2% of the time, Pallas kernels for 19%

profile of v3, /device:TPU:6, one launch (start us, length us, event | category | flops | bytes accessed | tf_op | source)
XLA Modules:
  0.0 317.4 jit_solution(10723183690205306441)
XLA Ops:
  0.6 3.1 pack.1
  3.8 7.6 %all-to-all-start = ((bf16[8,4,128,384]{3,2,1,0:T(8,128)(2,1)}), bf16[8,4,128,384]{3,2,1,0:T(8,128)(2,1)}, u32[]{:S(2)}, u32[]{:S(2)}) async-start(bf16[8,4,128,384]{3,2,1,0:T(8,128)(2,1)} %pack.1), calls=%async_computation | async-start | bytes 6291456 | tf_op jit(solution)/shard_map/all_to_all | solution.py:745
  11.4 0.7 dynamic_slice.7.count_ref
  12.0 0.1 copy.31
  12.2 0.1 copy.34
  12.3 0.1 eq.76
  12.4 0.1 fusion.1
  12.5 0.1 reshape.115
  12.6 0.1 copy.35
  12.6 0.1 eq.69
  12.7 0.4 compare_reduce_fusion
  13.2 0.1 copy.32
  13.3 0.1 select_reduce_fusion.1
  13.5 0.1 select_n.80
  13.6 0.1 copy.33
  13.7 0.6 reshape.112.sel_ref
  14.3 0.6 fusion.4
  15.5 0.7 select_reduce_fusion.slot_ref
  16.2 32.0 %all-to-all-done.x_ref = bf16[8,4,128,384]{3,2,1,0:T(8,128)(2,1)} async-done(((bf16[8,4,128,384]{3,2,1,0:T(8,128)(2,1)}), bf16[8,4,128,384]{3,2,1,0:T(8,128)(2,1)}, u32[]{:S(2)}, u32[]{:S(2)}) %all-to-all-start) | async-done | bytes 3145760 | tf_op jit(solution)/shard_map/all_to_all | solution.py:745
  48.2 7.0 %send.1 = (bf16[16,544,256]{2,1,0:T(8,128)(2,1)}, bf16[16,528,128]{2,1,0:T(8,128)(2,1)}) custom-call(s32[32]{0:T(128)} %reshape.112.sel_ref, s32[1]{0:T(128)S(6)} %select_n.83.n_ref, bf16[256,384]{1,0:T(8,128)(2,1)} %tq_ref.3, bf16[256,384]{1,0:T(8,128)(2,1)} %tk_ref.7, bf16[256,384]{1,0:T(8,128)(2,1)} %tv_ref.7, bf16[8,4,128,384]{3,2,1,0:T(8,128)(2,1)} %all-to-all-done.x_ref), custom_call_target="tpu_custom_call" | custom-call | flops 503316480 | bytes 5242880 | tf_op jit(solution)/shard_map/send/pallas_call | solution.py:261
  55.2 58.6 %all_to_all.30.got_ref = bf16[16,544,256]{2,1,0:T(8,128)(2,1)} all-to-all(bf16[16,544,256]{2,1,0:T(8,128)(2,1)} %get-tuple-element.36), channel_id=1, replica_groups=mesh['seq'=16,'head'=8] {'seq'}, dimensions={0} | all-to-all | bytes 8912896 | tf_op jit(solution)/shard_map/all_to_all | solution.py:755
  113.8 3.7 %text_stats.1 = (bf16[16,528,128]{2,1,0:T(8,128)(2,1)}, bf16[16,384]{1,0:T(8,128)(2,1)}) custom-call(s32[1]{0:T(128)} %bitcast.2.own_ref, bf16[16,544,256]{2,1,0:T(8,128)(2,1)} %all_to_all.30.got_ref, bf16[256,384]{1,0:T(8,128)(2,1)} %tg_ref.3, bf16[16,528,128]{2,1,0:T(8,128)(2,1)} %get-tuple-element.37.in_ref), custom_call_target="tpu_custom_call", output_to_operand_aliasing={{0}: (3, {})} | custom-call | flops 786432 | bytes 524288 | tf_op jit(solution)/shard_map/text_stats/pallas_call | solution.py:318
  117.5 5.6 %all-to-all-start.2 = ((bf16[16,528,128]{2,1,0:T(8,128)(2,1)}), bf16[16,528,128]{2,1,0:T(8,128)(2,1)}, u32[]{:S(2)}, u32[]{:S(2)}) async-start(bf16[16,528,128]{2,1,0:T(8,128)(2,1)} %get-tuple-element.38), calls=%async_computation.2 | async-start | bytes 4325376 | tf_op jit(solution)/shard_map/all_to_all | solution.py:757
  123.1 24.9 %video_first.1 = (bf16[8,2,128,256]{3,2,1,0:T(8,128)(2,1)}, bf16[16,512,256]{2,1,0:T(8,128)(2,1)}, f32[8,2,128,256]{3,2,1,0:T(8,128)}, f32[2,256,256]{2,1,0:T(8,128)}) custom-call(s32[64]{0:T(128)} %select_reduce_fusion.slot_ref, s32[8]{0:T(128)} %dynamic_slice.7.count_ref, s32[1]{0:T(128)} %bitcast.n_ref, bf16[8,4,128,384]{3,2,1,0:T(8,128)(2,1)} %all-to-all-done.x_ref, ...), custom_call_target="tpu_custom_call" | custom-call | flops 4026531840 | bytes 16777216 | tf_op jit(solution)/shard_map/video_first/pallas_call | solution.py:597
  148.0 2.8 all-to-all-done.2.got_ref
  150.8 7.9 %all-to-all-start.4 = ((bf16[16,512,256]{2,1,0:T(8,128)(2,1)}), bf16[16,512,256]{2,1,0:T(8,128)(2,1)}, u32[]{:S(2)}, u32[]{:S(2)}) async-start(bf16[16,512,256]{2,1,0:T(8,128)(2,1)} %get-tuple-element.46), calls=%async_computation.4 | async-start | bytes 8388608 | tf_op jit(solution)/shard_map/all_to_all | solution.py:761
  158.7 10.2 %text_backward.1 = (f32[256,384]{1,0:T(8,128)}, f32[2,256,384]{2,1,0:T(8,128)}, f32[8,2,128,384]{3,2,1,0:T(8,128)}) custom-call(s32[1]{0:T(128)S(6)} %select_n.83.n_ref, bf16[16,528,128]{2,1,0:T(8,128)(2,1)} %all-to-all-done.2.got_ref, bf16[256,384]{1,0:T(8,128)(2,1)} %tq_ref.3, bf16[256,384]{1,0:T(8,128)(2,1)} %tk_ref.7, bf16[256,384]{1,0:T(8,128)(2,1)} %tv_ref.7, ...), custom_call_target="tpu_custom_call" | custom-call | flops 1258291200 | bytes 8388608 | tf_op jit(solution)/shard_map/text_backward/pallas_call | solution.py:390
  168.8 18.1 %video_rest.1 = (bf16[8,2,128,128]{3,2,1,0:T(8,128)(2,1)}, bf16[16,656,128]{2,1,0:T(8,128)(2,1)}, f32[8,2,128,128]{3,2,1,0:T(8,128)}) custom-call(s32[64]{0:T(128)} %select_reduce_fusion.slot_ref, s32[8]{0:T(128)} %dynamic_slice.7.count_ref, s32[1]{0:T(128)} %bitcast.n_ref, bf16[8,4,128,384]{3,2,1,0:T(8,128)(2,1)} %all-to-all-done.x_ref, ...), custom_call_target="tpu_custom_call" | custom-call | flops 2013265920 | bytes 8388608 | tf_op jit(solution)/shard_map/video_rest/pallas_call | solution.py:597
  186.9 25.9 %all-to-all-done.4.back_ref = bf16[16,512,256]{2,1,0:T(8,128)(2,1)} async-done(((bf16[16,512,256]{2,1,0:T(8,128)(2,1)}), bf16[16,512,256]{2,1,0:T(8,128)(2,1)}, u32[]{:S(2)}, u32[]{:S(2)}) %all-to-all-start.4) | async-done | bytes 4194336 | tf_op jit(solution)/shard_map/all_to_all | solution.py:761
  212.9 13.1 %all-to-all-start.3 = ((bf16[16,656,128]{2,1,0:T(8,128)(2,1)}), bf16[16,656,128]{2,1,0:T(8,128)(2,1)}, u32[]{:S(2)}, u32[]{:S(2)}) async-start(bf16[16,656,128]{2,1,0:T(8,128)(2,1)} %get-tuple-element.42), calls=%async_computation.3 | async-start | bytes 5373952 | tf_op jit(solution)/shard_map/all_to_all | solution.py:766
  225.9 5.4 %combine_first.1.refs_0_ = bf16[8,4,128,384]{3,2,1,0:T(8,128)(2,1)} custom-call(s32[32]{0:T(128)} %reshape.112.sel_ref, bf16[16,512,256]{2,1,0:T(8,128)(2,1)} %all-to-all-done.4.back_ref, f32[8,2,128,256]{3,2,1,0:T(8,128)} %get-tuple-element.47.own_ref, f32[8,2,128,384]{3,2,1,0:T(8,128)} %get-tuple-element.44.dx_ref, ...), custom_call_target="tpu_custom_call" | custom-call | flops 16777216 | bytes 10485760 | tf_op jit(solution)/shard_map/combine_first/pallas_call | solution.py:649
  231.3 28.1 %all-to-all-done.3.back_ref = bf16[16,656,128]{2,1,0:T(8,128)(2,1)} async-done(((bf16[16,656,128]{2,1,0:T(8,128)(2,1)}), bf16[16,656,128]{2,1,0:T(8,128)(2,1)}, u32[]{:S(2)}, u32[]{:S(2)}) %all-to-all-start.3) | async-done | bytes 2687008 | tf_op jit(solution)/shard_map/all_to_all | solution.py:766
  259.4 4.1 %combine_rest.1 = bf16[8,4,128,384]{3,2,1,0:T(8,128)(2,1)} custom-call(s32[32]{0:T(128)} %reshape.112.sel_ref, bf16[16,656,128]{2,1,0:T(8,128)(2,1)} %all-to-all-done.3.back_ref, f32[8,2,128,128]{3,2,1,0:T(8,128)} %get-tuple-element.43.own_ref, f32[8,2,128,384]{3,2,1,0:T(8,128)} %get-tuple-element.44.dx_ref, ...), custom_call_target="tpu_custom_call", output_to_operand_aliasing={{}: (5, {})} | custom-call | flops 8388608 | bytes 5242880 | tf_op jit(solution)/shard_map/combine_rest/pallas_call | solution.py:649
  263.5 5.7 %all-to-all-start.5 = ((bf16[8,4,128,384]{3,2,1,0:T(8,128)(2,1)}), bf16[8,4,128,384]{3,2,1,0:T(8,128)(2,1)}, u32[]{:S(2)}, u32[]{:S(2)}) async-start(bf16[8,4,128,384]{3,2,1,0:T(8,128)(2,1)} %combine_rest.1), calls=%async_computation.5 | async-start | bytes 6291456 | tf_op jit(solution)/shard_map/all_to_all | solution.py:779
  269.2 2.5 text_sum.1
  271.7 0.1 collective-permute-start
  271.8 1.4 collective-permute-done
  273.2 0.9 maximum_select_fusion.3
  274.1 3.8 %collective-permute-start.1 = (bf16[2,4,16,384]{3,2,1,0:T(8,128)(2,1)S(1)}, bf16[2,4,16,384]{3,2,1,0:T(8,128)(2,1)S(1)}, u32[]{:S(2)}, u32[]{:S(2)}) collective-permute-start(bf16[2,4,16,384]{3,2,1,0:T(8,128)(2,1)S(1)} %maximum_select_fusion.3), channel_id=1, source_target_pairs={{0,16},{8,24},{16,0},{24,8},{32,48},{40,56},{48,32},{56,40},{64,80... | collective-permute-start | bytes 294920 | tf_op jit(solution)/shard_map/ppermute | solution.py:701
  277.9 3.1 collective-permute-done.1
  281.0 5.3 %collective-permute-start.2 = (bf16[4,4,16,384]{3,2,1,0:T(8,128)(2,1)S(1)}, bf16[4,4,16,384]{3,2,1,0:T(8,128)(2,1)S(1)}, u32[]{:S(2)}, u32[]{:S(2)}) collective-permute-start(bf16[4,4,16,384]{3,2,1,0:T(8,128)(2,1)S(1)} %maximum_select_fusion.2), channel_id=1, source_target_pairs={{0,48},{8,56},{16,32},{24,40},{32,16},{40,24},{48,0},{56,8},{64,11... | collective-permute-start | bytes 589832 | tf_op jit(solution)/shard_map/ppermute | solution.py:701
  286.4 4.5 %collective-permute-done.2 = bf16[4,4,16,384]{3,2,1,0:T(8,128)(2,1)S(1)} collective-permute-done((bf16[4,4,16,384]{3,2,1,0:T(8,128)(2,1)S(1)}, bf16[4,4,16,384]{3,2,1,0:T(8,128)(2,1)S(1)}, u32[]{:S(2)}, u32[]{:S(2)}) %collective-permute-start.2) | collective-permute-done | bytes 196640 | tf_op jit(solution)/shard_map/ppermute | solution.py:701
  290.8 0.1 maximum_select_fusion.1
  290.9 0.6 collective-permute-start.3
  291.5 21.5 %collective-permute-done.3 = bf16[8,4,16,384]{3,2,1,0:T(8,128)(2,1)S(1)} collective-permute-done((bf16[8,4,16,384]{3,2,1,0:T(8,128)(2,1)S(1)}, bf16[8,4,16,384]{3,2,1,0:T(8,128)(2,1)S(1)}, u32[]{:S(2)}, u32[]{:S(2)}) %collective-permute-start.3) | collective-permute-done | bytes 393248 | tf_op jit(solution)/shard_map/ppermute | solution.py:701
  313.0 0.1 fusion
  313.2 0.9 fusion.5
  314.1 3.2 %unpack.1 = (bf16[128,3072]{1,0:T(8,128)(2,1)}, bf16[128,3072]{1,0:T(8,128)(2,1)}, bf16[128,3072]{1,0:T(8,128)(2,1)}, bf16[128,3072]{1,0:T(8,128)(2,1)}) custom-call(bf16[8,4,128,384]{3,2,1,0:T(8,128)(2,1)} %all-to-all-done.5.x_ref), custom_call_target="tpu_custom_call" | custom-call | bytes 6291456 | tf_op jit(solution)/shard_map/unpack/pallas_call | solution.py:141
  (19 shorter events, 0.3 us)
Async XLA Ops:
  3.8 7.6 %copy-start.1 = (s32[128]{0:T(128)S(1)}, s32[128]{0:T(128)}, u32[]{:S(2)}) copy-start(s32[128]{0:T(128)} %param.20) | copy-start | bytes 1540
  3.8 8.3 %copy-start = (s32[128,8]{0,1:T(8,128)S(1)}, s32[128,8]{0,1:T(8,128)}, u32[]{:S(2)}) copy-start(s32[128,8]{0,1:T(8,128)} %param.19) | copy-start | bytes 12292
  3.8 10.5 %copy-start.2 = (s32[256]{0:T(256)S(1)}, s32[256]{0:T(256)}, u32[]{:S(2)}) copy-start(s32[256]{0:T(256)} %param.21) | copy-start | bytes 3076
  3.8 44.4 %all-to-all-start = ((bf16[8,4,128,384]{3,2,1,0:T(8,128)(2,1)}), bf16[8,4,128,384]{3,2,1,0:T(8,128)(2,1)}, u32[]{:S(2)}, u32[]{:S(2)}) async-start(bf16[8,4,128,384]{3,2,1,0:T(8,128)(2,1)} %pack.1), calls=%async_computation | async-start | bytes 6291456 | tf_op jit(solution)/shard_map/all_to_all | solution.py:745
  117.5 33.3 %all-to-all-start.2 = ((bf16[16,528,128]{2,1,0:T(8,128)(2,1)}), bf16[16,528,128]{2,1,0:T(8,128)(2,1)}, u32[]{:S(2)}, u32[]{:S(2)}) async-start(bf16[16,528,128]{2,1,0:T(8,128)(2,1)} %get-tuple-element.38), calls=%async_computation.2 | async-start | bytes 4325376 | tf_op jit(solution)/shard_map/all_to_all | solution.py:757
  150.8 62.1 %all-to-all-start.4 = ((bf16[16,512,256]{2,1,0:T(8,128)(2,1)}), bf16[16,512,256]{2,1,0:T(8,128)(2,1)}, u32[]{:S(2)}, u32[]{:S(2)}) async-start(bf16[16,512,256]{2,1,0:T(8,128)(2,1)} %get-tuple-element.46), calls=%async_computation.4 | async-start | bytes 8388608 | tf_op jit(solution)/shard_map/all_to_all | solution.py:761
  212.9 46.5 %all-to-all-start.3 = ((bf16[16,656,128]{2,1,0:T(8,128)(2,1)}), bf16[16,656,128]{2,1,0:T(8,128)(2,1)}, u32[]{:S(2)}, u32[]{:S(2)}) async-start(bf16[16,656,128]{2,1,0:T(8,128)(2,1)} %get-tuple-element.42), calls=%async_computation.3 | async-start | bytes 5373952 | tf_op jit(solution)/shard_map/all_to_all | solution.py:766
  263.5 50.6 %all-to-all-start.5 = ((bf16[8,4,128,384]{3,2,1,0:T(8,128)(2,1)}), bf16[8,4,128,384]{3,2,1,0:T(8,128)(2,1)}, u32[]{:S(2)}, u32[]{:S(2)}) async-start(bf16[8,4,128,384]{3,2,1,0:T(8,128)(2,1)} %combine_rest.1), calls=%async_computation.5 | async-start | bytes 6291456 | tf_op jit(solution)/shard_map/all_to_all | solution.py:779
  271.7 1.5 collective-permute-start
  274.1 6.9 %collective-permute-start.1 = (bf16[2,4,16,384]{3,2,1,0:T(8,128)(2,1)S(1)}, bf16[2,4,16,384]{3,2,1,0:T(8,128)(2,1)S(1)}, u32[]{:S(2)}, u32[]{:S(2)}) collective-permute-start(bf16[2,4,16,384]{3,2,1,0:T(8,128)(2,1)S(1)} %maximum_select_fusion.3), channel_id=1, source_target_pairs={{0,16},{8,24},{16,0},{24,8},{32,48},{40,56},{48,32},{56,40},{64,80... | collective-permute-start | bytes 294920 | tf_op jit(solution)/shard_map/ppermute | solution.py:701
  281.0 9.8 %collective-permute-start.2 = (bf16[4,4,16,384]{3,2,1,0:T(8,128)(2,1)S(1)}, bf16[4,4,16,384]{3,2,1,0:T(8,128)(2,1)S(1)}, u32[]{:S(2)}, u32[]{:S(2)}) collective-permute-start(bf16[4,4,16,384]{3,2,1,0:T(8,128)(2,1)S(1)} %maximum_select_fusion.2), channel_id=1, source_target_pairs={{0,48},{8,56},{16,32},{24,40},{32,16},{40,24},{48,0},{56,8},{64,11... | collective-permute-start | bytes 589832 | tf_op jit(solution)/shard_map/ppermute | solution.py:701
  290.9 22.1 %collective-permute-start.3 = (bf16[8,4,16,384]{3,2,1,0:T(8,128)(2,1)S(1)}, bf16[8,4,16,384]{3,2,1,0:T(8,128)(2,1)S(1)}, u32[]{:S(2)}, u32[]{:S(2)}) collective-permute-start(bf16[8,4,16,384]{3,2,1,0:T(8,128)(2,1)S(1)} %maximum_select_fusion.1), channel_id=1, source_target_pairs={{0,64},{8,72},{16,80},{24,88},{32,96},{40,104},{48,112},{56,120},{... | collective-permute-start | bytes 1179656 | tf_op jit(solution)/shard_map/ppermute | solution.py:701

commit v4 on v3

--- a/solution.py
+++ b/solution.py
@@ -25,7 +25,7 @@
 PAIR_ROWS = MOST * 2 * TILE
 SEND_FIRST = PAIR_ROWS + 2 * TROWS
 SEND_REST = PAIR_ROWS + TROWS
-BACK_REST = PAIR_ROWS + 3 * NH * TROWS
+BACK_REST = PAIR_ROWS + 5 * TROWS
 NF = 2
 WF = NF * HD
 WR = W - WF
@@ -213,8 +213,12 @@
     part_ref,
     sems,
     rest_sems,
-    part_sems,
+    part_sem,
 ):
+    def put_part(n, rows):
+        at, lanes = n // 2 * TROWS, slice(n % 2 * HD, (n % 2 + 1) * HD)
+        part_ref[:, at : at + TROWS, lanes] = rows.astype(BF16).reshape(GROUPS, TROWS, HD)
+
     tiles = go(picked(sel_ref, x_ref, o_ref, sems, pl.ds(0, WF)))
     tiles += go(picked(sel_ref, x_ref, rest_ref, rest_sems, pl.ds(WF, WR)))
     live = lax.broadcasted_iota(jnp.int32, (TXT, TXT), 1) < n_ref[0]
@@ -238,21 +242,13 @@
             total = p if total is None else total + p
             out = part if out is None else out + part
         total = jnp.sum(total, axis=1, keepdims=True)
-        part_ref[j] = out.astype(BF16)
+        put_part(j, out)
         stats = put(lane, stats, j, top)
         for n, third in enumerate(thirds(total)):
             stats = put(lane, stats, 8 * (n + 1) + j, third)
-    part_ref[NH] = stats.astype(BF16)
+    put_part(NH, stats)
     parts = go(
-        [
-            pltpu.make_async_copy(
-                part_ref.at[n, pl.ds(g * TROWS, TROWS)],
-                o_ref.at[g, pl.ds(PAIR_ROWS + n // 2 * TROWS, TROWS), pl.ds(n % 2 * HD, HD)],
-                part_sems.at[g, n],
-            )
-            for g in range(GROUPS)
-            for n in range(NH + 1)
-        ]
+        [pltpu.make_async_copy(part_ref, o_ref.at[:, pl.ds(PAIR_ROWS, 2 * TROWS)], part_sem)]
     )
     finish(tiles + parts)
 
@@ -269,10 +265,10 @@
         ],
         scratch_shapes=[
             pltpu.VMEM((TCHUNKS, TXT, 256), F32),
-            pltpu.VMEM((NH + 1, TXT, HD), BF16),
+            pltpu.VMEM((GROUPS, 2 * TROWS, WF), BF16),
             pltpu.SemaphoreType.DMA((GROUPS, 2 * MOST)),
             pltpu.SemaphoreType.DMA((GROUPS, 2 * MOST)),
-            pltpu.SemaphoreType.DMA((GROUPS, NH + 1)),
+            pltpu.SemaphoreType.DMA,
         ],
         compiler_params=params(),
         cost_estimate=cost(4 * NH * TXT * TCHUNKS * 256 * HD, 5 << 20, NH * TXT * 1280),
@@ -280,11 +276,18 @@
     )(sel, n, tq, tk, tv, x)
 
 
-def text_stats_kernel(own_ref, got_ref, tg_ref, in_ref, o_ref, out_ref, parts, stats_ref, sem, sems):
-    load = go([pltpu.make_async_copy(got_ref.at[:, pl.ds(PAIR_ROWS, 2 * TROWS)], parts, sem)])
+def text_stats_kernel(own_ref, got_ref, tg_ref, in_ref, o_ref, out_ref, parts, tg, stats_ref, sems):
+    mine = pl.ds(pl.multiple_of(own_ref[0] * TROWS, TROWS), TROWS)
+    load = go(
+        [
+            pltpu.make_async_copy(
+                got_ref.at[:, pl.ds(PAIR_ROWS, 2 * TROWS)], parts, sems.at[0]
+            ),
+            pltpu.make_async_copy(tg_ref.at[mine], tg, sems.at[1]),
+        ]
+    )
     lane_all = lax.broadcasted_iota(jnp.int32, (TXT, HD), 1)
     lane = lax.broadcasted_iota(jnp.int32, (TROWS, HD), 1)
-    mine = pl.ds(pl.multiple_of(own_ref[0] * TROWS, TROWS), TROWS)
     finish(load)
     received = parts[:, TROWS:, HD:].astype(F32).reshape(TXT, HD)
     stats = jnp.zeros((TROWS, HD), F32)
@@ -298,19 +301,12 @@
         part = parts[:, j // 2 * TROWS : (j // 2 + 1) * TROWS, j % 2 * HD : (j % 2 + 1) * HD]
         out = jnp.sum(scale * part.astype(F32), axis=0) / total
         out_ref[:, lanes] = out.astype(BF16)
-        offset = jnp.sum(tg_ref[mine, lanes].astype(F32) * out, axis=1, keepdims=True)
+        offset = jnp.sum(tg[:, lanes].astype(F32) * out, axis=1, keepdims=True)
         for n, third in enumerate(thirds(top + jnp.log2(total)) + thirds(offset)):
             stats = put(lane, stats, 8 * n + j, third)
-    stats_ref[...] = stats.astype(BF16)
+    stats_ref[...] = jnp.broadcast_to(stats.astype(BF16)[None], (GROUPS, TROWS, HD))
     finish(
-        go(
-            [
-                pltpu.make_async_copy(
-                    stats_ref, o_ref.at[g, pl.ds(PAIR_ROWS, TROWS)], sems.at[g]
-                )
-                for g in range(GROUPS)
-            ]
-        )
+        go([pltpu.make_async_copy(stats_ref, o_ref.at[:, pl.ds(PAIR_ROWS, TROWS)], sems.at[2])])
     )
 
 
@@ -318,10 +314,7 @@
     return pl.pallas_call(
         text_stats_kernel,
         grid=(1,),
-        in_specs=[pl.BlockSpec(memory_space=SMEM)]
-        + any_specs(1)
-        + [whole(TEXT)]
-        + any_specs(1),
+        in_specs=[pl.BlockSpec(memory_space=SMEM)] + any_specs(3),
         out_specs=[pl.BlockSpec(memory_space=ANY), whole((TROWS, W))],
         out_shape=[
             jax.ShapeDtypeStruct(send.shape, BF16),
@@ -329,9 +322,9 @@
         ],
         scratch_shapes=[
             pltpu.VMEM((GROUPS, 2 * TROWS, WF), BF16),
-            pltpu.VMEM((TROWS, WR), BF16),
-            pltpu.SemaphoreType.DMA,
-            pltpu.SemaphoreType.DMA((GROUPS,)),
+            pltpu.VMEM((TROWS, W), BF16),
+            pltpu.VMEM((GROUPS, TROWS, WR), BF16),
+            pltpu.SemaphoreType.DMA((3,)),
         ],
         input_output_aliases={3: 0},
         compiler_params=params(),
@@ -341,7 +334,7 @@
 
 
 def text_backward_kernel(
-    n_ref, got_ref, tq_ref, tk_ref, tv_ref, tg_ref, x_ref, tqg_ref, acc_ref, dx_ref, rows, sem
+    n_ref, got_ref, tq_ref, tk_ref, tv_ref, tg_ref, x_ref, own_ref, tqg_ref, acc_ref, dx_ref, rows, sem
 ):
     load = go(
         [
@@ -384,16 +377,18 @@
         return carry
 
     lax.fori_loop(0, NH, head, 0)
-
-
-def text_backward(n, got, tq, tk, tv, tg, x):
+    for t in range(TILES):
+        dx_ref[t, :, :, :WF] += own_ref[t]
+
+
+def text_backward(n, got, tq, tk, tv, tg, x, own):
     return pl.pallas_call(
         text_backward_kernel,
         grid=(1,),
         in_specs=[pl.BlockSpec(memory_space=SMEM)]
         + any_specs(1)
         + [whole(TEXT)] * 4
-        + [whole(LOCAL_KV)],
+        + [whole(LOCAL_KV), whole((TILES, 2, TILE, WF))],
         out_specs=[whole(TEXT), whole((2, TXT, W)), whole(LOCAL_KV)],
         out_shape=[
             jax.ShapeDtypeStruct(TEXT, F32),
@@ -407,7 +402,7 @@
         compiler_params=params(),
         cost_estimate=cost(10 * NH * TXT * TCHUNKS * 256 * HD, 8 << 20, NH * TXT * 1280),
         name="text_backward",
-    )(n, got, tq, tk, tv, tg, x)
+    )(n, got, tq, tk, tv, tg, x, own)
 
 
 CHUNKS = KT // 2 + 1
@@ -417,13 +412,14 @@
     first, slot_ref, count_ref, n_ref, x_ref, got_ref, tk_ref, tv_ref, *refs
 ):
     if first:
-        out_ref, back_ref, own_ref, text_ref = refs[:4]
-        refs = refs[4:]
+        packed_ref, back_ref, own_ref, both_ref, text_ref = refs[:5]
+        refs = refs[5:]
     else:
-        tqg_ref, tacc_ref, text0_ref, out_ref, back_ref, own_ref = refs[:6]
-        refs = refs[6:]
-    keys, values, s_ref, p_ref, dk_acc, dv_acc, tk_acc, tv_acc, pool, qg, stage = refs[:11]
-    kv_sems, got_sems, qg_sem, back_sems, own_sems = refs[11:]
+        tqg_ref, tacc_ref, text0_ref, dx_ref = refs[:4]
+        packed_ref, both_ref, own_ref = refs[6:9]
+        refs = refs[9:]
+    keys, values, s_ref, p_ref, dk_acc, dv_acc, tk_acc, tv_acc, pool, qg, out_ref, stage = refs[:12]
+    text_stage, kv_sems, got_sems, qg_sem, back_sems, own_sems, dx_sems, out_sems = refs[12:]
     base, heads = (0, NF) if first else (NF, NH - NF)
     mine = slice(base * HD, (base + heads) * HD)
     lanes = pl.ds(base * HD, heads * HD)
@@ -447,6 +443,13 @@
         )
         for g in range(GROUPS)
     ]
+    if not first:
+        loads += [
+            pltpu.make_async_copy(
+                dx_ref.at[:, n, :, lanes], acc.at[pl.ds(0, TILES)], dx_sems.at[n]
+            )
+            for n, acc in enumerate((dk_acc, dv_acc))
+        ]
     go(loads)
     keys[0] = tk_ref[:, mine]
     values[0] = tv_ref[:, mine]
@@ -456,7 +459,7 @@
         dv_acc[slot] = jnp.zeros((TILE, heads * HD), F32)
         return carry
 
-    lax.fori_loop(0, POOL, clear, 0)
+    lax.fori_loop(0 if first else TILES, POOL, clear, 0)
     if first:
         tk_acc[...] = jnp.zeros((TXT, heads * HD), F32)
         tv_acc[...] = jnp.zeros((TXT, heads * HD), F32)
@@ -548,6 +551,11 @@
             pltpu.make_async_copy(acc.at[pl.ds(0, TILES)], own_ref.at[:, n], own_sems.at[n])
             for n, acc in enumerate((dk_acc, dv_acc))
         ]
+        + [
+            pltpu.make_async_copy(
+                out_ref, packed_ref.at[:, pl.ds(0, 2), :, lanes], out_sems.at[0]
+            )
+        ]
     )
     if first:
         text_ref[0] = tk_acc[...]
@@ -555,8 +563,9 @@
     else:
 
         def store(n, values):
-            at = PAIR_ROWS + n * TROWS
-            stage[:, at : at + TROWS] = values.reshape(GROUPS, TROWS, HD).astype(BF16)
+            at, cut = n // 2 * TROWS, slice(n % 2 * HD, (n % 2 + 1) * HD)
+            values = values.reshape(GROUPS, TROWS, HD).astype(BF16)
+            text_stage[:, at : at + TROWS, cut] = values
 
         for h in range(NH):
             cut = slice(h * HD, (h + 1) * HD)
@@ -568,32 +577,53 @@
             store(h, tqg_ref[:, cut])
             store(NH + h, key_grad * FACTOR)
             store(2 * NH + h, value_grad)
+        store(3 * NH, jnp.zeros((TXT, HD), F32))
+        stores += go(
+            [
+                pltpu.make_async_copy(
+                    text_stage, both_ref.at[:, pl.ds(PAIR_ROWS, 5 * TROWS)], out_sems.at[1]
+                )
+            ]
+        )
+    pair_rows = pl.ds(0, PAIR_ROWS)
     for g in range(GROUPS):
         for m in range(MOST):
             slot = TILES + g * MOST + m
             stage[g, 2 * m * TILE : (2 * m + 1) * TILE] = (dk_acc[slot] * FACTOR).astype(BF16)
             stage[g, (2 * m + 1) * TILE : (2 * m + 2) * TILE] = dv_acc[slot].astype(BF16)
-        stores += go([pltpu.make_async_copy(stage.at[g], back_ref.at[g], back_sems.at[g])])
+        if first:
+            targets = (back_ref.at[g], both_ref.at[g, pair_rows, pl.ds(0, HD)])
+        else:
+            targets = (both_ref.at[g, pair_rows, pl.ds(HD, HD)],)
+        stores += go(
+            [
+                pltpu.make_async_copy(
+                    stage.at[g, :, pl.ds(n * HD, HD)], target, back_sems.at[g, n]
+                )
+                for n, target in enumerate(targets)
+            ]
+        )
     finish(stores)
 
 
 def video(first, slot, count, n, x, got, tk, tv, *text):
     heads = NF if first else NH - NF
-    rows = PAIR_ROWS if first else BACK_REST
     width = heads * HD
     pair = (TILES, 2, TILE, width)
     in_specs = [pl.BlockSpec(memory_space=SMEM)] * 3 + any_specs(2) + [whole(TEXT)] * 2
-    out_specs = [whole(pair)] + any_specs(2)
-    out_shape = [
-        jax.ShapeDtypeStruct(pair, BF16),
-        jax.ShapeDtypeStruct((GROUPS, rows, width), BF16),
-        jax.ShapeDtypeStruct(pair, F32),
-    ]
+    packed = jax.ShapeDtypeStruct((TILES, 4, TILE, W), BF16)
+    both = jax.ShapeDtypeStruct((GROUPS, BACK_REST, 2 * HD), BF16)
+    own = jax.ShapeDtypeStruct(pair, F32)
     if first:
-        out_specs.append(whole((2, TXT, WF)))
-        out_shape.append(jax.ShapeDtypeStruct((2, TXT, WF), F32))
+        out_specs = any_specs(4) + [whole((2, TXT, WF))]
+        back = jax.ShapeDtypeStruct((GROUPS, PAIR_ROWS, HD), BF16)
+        out_shape = [packed, back, own, both, jax.ShapeDtypeStruct((2, TXT, WF), F32)]
+        aliases = {}
     else:
-        in_specs += [whole(TEXT), whole((2, TXT, W)), whole((2, TXT, WF))]
+        in_specs += [whole(TEXT), whole((2, TXT, W)), whole((2, TXT, WF))] + any_specs(3)
+        out_specs = any_specs(3)
+        out_shape = [packed, both, own]
+        aliases = {11: 0, 12: 1}
     return pl.pallas_call(
         functools.partial(video_kernel, first),
         grid=(1,),
@@ -611,13 +641,18 @@
             pltpu.VMEM((TXT, width), F32),
             pltpu.VMEM((POOL * 2 * TILE, width), BF16),
             pltpu.VMEM(pair, BF16),
-            pltpu.VMEM((GROUPS, rows, width), BF16),
+            pltpu.VMEM(pair, BF16),
+            pltpu.VMEM((GROUPS, PAIR_ROWS, width), BF16),
+            pltpu.VMEM((GROUPS, 5 * TROWS, 2 * HD), BF16),
             pltpu.SemaphoreType.DMA((TILES, 2)),
             pltpu.SemaphoreType.DMA((GROUPS,)),
             pltpu.SemaphoreType.DMA,
-            pltpu.SemaphoreType.DMA((GROUPS,)),
+            pltpu.SemaphoreType.DMA((GROUPS, 2)),
             pltpu.SemaphoreType.DMA((2,)),
-        ],
+            pltpu.SemaphoreType.DMA((2,)),
+            pltpu.SemaphoreType.DMA((2,)),
+        ],
+        input_output_aliases=aliases,
         compiler_params=params(),
         cost_estimate=cost(
             12 * heads * TLOCAL * 1280 * HD, heads * (8 << 20), heads * TLOCAL * 1280
@@ -626,55 +661,78 @@
     )(slot, count, n, x, got, tk, tv, *text)
 
 
-def combine_kernel(sel_ref, back_ref, own_ref, dx_ref, half_ref, *refs):
-    out_ref, acc = refs[-2:]
-    acc[:, 0] = (own_ref[:, 0] + dx_ref[:, 0]) * FACTOR
-    acc[:, 1] = own_ref[:, 1] + dx_ref[:, 1]
+def combine_kernel(
+    sel_ref, first_ref, both_ref, dx_ref, own_ref, in_ref, packed_ref, acc, back, out, own_sems, sems, out_sem
+):
+    loads = go(
+        [
+            pltpu.make_async_copy(
+                dx_ref.at[:, :, :, pl.ds(0, WF)], acc.at[:, :, :, pl.ds(0, WF)], own_sems.at[0]
+            ),
+            pltpu.make_async_copy(own_ref, acc.at[:, :, :, pl.ds(WF, WR)], own_sems.at[1]),
+        ]
+    )
+
+    def parts(g):
+        rows = pl.ds(0, PAIR_ROWS)
+        return [
+            pltpu.make_async_copy(first_ref.at[g], back.at[g, :, pl.ds(0, HD)], sems.at[g, 0]),
+            pltpu.make_async_copy(
+                both_ref.at[g, rows], back.at[g, :, pl.ds(HD, 2 * HD)], sems.at[g, 1]
+            ),
+        ]
+
+    for g in range(GROUPS):
+        go(parts(g))
+    finish(loads)
+    for t in range(TILES):
+        acc[t, 0] = acc[t, 0] * FACTOR
 
     def add(g, carry):
+        finish(parts(g))
         for m in range(MOST):
             at = sel_ref[g * MOST + m]
-            part = back_ref[g, 2 * m * TILE : 2 * (m + 1) * TILE].astype(F32)
-            acc[at] += part.reshape(2, TILE, HD)
+            part = back[g, 2 * m * TILE : 2 * (m + 1) * TILE].astype(F32)
+            acc[at] += part.reshape(2, TILE, W)
         return carry
 
     lax.fori_loop(0, GROUPS, add, 0)
-    out_ref[:, :2] = half_ref[...]
-    out_ref[:, 2:] = acc[...].astype(BF16)
-
-
-def combine(first, sel, back, own, dx, half, *packed):
-    base, heads = (0, NF) if first else (NF, NH - NF)
-    pair = (TILES, 2, TILE, HD)
+    for t in range(TILES):
+        out[t] = acc[t].astype(BF16)
+    finish(go([pltpu.make_async_copy(out, packed_ref.at[:, pl.ds(2, 2)], out_sem)]))
+
+
+def combine(sel, first, both, dx, own, packed):
     return pl.pallas_call(
         combine_kernel,
-        grid=(heads,),
-        in_specs=[
-            pl.BlockSpec(memory_space=SMEM),
-            pl.BlockSpec((GROUPS, PAIR_ROWS, HD), lambda j: (0, 0, j)),
-            pl.BlockSpec(pair, lambda j: (0, 0, 0, j)),
-            pl.BlockSpec(pair, lambda j: (0, 0, 0, base + j)),
-            pl.BlockSpec(pair, lambda j: (0, 0, 0, j)),
-        ]
-        + any_specs(len(packed)),
-        out_specs=pl.BlockSpec((TILES, 4, TILE, HD), lambda j: (0, 0, 0, base + j)),
+        grid=(1,),
+        in_specs=[pl.BlockSpec(memory_space=SMEM)] + any_specs(5),
+        out_specs=pl.BlockSpec(memory_space=ANY),
         out_shape=jax.ShapeDtypeStruct((TILES, 4, TILE, W), BF16),
-        scratch_shapes=[pltpu.VMEM(pair, F32)],
-        input_output_aliases={5: 0} if packed else {},
+        scratch_shapes=[
+            pltpu.VMEM(LOCAL_KV, F32),
+            pltpu.VMEM((GROUPS, PAIR_ROWS, W), BF16),
+            pltpu.VMEM(LOCAL_KV, BF16),
+            pltpu.SemaphoreType.DMA((2,)),
+            pltpu.SemaphoreType.DMA((GROUPS, 2)),
+            pltpu.SemaphoreType.DMA,
+        ],
+        input_output_aliases={5: 0},
         compiler_params=params(),
-        cost_estimate=cost(heads * TLOCAL * HD * 64, heads * (5 << 20)),
-        name="combine_first" if first else "combine_rest",
-    )(sel, back, own, dx, half, *packed)
+        cost_estimate=cost(TLOCAL * W * 64, 14 << 20),
+        name="combine",
+    )(sel, first, both, dx, own, packed)
 
 
 def text_sum_kernel(back_ref, out_ref, o_ref, rows, sem):
-    load = [pltpu.make_async_copy(back_ref.at[:, pl.ds(PAIR_ROWS, 3 * NH * TROWS)], rows, sem)]
+    load = [pltpu.make_async_copy(back_ref.at[:, pl.ds(PAIR_ROWS, 5 * TROWS)], rows, sem)]
     finish(go(load))
     total = jnp.sum(rows[...].astype(F32), axis=0).astype(BF16)
     o_ref[0] = out_ref[...]
     for n in range(3 * NH):
         h = n % NH
-        o_ref[n // NH + 1, :, h * HD : (h + 1) * HD] = total[n * TROWS : (n + 1) * TROWS]
+        at, cut = n // 2 * TROWS, slice(n % 2 * HD, (n % 2 + 1) * HD)
+        o_ref[n // NH + 1, :, h * HD : (h + 1) * HD] = total[at : at + TROWS, cut]
 
 
 def text_sum(back, out):
@@ -685,7 +743,7 @@
         out_specs=whole((4, TROWS, W)),
         out_shape=jax.ShapeDtypeStruct((4, TROWS, W), BF16),
         scratch_shapes=[
-            pltpu.VMEM((GROUPS, 3 * NH * TROWS, WR), BF16),
+            pltpu.VMEM((GROUPS, 5 * TROWS, 2 * HD), BF16),
             pltpu.SemaphoreType.DMA,
         ],
         compiler_params=params(),
@@ -755,17 +813,29 @@
     got0 = lax.all_to_all(send0, "seq", 0, 0, tiled=True)
     send1, text_out = text_stats(own.reshape(1), got0, text_grad, send1)
     got = lax.all_to_all(send1, "seq", 0, 0, tiled=True)
-    half0, back0, own0, text0 = video(
+    packed, back0, own0, both, text0 = video(
         True, slot, count, n, x, got0, text_key, text_value
     )
     back0 = lax.all_to_all(back0, "seq", 0, 0, tiled=True)
-    tqg, tacc, dx = text_backward(n_own, got, *text, text_grad, x)
-    half, back, own_grads = video(
-        False, slot, count, n, x, got, text_key, text_value, tqg, tacc, text0
-    )
-    back = lax.all_to_all(back, "seq", 0, 0, tiled=True)
-    packed = combine(True, sel, back0, own0, dx, half0)
-    packed = combine(False, sel, back, own_grads, dx, half, packed)
+    tqg, tacc, dx = text_backward(n_own, got, *text, text_grad, x, own0)
+    packed, both, own_grads = video(
+        False,
+        slot,
+        count,
+        n,
+        x,
+        got,
+        text_key,
+        text_value,
+        tqg,
+        tacc,
+        text0,
+        dx,
+        packed,
+        both,
+    )
+    back = lax.all_to_all(both, "seq", 0, 0, tiled=True)
+    packed = combine(sel, back0, back, dx, own_grads, packed)
 
     gathered = text_sum(back, text_out)[None]
     for bit, mask in STEPS:

time: 322 us -> 312 us (0.969); the launches traced: 317 us -> 311 us
  blocking collectives: 58.6 us -> 122 us
  waiting for transfers between devices: 119 us -> 71.1 us
  starting transfers between devices: 49.6 us -> 29.9 us
    all_to_all x0 -> x1, blocking collectives: none -> 63.4 us  [body(): back = lax.all_to_all(both, 'seq', 0, 0, tiled=True)]
    all_to_all x1 -> x0, waiting for transfers between devices: 28.1 us -> none  [body(): back = lax.all_to_all(back, 'seq', 0, 0, tiled=True)]
    all_to_all x1, waiting for transfers between devices: 25.9 us -> 0.01 us  [body(): back0 = lax.all_to_all(back0, 'seq', 0, 0, tiled=True)]
    all_to_all x1 -> x0, starting transfers between devices: 13.1 us -> none  [body(): back = lax.all_to_all(back, 'seq', 0, 0, tiled=True)]
    ppermute x4, waiting for transfers between devices: 30.5 us -> 37.2 us  [swapped(): return lax.ppermute(x, 'seq', [(i, i ^ mask) for i in range(GROUPS)])]
    ppermute x4, starting transfers between devices: 9.8 us -> 3.25 us  [swapped(): return lax.ppermute(x, 'seq', [(i, i ^ mask) for i in range(GROUPS)])]
    pallas_call x2 -> x1, Pallas kernels: 9.44 us -> 7.88 us  [combine(): pl.pallas_call(combine_kernel, grid=(1,), in_specs=[pl.BlockSpec(memory_s...]
  transfers between devices with their start and end apart: 9 -> 8, of which waited for: 8 -> 6; matrix products, arithmetic and copies ran while one was open for 2% -> 2% of each run, Pallas kernels for 19% -> 19%
where the time goes in v4:
time: 312 us; the launch traced here: 311 us
  blocking collectives  122 us (39%)
  Pallas kernels  80.4 us (26%)
  waiting for transfers between devices  71.1 us (23%)
  starting transfers between devices  29.9 us (10%)
    all_to_all x1, blocking collectives, body(): back = lax.all_to_all(both, 'seq', 0, 0, tiled=True)  63.4 us
    all_to_all x1, blocking collectives, body(): got0 = lax.all_to_all(send0, 'seq', 0, 0, tiled=True)  58.6 us
    pallas_call x2, Pallas kernels, video(): pl.pallas_call(functools.partial(video_kernel, first), grid=(1,), in_spec...  44.3 us
    ppermute x4, waiting for transfers between devices, swapped(): return lax.ppermute(x, 'seq', [(i, i ^ mask) for i in range(GROUPS)])  37.2 us
    all_to_all x1, waiting for transfers between devices, body(): lax.all_to_all(pack(video_key, video_value, video_query, video_grad), 'he...  32.2 us
    pallas_call x1, Pallas kernels, text_backward(): pl.pallas_call(text_backward_kernel, grid=(1,), in_specs=[pl.BlockSpec(me...  10.8 us
    pallas_call x1, Pallas kernels, combine(): pl.pallas_call(combine_kernel, grid=(1,), in_specs=[pl.BlockSpec(memory_s...  7.88 us
    all_to_all x1, starting transfers between devices, body(): back0 = lax.all_to_all(back0, 'seq', 0, 0, tiled=True)  7.83 us
  transfers between devices with their start and end apart: 8, of which 6 were waited for; matrix products, arithmetic and copies ran while one was open for 2% of the time, Pallas kernels for 19%

profile of v4, /device:TPU:6, one launch (start us, length us, event | category | flops | bytes accessed | tf_op | source)
XLA Modules:
  0.0 311.1 jit_solution(7967857951295804376)
XLA Ops:
  0.6 3.1 pack.1
  3.8 0.0 copy-start
  3.8 7.6 %all-to-all-start = ((bf16[8,4,128,384]{3,2,1,0:T(8,128)(2,1)}), bf16[8,4,128,384]{3,2,1,0:T(8,128)(2,1)}, u32[]{:S(2)}, u32[]{:S(2)}) async-start(bf16[8,4,128,384]{3,2,1,0:T(8,128)(2,1)} %pack.1), calls=%async_computation | async-start | bytes 6291456 | tf_op jit(solution)/shard_map/all_to_all | solution.py:803
  11.4 0.1 copy.33
  11.5 0.6 dynamic_slice.7.count_ref
  12.1 0.1 constant_dynamic-slice_fusion
  12.1 0.1 copy.36
  12.2 0.1 eq.76
  12.3 0.1 fusion.1
  12.4 0.1 reshape.115
  12.5 0.1 copy.37
  12.6 0.1 eq.69
  12.7 0.4 compare_reduce_fusion
  13.1 0.1 copy.34
  13.2 0.1 select_reduce_fusion.1
  13.3 0.1 copy.35
  13.4 0.6 reshape.112.sel_ref
  14.0 0.1 copy.38
  14.1 0.1 select_n.80
  14.2 0.6 fusion.4
  15.3 0.7 select_reduce_fusion.slot_ref
  16.0 32.2 %all-to-all-done.x_ref = bf16[8,4,128,384]{3,2,1,0:T(8,128)(2,1)} async-done(((bf16[8,4,128,384]{3,2,1,0:T(8,128)(2,1)}), bf16[8,4,128,384]{3,2,1,0:T(8,128)(2,1)}, u32[]{:S(2)}, u32[]{:S(2)}) %all-to-all-start) | async-done | bytes 3145760 | tf_op jit(solution)/shard_map/all_to_all | solution.py:803
  48.2 5.9 %send.1 = (bf16[16,544,256]{2,1,0:T(8,128)(2,1)}, bf16[16,528,128]{2,1,0:T(8,128)(2,1)}) custom-call(s32[32]{0:T(128)} %reshape.112.sel_ref, s32[1]{0:T(128)S(6)} %select_n.83.n_ref, bf16[256,384]{1,0:T(8,128)(2,1)} %tq_ref.3, bf16[256,384]{1,0:T(8,128)(2,1)} %tk_ref.7, bf16[256,384]{1,0:T(8,128)(2,1)} %tv_ref.7, bf16[8,4,128,384]{3,2,1,0:T(8,128)(2,1)} %all-to-all-done.x_ref), custom_call_target="tpu_custom_call" | custom-call | flops 503316480 | bytes 5242880 | tf_op jit(solution)/shard_map/send/pallas_call | solution.py:257
  54.1 58.6 %all_to_all.30.got_ref = bf16[16,544,256]{2,1,0:T(8,128)(2,1)} all-to-all(bf16[16,544,256]{2,1,0:T(8,128)(2,1)} %get-tuple-element.37), channel_id=1, replica_groups=mesh['seq'=16,'head'=8] {'seq'}, dimensions={0} | all-to-all | bytes 8912896 | tf_op jit(solution)/shard_map/all_to_all | solution.py:813
  112.7 2.6 text_stats.1
  115.3 5.6 %all-to-all-start.3 = ((bf16[16,528,128]{2,1,0:T(8,128)(2,1)}), bf16[16,528,128]{2,1,0:T(8,128)(2,1)}, u32[]{:S(2)}, u32[]{:S(2)}) async-start(bf16[16,528,128]{2,1,0:T(8,128)(2,1)} %get-tuple-element.40), calls=%async_computation.3 | async-start | bytes 4325376 | tf_op jit(solution)/shard_map/all_to_all | solution.py:815
  120.9 25.9 %video_first.1 = (bf16[8,4,128,384]{3,2,1,0:T(8,128)(2,1)}, bf16[16,512,128]{2,1,0:T(8,128)(2,1)}, f32[8,2,128,256]{3,2,1,0:T(8,128)}, bf16[16,592,256]{2,1,0:T(8,128)(2,1)}, f32[2,256,256]{2,1,0:T(8,128)}) custom-call(s32[64]{0:T(128)} %select_reduce_fusion.slot_ref, s32[8]{0:T(128)} %dynamic_slice.7.count_ref, s32[1]{0:T(128)} %bitcast.n_ref, ...), custom_call_target="tpu_custom_call" | custom-call | flops 4026531840 | bytes 16777216 | tf_op jit(solution)/shard_map/video_first/pallas_call | solution.py:627
  146.8 1.8 all-to-all-done.3.got_ref
  148.6 7.8 %all-to-all-start.2 = ((bf16[16,512,128]{2,1,0:T(8,128)(2,1)}), bf16[16,512,128]{2,1,0:T(8,128)(2,1)}, u32[]{:S(2)}, u32[]{:S(2)}) async-start(bf16[16,512,128]{2,1,0:T(8,128)(2,1)} %get-tuple-element.38), calls=%async_computation.2 | async-start | bytes 4194304 | tf_op jit(solution)/shard_map/all_to_all | solution.py:819
  156.5 10.8 %text_backward.1 = (f32[256,384]{1,0:T(8,128)}, f32[2,256,384]{2,1,0:T(8,128)}, f32[8,2,128,384]{3,2,1,0:T(8,128)}) custom-call(s32[1]{0:T(128)S(6)} %select_n.83.n_ref, bf16[16,528,128]{2,1,0:T(8,128)(2,1)} %all-to-all-done.3.got_ref, bf16[256,384]{1,0:T(8,128)(2,1)} %tq_ref.3, bf16[256,384]{1,0:T(8,128)(2,1)} %tk_ref.7, bf16[256,384]{1,0:T(8,128)(2,1)} %tv_ref.7, ...), custom_call_target="tpu_custom_call" | custom-call | flops 1258291200 | bytes 8388608 | tf_op jit(solution)/shard_map/text_backward/pallas_call | solution.py:385
  167.3 18.4 %video_rest.1 = (bf16[8,4,128,384]{3,2,1,0:T(8,128)(2,1)}, bf16[16,592,256]{2,1,0:T(8,128)(2,1)}, f32[8,2,128,128]{3,2,1,0:T(8,128)}) custom-call(s32[64]{0:T(128)} %select_reduce_fusion.slot_ref, s32[8]{0:T(128)} %dynamic_slice.7.count_ref, s32[1]{0:T(128)} %bitcast.n_ref, ...), custom_call_target="tpu_custom_call", output_to_operand_aliasing={{0}: (11, {}), {1}: (12, {})} | custom-call | flops 2013265920 | bytes 8388608 | tf_op jit(solution)/shard_map/video_rest/pallas_call | solution.py:627
  185.7 63.4 %all_to_all.31.both_ref.back_ref = bf16[16,592,256]{2,1,0:T(8,128)(2,1)} all-to-all(bf16[16,592,256]{2,1,0:T(8,128)(2,1)} %get-tuple-element.48), channel_id=1, replica_groups=mesh['seq'=16,'head'=8] {'seq'}, dimensions={0} | all-to-all | bytes 9699328 | tf_op jit(solution)/shard_map/all_to_all | solution.py:837
  249.2 7.9 %combine.1 = bf16[8,4,128,384]{3,2,1,0:T(8,128)(2,1)} custom-call(s32[32]{0:T(128)} %reshape.112.sel_ref, bf16[16,512,128]{2,1,0:T(8,128)(2,1)} %all-to-all-done.2.first_ref, bf16[16,592,256]{2,1,0:T(8,128)(2,1)} %all_to_all.31.both_ref.back_ref, f32[8,2,128,384]{3,2,1,0:T(8,128)} %get-tuple-element.45.refs_3_.dx_ref, ...), custom_call_target="tpu_custom_call", output_to_operand_aliasing={{}: (5, {})} | custom-call | flops 25165824 | bytes 14680064 | tf_op jit(solution)/shard_map/combine/pallas_call | solution.py:706
  257.1 5.7 %all-to-all-start.5 = ((bf16[8,4,128,384]{3,2,1,0:T(8,128)(2,1)}), bf16[8,4,128,384]{3,2,1,0:T(8,128)(2,1)}, u32[]{:S(2)}, u32[]{:S(2)}) async-start(bf16[8,4,128,384]{3,2,1,0:T(8,128)(2,1)} %combine.1), calls=%async_computation.5 | async-start | bytes 6291456 | tf_op jit(solution)/shard_map/all_to_all | solution.py:849
  262.8 2.5 text_sum.1
  265.3 0.1 collective-permute-start
  265.4 1.4 collective-permute-done
  266.8 0.9 maximum_select_fusion.3
  267.7 0.5 collective-permute-start.1
  268.2 4.5 %collective-permute-done.1 = bf16[2,4,16,384]{3,2,1,0:T(8,128)(2,1)S(1)} collective-permute-done((bf16[2,4,16,384]{3,2,1,0:T(8,128)(2,1)S(1)}, bf16[2,4,16,384]{3,2,1,0:T(8,128)(2,1)S(1)}, u32[]{:S(2)}, u32[]{:S(2)}) %collective-permute-start.1) | collective-permute-done | bytes 98336 | tf_op jit(solution)/shard_map/ppermute | solution.py:759
  272.7 1.1 collective-permute-start.2
  273.8 6.4 %collective-permute-done.2 = bf16[4,4,16,384]{3,2,1,0:T(8,128)(2,1)S(1)} collective-permute-done((bf16[4,4,16,384]{3,2,1,0:T(8,128)(2,1)S(1)}, bf16[4,4,16,384]{3,2,1,0:T(8,128)(2,1)S(1)}, u32[]{:S(2)}, u32[]{:S(2)}) %collective-permute-start.2) | collective-permute-done | bytes 196640 | tf_op jit(solution)/shard_map/ppermute | solution.py:759
  280.2 0.1 maximum_select_fusion.1
  280.3 1.5 collective-permute-start.3
  281.8 24.9 %collective-permute-done.3 = bf16[8,4,16,384]{3,2,1,0:T(8,128)(2,1)S(1)} collective-permute-done((bf16[8,4,16,384]{3,2,1,0:T(8,128)(2,1)S(1)}, bf16[8,4,16,384]{3,2,1,0:T(8,128)(2,1)S(1)}, u32[]{:S(2)}, u32[]{:S(2)}) %collective-permute-start.3) | collective-permute-done | bytes 393248 | tf_op jit(solution)/shard_map/ppermute | solution.py:759
  306.7 0.1 fusion
  306.9 0.9 fusion.5
  307.8 3.2 %unpack.1 = (bf16[128,3072]{1,0:T(8,128)(2,1)}, bf16[128,3072]{1,0:T(8,128)(2,1)}, bf16[128,3072]{1,0:T(8,128)(2,1)}, bf16[128,3072]{1,0:T(8,128)(2,1)}) custom-call(bf16[8,4,128,384]{3,2,1,0:T(8,128)(2,1)} %all-to-all-done.5.x_ref), custom_call_target="tpu_custom_call" | custom-call | bytes 6291456 | tf_op jit(solution)/shard_map/unpack/pallas_call | solution.py:141
  (17 shorter events, 0.1 us)
Async XLA Ops:
  3.8 7.6 %copy-start = (s32[128,8]{0,1:T(8,128)S(1)}, s32[128,8]{0,1:T(8,128)}, u32[]{:S(2)}) copy-start(s32[128,8]{0,1:T(8,128)} %param.19) | copy-start | bytes 12292
  3.8 7.6 %copy-start.1 = (s32[128]{0:T(128)S(1)}, s32[128]{0:T(128)}, u32[]{:S(2)}) copy-start(s32[128]{0:T(128)} %param.20) | copy-start | bytes 1540
  3.8 10.4 %copy-start.2 = (s32[256]{0:T(256)S(1)}, s32[256]{0:T(256)}, u32[]{:S(2)}) copy-start(s32[256]{0:T(256)} %param.21) | copy-start | bytes 3076
  3.8 44.4 %all-to-all-start = ((bf16[8,4,128,384]{3,2,1,0:T(8,128)(2,1)}), bf16[8,4,128,384]{3,2,1,0:T(8,128)(2,1)}, u32[]{:S(2)}, u32[]{:S(2)}) async-start(bf16[8,4,128,384]{3,2,1,0:T(8,128)(2,1)} %pack.1), calls=%async_computation | async-start | bytes 6291456 | tf_op jit(solution)/shard_map/all_to_all | solution.py:803
  115.3 33.3 %all-to-all-start.3 = ((bf16[16,528,128]{2,1,0:T(8,128)(2,1)}), bf16[16,528,128]{2,1,0:T(8,128)(2,1)}, u32[]{:S(2)}, u32[]{:S(2)}) async-start(bf16[16,528,128]{2,1,0:T(8,128)(2,1)} %get-tuple-element.40), calls=%async_computation.3 | async-start | bytes 4325376 | tf_op jit(solution)/shard_map/all_to_all | solution.py:815
  148.6 37.1 %all-to-all-start.2 = ((bf16[16,512,128]{2,1,0:T(8,128)(2,1)}), bf16[16,512,128]{2,1,0:T(8,128)(2,1)}, u32[]{:S(2)}, u32[]{:S(2)}) async-start(bf16[16,512,128]{2,1,0:T(8,128)(2,1)} %get-tuple-element.38), calls=%async_computation.2 | async-start | bytes 4194304 | tf_op jit(solution)/shard_map/all_to_all | solution.py:819
  257.1 50.7 %all-to-all-start.5 = ((bf16[8,4,128,384]{3,2,1,0:T(8,128)(2,1)}), bf16[8,4,128,384]{3,2,1,0:T(8,128)(2,1)}, u32[]{:S(2)}, u32[]{:S(2)}) async-start(bf16[8,4,128,384]{3,2,1,0:T(8,128)(2,1)} %combine.1), calls=%async_computation.5 | async-start | bytes 6291456 | tf_op jit(solution)/shard_map/all_to_all | solution.py:849
  265.3 1.5 collective-permute-start
  267.7 4.9 %collective-permute-start.1 = (bf16[2,4,16,384]{3,2,1,0:T(8,128)(2,1)S(1)}, bf16[2,4,16,384]{3,2,1,0:T(8,128)(2,1)S(1)}, u32[]{:S(2)}, u32[]{:S(2)}) collective-permute-start(bf16[2,4,16,384]{3,2,1,0:T(8,128)(2,1)S(1)} %maximum_select_fusion.3), channel_id=1, source_target_pairs={{0,16},{8,24},{16,0},{24,8},{32,48},{40,56},{48,32},{56,40},{64,80... | collective-permute-start | bytes 294920 | tf_op jit(solution)/shard_map/ppermute | solution.py:759
  272.7 7.5 %collective-permute-start.2 = (bf16[4,4,16,384]{3,2,1,0:T(8,128)(2,1)S(1)}, bf16[4,4,16,384]{3,2,1,0:T(8,128)(2,1)S(1)}, u32[]{:S(2)}, u32[]{:S(2)}) collective-permute-start(bf16[4,4,16,384]{3,2,1,0:T(8,128)(2,1)S(1)} %maximum_select_fusion.2), channel_id=1, source_target_pairs={{0,48},{8,56},{16,32},{24,40},{32,16},{40,24},{48,0},{56,8},{64,11... | collective-permute-start | bytes 589832 | tf_op jit(solution)/shard_map/ppermute | solution.py:759
  280.3 26.5 %collective-permute-start.3 = (bf16[8,4,16,384]{3,2,1,0:T(8,128)(2,1)S(1)}, bf16[8,4,16,384]{3,2,1,0:T(8,128)(2,1)S(1)}, u32[]{:S(2)}, u32[]{:S(2)}) collective-permute-start(bf16[8,4,16,384]{3,2,1,0:T(8,128)(2,1)S(1)} %maximum_select_fusion.1), channel_id=1, source_target_pairs={{0,64},{8,72},{16,80},{24,88},{32,96},{40,104},{48,112},{56,120},{... | collective-permute-start | bytes 1179656 | tf_op jit(solution)/shard_map/ppermute | solution.py:759

commit v5 on v4

--- a/solution.py
+++ b/solution.py
@@ -752,9 +752,6 @@
     )(back, out)
 
 
-STEPS = ((1, 1), (2, 2), (4, 6), (8, 8))
-
-
 def swapped(x, mask):
     return lax.ppermute(x, "seq", [(i, i ^ mask) for i in range(GROUPS)])
 
@@ -834,16 +831,23 @@
         packed,
         both,
     )
+    both, back0 = lax.optimization_barrier((both, back0))
     back = lax.all_to_all(both, "seq", 0, 0, tiled=True)
-    packed = combine(sel, back0, back, dx, own_grads, packed)
-
-    gathered = text_sum(back, text_out)[None]
-    for bit, mask in STEPS:
-        theirs = swapped(gathered, mask)
+
+    def exchanged(gathered, bit, theirs):
         first = jnp.concatenate([gathered, theirs], axis=0)
         second = jnp.concatenate([theirs, gathered], axis=0)
-        gathered = jnp.where((own & bit) == 0, first, second)
-    text_rows = jnp.transpose(gathered, (1, 0, 2, 3)).reshape(4, TXT, W)
+        return jnp.where((own & bit) == 0, first, second)
+
+    rows = text_sum(back, text_out)[None]
+    theirs = swapped(rows, 8)
+    packed = combine(sel, back0, back, dx, own_grads, packed)
+    packed, theirs = lax.optimization_barrier((packed, theirs))
+    gathered = exchanged(rows, 8, theirs)
+    for bit, mask in ((1, 1), (2, 2), (4, 6)):
+        gathered = exchanged(gathered, bit, swapped(gathered, mask))
+    gathered = gathered.reshape(2, 2, 2, 2, 4, TROWS, W)
+    text_rows = jnp.transpose(gathered, (4, 3, 0, 1, 2, 5, 6)).reshape(4, TXT, W)
 
     attended_video, video_query_grad, video_key_grad, video_value_grad = unpack(
         lax.all_to_all(packed, "head", 0, 0, tiled=True)

time: 312 us -> 308 us (0.987)
  waiting for transfers between devices: 71.1 us -> 63 us
  Pallas kernels: 80.4 us -> 86.2 us
    ppermute x4, waiting for transfers between devices: 37.2 us -> 18.7 us  [swapped(): return lax.ppermute(x, 'seq', [(i, i ^ mask) for i in range(GROUPS)])]
    all_to_all x1, waiting for transfers between devices: 0.01 us -> 12.4 us  [body(): lax.all_to_all(packed, 'head', 0, 0, tiled=True)]
    pallas_call x2, Pallas kernels: 44.3 us -> 50.1 us  [video(): pl.pallas_call(functools.partial(video_kernel, first), grid=(1,), in_spec...]
  transfers between devices with their start and end apart: 8 -> 8, of which waited for: 6 -> 5; matrix products, arithmetic and copies ran while one was open for 2% -> 3% of each run, Pallas kernels for 19% -> 22%
where the time goes in v5:
time: 308 us; the launch traced here: 307 us
  blocking collectives  120 us (39%)
  Pallas kernels  86.2 us (28%)
  waiting for transfers between devices  63 us (20%)
  starting transfers between devices  27.6 us (9%)
  local copies, waits for them, and re-layouts  5.03 us (2%)
  other arithmetic  3.19 us (1%)
    all_to_all x1, blocking collectives, body(): back = lax.all_to_all(both, 'seq', 0, 0, tiled=True)  61.2 us
    all_to_all x1, blocking collectives, body(): got0 = lax.all_to_all(send0, 'seq', 0, 0, tiled=True)  58.6 us
    pallas_call x2, Pallas kernels, video(): pl.pallas_call(functools.partial(video_kernel, first), grid=(1,), in_spec...  50.1 us
    all_to_all x1, waiting for transfers between devices, body(): lax.all_to_all(pack(video_key, video_value, video_query, video_grad), 'he...  31.9 us
    ppermute x4, waiting for transfers between devices, swapped(): return lax.ppermute(x, 'seq', [(i, i ^ mask) for i in range(GROUPS)])  18.7 us
    all_to_all x1, waiting for transfers between devices, body(): lax.all_to_all(packed, 'head', 0, 0, tiled=True)  12.4 us
    pallas_call x1, Pallas kernels, text_backward(): pl.pallas_call(text_backward_kernel, grid=(1,), in_specs=[pl.BlockSpec(me...  10.8 us
    pallas_call x1, Pallas kernels, combine(): pl.pallas_call(combine_kernel, grid=(1,), in_specs=[pl.BlockSpec(memory_s...  7.97 us
  transfers between devices with their start and end apart: 8, of which 5 were waited for; matrix products, arithmetic and copies ran while one was open for 3% of the time, Pallas kernels for 22%

profile of v5, /device:TPU:6, one launch (start us, length us, event | category | flops | bytes accessed | tf_op | source)
XLA Modules:
  0.0 306.5 jit_solution(14962684931087262094)
XLA Ops:
  0.6 3.1 %pack.1 = bf16[8,4,128,384]{3,2,1,0:T(8,128)(2,1)} custom-call(bf16[128,3072]{1,0:T(8,128)(2,1)} %k_ref.1, bf16[128,3072]{1,0:T(8,128)(2,1)} %v_ref.1, bf16[128,3072]{1,0:T(8,128)(2,1)} %q_ref.1, bf16[128,3072]{1,0:T(8,128)(2,1)} %g_ref.1), custom_call_target="tpu_custom_call" | custom-call | bytes 6291456 | tf_op jit(solution)/shard_map/pack/pallas_call | solution.py:104
  3.8 7.6 %all-to-all-start = ((bf16[8,4,128,384]{3,2,1,0:T(8,128)(2,1)}), bf16[8,4,128,384]{3,2,1,0:T(8,128)(2,1)}, u32[]{:S(2)}, u32[]{:S(2)}) async-start(bf16[8,4,128,384]{3,2,1,0:T(8,128)(2,1)} %pack.1), calls=%async_computation | async-start | bytes 6291456 | tf_op jit(solution)/shard_map/all_to_all | solution.py:800
  11.4 0.1 copy.45
  11.5 0.6 dynamic_slice.7.count_ref
  12.2 0.1 copy.48
  12.2 0.1 eq.76
  12.3 0.1 fusion
  12.4 0.1 reshape.120
  12.5 0.1 copy.49
  12.6 0.1 eq.69
  12.7 0.4 compare_reduce_fusion
  13.1 0.1 copy.46
  13.2 0.1 select_reduce_fusion.1
  13.4 0.1 select_n.84
  13.5 0.1 copy.47
  13.6 0.6 reshape.117.sel_ref
  14.2 0.7 fusion.3
  15.6 0.7 select_reduce_fusion.slot_ref
  16.3 31.9 %all-to-all-done.x_ref = bf16[8,4,128,384]{3,2,1,0:T(8,128)(2,1)} async-done(((bf16[8,4,128,384]{3,2,1,0:T(8,128)(2,1)}), bf16[8,4,128,384]{3,2,1,0:T(8,128)(2,1)}, u32[]{:S(2)}, u32[]{:S(2)}) %all-to-all-start) | async-done | bytes 3145760 | tf_op jit(solution)/shard_map/all_to_all | solution.py:800
  48.2 5.9 %send.1 = (bf16[16,544,256]{2,1,0:T(8,128)(2,1)}, bf16[16,528,128]{2,1,0:T(8,128)(2,1)}) custom-call(s32[32]{0:T(128)} %reshape.117.sel_ref, s32[1]{0:T(128)S(6)} %select_n.87.n_ref, bf16[256,384]{1,0:T(8,128)(2,1)} %tq_ref.3, bf16[256,384]{1,0:T(8,128)(2,1)} %tk_ref.7, bf16[256,384]{1,0:T(8,128)(2,1)} %tv_ref.7, bf16[8,4,128,384]{3,2,1,0:T(8,128)(2,1)} %all-to-all-done.x_ref), custom_call_target="tpu_custom_call" | custom-call | flops 503316480 | bytes 5242880 | tf_op jit(solution)/shard_map/send/pallas_call | solution.py:257
  54.1 58.6 %all_to_all.30.got_ref = bf16[16,544,256]{2,1,0:T(8,128)(2,1)} all-to-all(bf16[16,544,256]{2,1,0:T(8,128)(2,1)} %get-tuple-element.41), channel_id=1, replica_groups=mesh['seq'=16,'head'=8] {'seq'}, dimensions={0} | all-to-all | bytes 8912896 | tf_op jit(solution)/shard_map/all_to_all | solution.py:810
  112.7 2.6 text_stats.1
  115.4 5.6 %all-to-all-start.2 = ((bf16[16,528,128]{2,1,0:T(8,128)(2,1)}), bf16[16,528,128]{2,1,0:T(8,128)(2,1)}, u32[]{:S(2)}, u32[]{:S(2)}) async-start(bf16[16,528,128]{2,1,0:T(8,128)(2,1)} %get-tuple-element.43), calls=%async_computation.2 | async-start | bytes 4325376 | tf_op jit(solution)/shard_map/all_to_all | solution.py:812
  120.9 29.6 %video_first.1 = (bf16[8,4,128,384]{3,2,1,0:T(8,128)(2,1)}, bf16[16,512,128]{2,1,0:T(8,128)(2,1)}, f32[8,2,128,256]{3,2,1,0:T(8,128)}, bf16[16,592,256]{2,1,0:T(8,128)(2,1)}, f32[2,256,256]{2,1,0:T(8,128)}) custom-call(s32[64]{0:T(128)} %select_reduce_fusion.slot_ref, s32[8]{0:T(128)} %dynamic_slice.7.count_ref, s32[1]{0:T(128)} %bitcast.n_ref, ...), custom_call_target="tpu_custom_call" | custom-call | flops 4026531840 | bytes 16777216 | tf_op jit(solution)/shard_map/video_first/pallas_call | solution.py:627
  150.6 5.8 %all-to-all-start.3 = ((bf16[16,512,128]{2,1,0:T(8,128)(2,1)}), bf16[16,512,128]{2,1,0:T(8,128)(2,1)}, u32[]{:S(2)}, u32[]{:S(2)}) async-start(bf16[16,512,128]{2,1,0:T(8,128)(2,1)} %get-tuple-element.52), calls=%async_computation.3 | async-start | bytes 4194304 | tf_op jit(solution)/shard_map/all_to_all | solution.py:816
  156.4 10.8 %text_backward.1 = (f32[256,384]{1,0:T(8,128)}, f32[2,256,384]{2,1,0:T(8,128)}, f32[8,2,128,384]{3,2,1,0:T(8,128)}) custom-call(s32[1]{0:T(128)S(6)} %select_n.87.n_ref, bf16[16,528,128]{2,1,0:T(8,128)(2,1)} %all-to-all-done.2.got_ref, bf16[256,384]{1,0:T(8,128)(2,1)} %tq_ref.3, bf16[256,384]{1,0:T(8,128)(2,1)} %tk_ref.7, bf16[256,384]{1,0:T(8,128)(2,1)} %tv_ref.7, ...), custom_call_target="tpu_custom_call" | custom-call | flops 1258291200 | bytes 8388608 | tf_op jit(solution)/shard_map/text_backward/pallas_call | solution.py:385
  167.2 20.5 %video_rest.1 = (bf16[8,4,128,384]{3,2,1,0:T(8,128)(2,1)}, bf16[16,592,256]{2,1,0:T(8,128)(2,1)}, f32[8,2,128,128]{3,2,1,0:T(8,128)}) custom-call(s32[64]{0:T(128)} %select_reduce_fusion.slot_ref, s32[8]{0:T(128)} %dynamic_slice.7.count_ref, s32[1]{0:T(128)} %bitcast.n_ref, ...), custom_call_target="tpu_custom_call", output_to_operand_aliasing={{0}: (11, {}), {1}: (12, {})} | custom-call | flops 2013265920 | bytes 8388608 | tf_op jit(solution)/shard_map/video_rest/pallas_call | solution.py:627
  187.7 61.2 %all_to_all.31.both_ref.back_ref = bf16[16,592,256]{2,1,0:T(8,128)(2,1)} all-to-all(bf16[16,592,256]{2,1,0:T(8,128)(2,1)} %get-tuple-element.54), channel_id=1, replica_groups=mesh['seq'=16,'head'=8] {'seq'}, dimensions={0} | all-to-all | bytes 9699328 | tf_op jit(solution)/shard_map/all_to_all | solution.py:835
  248.8 2.5 text_sum.1
  251.4 1.5 collective-permute-start
  252.9 8.0 %combine.1 = bf16[8,4,128,384]{3,2,1,0:T(8,128)(2,1)} custom-call(s32[32]{0:T(128)} %reshape.117.sel_ref, bf16[16,512,128]{2,1,0:T(8,128)(2,1)} %all-to-all-done.3.first_ref, bf16[16,592,256]{2,1,0:T(8,128)(2,1)} %all_to_all.31.both_ref.back_ref, f32[8,2,128,384]{3,2,1,0:T(8,128)} %get-tuple-element.48.refs_3_.dx_ref, ...), custom_call_target="tpu_custom_call", output_to_operand_aliasing={{}: (5, {})} | custom-call | flops 25165824 | bytes 14680064 | tf_op jit(solution)/shard_map/combine/pallas_call | solution.py:706
  260.9 5.7 %all-to-all-start.5 = ((bf16[8,4,128,384]{3,2,1,0:T(8,128)(2,1)}), bf16[8,4,128,384]{3,2,1,0:T(8,128)(2,1)}, u32[]{:S(2)}, u32[]{:S(2)}) async-start(bf16[8,4,128,384]{3,2,1,0:T(8,128)(2,1)} %combine.1), calls=%async_computation.5 | async-start | bytes 6291456 | tf_op jit(solution)/shard_map/all_to_all | solution.py:853
  266.6 0.9 maximum_select_fusion.3
  267.5 0.1 collective-permute-start.1
  267.6 1.3 collective-permute-done.1
  268.9 0.2 collective-permute-start.2
  269.1 6.8 %collective-permute-done.2 = bf16[4,4,16,384]{3,2,1,0:T(8,128)(2,1)S(1)} collective-permute-done((bf16[4,4,16,384]{3,2,1,0:T(8,128)(2,1)S(1)}, bf16[4,4,16,384]{3,2,1,0:T(8,128)(2,1)S(1)}, u32[]{:S(2)}, u32[]{:S(2)}) %collective-permute-start.2) | collective-permute-done | bytes 196640 | tf_op jit(solution)/shard_map/ppermute | solution.py:756
  276.0 0.1 maximum_select_fusion.1
  276.0 1.1 collective-permute-start.3
  277.2 10.6 %collective-permute-done.3 = bf16[8,4,16,384]{3,2,1,0:T(8,128)(2,1)S(1)} collective-permute-done((bf16[8,4,16,384]{3,2,1,0:T(8,128)(2,1)S(1)}, bf16[8,4,16,384]{3,2,1,0:T(8,128)(2,1)S(1)}, u32[]{:S(2)}, u32[]{:S(2)}) %collective-permute-start.3) | collective-permute-done | bytes 393248 | tf_op jit(solution)/shard_map/ppermute | solution.py:756
  287.8 0.1 maximum_select_fusion
  287.9 0.1 fusion.4
  288.0 0.7 copy.54
  288.7 0.7 copy.51
  289.4 0.7 copy.52
  290.1 0.7 copy.53
  290.8 12.4 %all-to-all-done.5.x_ref = bf16[8,4,128,384]{3,2,1,0:T(8,128)(2,1)} async-done(((bf16[8,4,128,384]{3,2,1,0:T(8,128)(2,1)}), bf16[8,4,128,384]{3,2,1,0:T(8,128)(2,1)}, u32[]{:S(2)}, u32[]{:S(2)}) %all-to-all-start.5) | async-done | bytes 3145760 | tf_op jit(solution)/shard_map/all_to_all | solution.py:853
  303.2 3.2 %unpack.1 = (bf16[128,3072]{1,0:T(8,128)(2,1)}, bf16[128,3072]{1,0:T(8,128)(2,1)}, bf16[128,3072]{1,0:T(8,128)(2,1)}, bf16[128,3072]{1,0:T(8,128)(2,1)}) custom-call(bf16[8,4,128,384]{3,2,1,0:T(8,128)(2,1)} %all-to-all-done.5.x_ref), custom_call_target="tpu_custom_call" | custom-call | bytes 6291456 | tf_op jit(solution)/shard_map/unpack/pallas_call | solution.py:141
  (23 shorter events, 0.3 us)
Async XLA Ops:
  3.8 7.6 %copy-start.1 = (s32[128,8]{0,1:T(8,128)S(1)}, s32[128,8]{0,1:T(8,128)}, u32[]{:S(2)}) copy-start(s32[128,8]{0,1:T(8,128)} %param.19) | copy-start | bytes 12292
  3.8 7.6 %copy-start.2 = (s32[128]{0:T(128)S(1)}, s32[128]{0:T(128)}, u32[]{:S(2)}) copy-start(s32[128]{0:T(128)} %param.20) | copy-start | bytes 1540
  3.8 10.4 %copy-start.3 = (s32[256]{0:T(256)S(1)}, s32[256]{0:T(256)}, u32[]{:S(2)}) copy-start(s32[256]{0:T(256)} %param.21) | copy-start | bytes 3076
  3.8 44.4 %all-to-all-start = ((bf16[8,4,128,384]{3,2,1,0:T(8,128)(2,1)}), bf16[8,4,128,384]{3,2,1,0:T(8,128)(2,1)}, u32[]{:S(2)}, u32[]{:S(2)}) async-start(bf16[8,4,128,384]{3,2,1,0:T(8,128)(2,1)} %pack.1), calls=%async_computation | async-start | bytes 6291456 | tf_op jit(solution)/shard_map/all_to_all | solution.py:800
  115.4 35.2 %all-to-all-start.2 = ((bf16[16,528,128]{2,1,0:T(8,128)(2,1)}), bf16[16,528,128]{2,1,0:T(8,128)(2,1)}, u32[]{:S(2)}, u32[]{:S(2)}) async-start(bf16[16,528,128]{2,1,0:T(8,128)(2,1)} %get-tuple-element.43), calls=%async_computation.2 | async-start | bytes 4325376 | tf_op jit(solution)/shard_map/all_to_all | solution.py:812
  150.6 37.1 %all-to-all-start.3 = ((bf16[16,512,128]{2,1,0:T(8,128)(2,1)}), bf16[16,512,128]{2,1,0:T(8,128)(2,1)}, u32[]{:S(2)}, u32[]{:S(2)}) async-start(bf16[16,512,128]{2,1,0:T(8,128)(2,1)} %get-tuple-element.52), calls=%async_computation.3 | async-start | bytes 4194304 | tf_op jit(solution)/shard_map/all_to_all | solution.py:816
  251.4 9.5 %collective-permute-start = (bf16[1,4,16,384]{3,2,1,0:T(8,128)(2,1)}, bf16[1,4,16,384]{3,2,1,0:T(8,128)(2,1)}, u32[]{:S(2)}, u32[]{:S(2)}) collective-permute-start(bf16[1,4,16,384]{3,2,1,0:T(8,128)(2,1)} %bitcast.12), channel_id=1, source_target_pairs={{0,64},{8,72},{16,80},{24,88},{32,96},{40,104},{48,112},{56,120},{... | collective-permute-start | bytes 147464 | tf_op jit(solution)/shard_map/ppermute | solution.py:756
  260.9 5.7 %copy-start = (bf16[4,16,384]{2,1,0:T(8,128)(2,1)S(1)}, bf16[4,16,384]{2,1,0:T(8,128)(2,1)}, u32[]{:S(2)}) copy-start(bf16[4,16,384]{2,1,0:T(8,128)(2,1)} %text_sum.1) | copy-start | bytes 147460
  260.9 42.3 %all-to-all-start.5 = ((bf16[8,4,128,384]{3,2,1,0:T(8,128)(2,1)}), bf16[8,4,128,384]{3,2,1,0:T(8,128)(2,1)}, u32[]{:S(2)}, u32[]{:S(2)}) async-start(bf16[8,4,128,384]{3,2,1,0:T(8,128)(2,1)} %combine.1), calls=%async_computation.5 | async-start | bytes 6291456 | tf_op jit(solution)/shard_map/all_to_all | solution.py:853
  267.5 1.4 collective-permute-start.1
  268.9 7.0 %collective-permute-start.2 = (bf16[4,4,16,384]{3,2,1,0:T(8,128)(2,1)S(1)}, bf16[4,4,16,384]{3,2,1,0:T(8,128)(2,1)S(1)}, u32[]{:S(2)}, u32[]{:S(2)}) collective-permute-start(bf16[4,4,16,384]{3,2,1,0:T(8,128)(2,1)S(1)} %maximum_select_fusion.2), channel_id=1, source_target_pairs={{0,16},{8,24},{16,0},{24,8},{32,48},{40,56},{48,32},{56,40},{64,80... | collective-permute-start | bytes 589832 | tf_op jit(solution)/shard_map/ppermute | solution.py:756
  276.0 11.7 %collective-permute-start.3 = (bf16[8,4,16,384]{3,2,1,0:T(8,128)(2,1)S(1)}, bf16[8,4,16,384]{3,2,1,0:T(8,128)(2,1)S(1)}, u32[]{:S(2)}, u32[]{:S(2)}) collective-permute-start(bf16[8,4,16,384]{3,2,1,0:T(8,128)(2,1)S(1)} %maximum_select_fusion.1), channel_id=1, source_target_pairs={{0,48},{8,56},{16,32},{24,40},{32,16},{40,24},{48,0},{56,8},{64,11... | collective-permute-start | bytes 1179656 | tf_op jit(solution)/shard_map/ppermute | solution.py:756
